TPU v7x, 512 devices: a whole 4x4x16 slice. The times are simulated.
512 devices in a mesh: fsdp: 16 (over y, x_lo, core), ctx: 32 (over z, x_hi).
Axes of the slice: x: 4 (x_hi: 2, x_lo: 2; x = x_hi * 2 + x_lo), y: 4, z: 16, core: 2. Of those that a mesh axis runs over, the one named last changes fastest.
Arguments:
- token_ids: int32 [8192], P('ctx'), may hold values from 0 to 15
- table: float32 [16, 4096], P(None, 'fsdp'), may hold values from -6 to 6
- norm_gain: float32 [4096], P('fsdp'), may hold values from 0.25 to 1.75
- conv_weight: float32 [4, 4096], P(None, 'fsdp'), may hold values from -4 to 4
- conv_bias: float32 [4096], P('fsdp'), may hold values from -4 to 4
- weight_b: bfloat16 [4096, 128], P('fsdp'), may hold values from -0.09375 to 0.09375
- weight_c: bfloat16 [4096, 128], P('fsdp'), may hold values from -0.09375 to 0.09375
- step_weight: bfloat16 [4096, 64], P('fsdp'), may hold values from -0.1875 to 0.1875
- step_bias: float32 [64], P('fsdp'), as said below
- log_rate: float32 [64], P('fsdp'), as said below
- skip_gain: float32 [64], P('fsdp'), may hold values from 0.25 to 1.75
- out_grad: bfloat16 [8192, 4096], P('ctx', 'fsdp'), may hold values from -6 to 6
Outputs:
- mixer_out: bfloat16 [8192, 4096], P('ctx', 'fsdp')
- grad_embedded: bfloat16 [8192, 4096], P('ctx', 'fsdp')
- grad_table: float32 [16, 4096], P(None, 'fsdp')
- grad_norm_gain: float32 [4096], P('fsdp')
- grad_conv_weight: float32 [4, 4096], P(None, 'fsdp')
- grad_conv_bias: float32 [4096], P('fsdp')
- grad_weight_b: float32 [4096, 128], P('fsdp')
- grad_weight_c: float32 [4096, 128], P('fsdp')
- grad_step_weight: float32 [4096, 64], P('fsdp')
- grad_step_bias: float32 [64], P('fsdp')
- grad_log_rate: float32 [64], P('fsdp')
- grad_skip_gain: float32 [64], P('fsdp')
Inputs may be any that keep to these rules, and one draw needn't show every extreme that they name: exp(log_rate) lies between 1 / 16 and 1 for every head. step_bias lies between log(1 / 8192) - 1 and log(0.2) - 1.
All inputs are finite; a program needn't handle non-finite values.
Results may differ from a plain program's by a relative error of at most 0.02.
Values may be sent and summed in bfloat16 or wider, within the bound.
No kernel may reach another device: no remote copies, remote signals or barrier semaphores. Data moves between devices by JAX's collectives and lax.ppermute only.
A program may use at most 64 MiB of HBM per device.

v0:
```python
import jax
import jax.numpy as jnp
from jax import lax
from jax.sharding import PartitionSpec as P

D = 4096
SPAN = 256


def with_halo(array, sides, width):
    for axis, dim in sides:
        size, length = (lax.axis_size(axis), array.shape[dim])
        up = [(i, (i + 1) % size) for i in range(size - 1)]
        down = [(j, i) for i, j in up]
        last = lax.slice_in_dim(array, length - width, length, axis=dim)
        first = lax.slice_in_dim(array, 0, width, axis=dim)
        before = lax.ppermute(last, axis, up)
        after = lax.ppermute(first, axis, down)
        array = jnp.concatenate([before, array, after], axis=dim)
    return array


def carried_in(array, axis, combine, identity, reverse):
    length, here = (lax.axis_size(axis), lax.axis_index(axis))
    everything = jax.tree.map(
        lambda part, kind: lax.all_gather(part.astype(kind), axis),
        array,
        (jnp.bfloat16, jnp.bfloat16),
    )
    start = jax.tree.map(
        lambda part, zero: jnp.broadcast_to(jnp.asarray(zero, part.dtype), part.shape),
        array,
        identity,
    )

    def carried_turn(k, before):
        at = length - 1 - k if reverse else k
        reached = at > here if reverse else at < here
        new = combine(
            before, jax.tree.map(lambda part, own: part[at].astype(own.dtype), everything, array)
        )
        return jax.tree.map(lambda a, b: jnp.where(reached, a, b), new, before)

    return lax.fori_loop(0, length, carried_turn, start)


def entering(array, axis, combine, identity):
    length, here = (lax.axis_size(axis), lax.axis_index(axis))
    everything = jax.tree.map(lambda part: lax.all_gather(part, axis), array)
    start = jax.tree.map(
        lambda part, zero: jnp.broadcast_to(jnp.asarray(zero, part.dtype), part.shape),
        array,
        identity,
    )

    def entering_turn(k, before):
        at = length - 1 - k
        reached = at > here
        new = combine(before, jax.tree.map(lambda part: part[at], everything))
        return jax.tree.map(lambda a, b: jnp.where(reached, a, b), new, before)

    return lax.fori_loop(0, length, entering_turn, start)


def from_behind(value, axis, steps):
    count = lax.axis_size(axis)
    first, last = (max(0, -steps), min(count, count - steps))
    return lax.ppermute(value, axis, [(source, source + steps) for source in range(first, last)])


def round_keep(value):
    rounded = lax.optimization_barrier(value.astype(jnp.bfloat16))
    return rounded.astype(jnp.float32)


def conv_pair(padded, conv_weight, conv_bias):
    radius = conv_weight.shape[0] - 1
    length = padded.shape[-2] - 2 * radius
    forward = conv_bias + jnp.zeros_like(padded[..., :length, :])
    backward = conv_bias + jnp.zeros_like(padded[..., :length, :])
    for offset in range(radius + 1):
        forward = (
            forward
            + conv_weight[offset] * padded[..., radius - offset : radius - offset + length, :]
        )
        backward = (
            backward
            + conv_weight[offset] * padded[..., radius + offset : radius + offset + length, :]
        )
    return (round_keep(jax.nn.silu(forward)), round_keep(jax.nn.silu(backward)))


def contract(form, left, right):
    return jnp.einsum(form, left, right, preferred_element_type=jnp.float32)


def local_terms(xvals, bvals, cvals, step_raw, step_bias, log_rate):
    total_rows = xvals.shape[0]
    heads = step_raw.shape[1]
    blocks = total_rows // SPAN
    b_half = bvals.astype(jnp.bfloat16).reshape(blocks, SPAN, -1)
    c_half = cvals.astype(jnp.bfloat16).reshape(blocks, SPAN, -1)
    steps = jax.nn.softplus(step_raw + step_bias).reshape(blocks, SPAN, heads)
    logdec = -steps * jnp.exp(log_rate)
    cumul = jnp.cumsum(logdec, axis=1)
    cumul_heads = jnp.transpose(cumul, (0, 2, 1))
    steps_heads = jnp.transpose(steps, (0, 2, 1))
    inner = contract("cqn,csn->cqs", c_half, b_half)
    lower = jnp.tril(jnp.ones((SPAN, SPAN), dtype=bool))
    spread = cumul_heads[:, :, :, None] - cumul_heads[:, :, None, :]
    decay = jnp.exp(jnp.where(lower, spread, -jnp.inf))
    mixing = (inner[:, None] * decay * steps_heads[:, :, None, :]).astype(jnp.bfloat16)
    x_half = xvals.astype(jnp.bfloat16).reshape(blocks, SPAN, heads, -1)
    intra = contract("chqs,cshp->cqhp", mixing, x_half)
    ending = cumul[:, -1:, :]
    weights = jnp.exp(ending - cumul) * steps
    b_scaled = (weights[..., None] * b_half[:, :, None, :].astype(jnp.float32)).astype(jnp.bfloat16)
    pieces = contract("cqhn,cqhp->chnp", b_scaled, x_half)
    totals = ending[:, 0, :]

    def advance(carry, inputs):
        total, piece = inputs
        return (jnp.exp(total)[:, None, None] * carry + piece, carry)

    start = jnp.zeros((heads, bvals.shape[1], xvals.shape[1] // heads), jnp.float32)
    final, entries = lax.scan(advance, start, (totals, pieces))
    device_decay = jnp.exp(jnp.sum(totals, axis=0))
    prior_decay = jnp.exp(jnp.cumsum(totals, axis=0) - totals)
    return (intra, final, device_decay, c_half, jnp.exp(cumul), entries, prior_decay)


def carried_terms(c_half, exp_cumul, entries, prior_decay, start_state):
    full_state = entries + prior_decay[:, :, None, None] * start_state[None]
    product = jnp.einsum(
        "cqn,chnp->cqhp", c_half.astype(jnp.float32), full_state, precision=lax.Precision.HIGHEST
    )
    return exp_cumul[..., None] * product


def start_grad(c_half, exp_cumul, prior_decay, grad_heads):
    weighted = grad_heads * (exp_cumul * prior_decay[:, None, :])[..., None]
    return jnp.einsum(
        "cqn,cqhp->hnp", c_half.astype(jnp.float32), weighted, precision=lax.Precision.HIGHEST
    )


def chain_pairs(earlier, later):
    result = []
    for member in range(0, len(earlier), 2):
        first_decay = earlier[member]
        first_state = earlier[member + 1]
        second_decay = later[member]
        second_state = later[member + 1]
        result.append(first_decay * second_decay)
        result.append(second_decay[..., None, None] * first_state + second_state)
    return tuple(result)


def mirror(value):
    return jnp.flip(value, 0)


def local(
    token_ids,
    table,
    norm_gain,
    conv_weight,
    conv_bias,
    weight_b,
    weight_c,
    step_weight,
    step_bias,
    log_rate,
    skip_gain,
    out_grad,
):
    local_rows = token_ids.shape[0]
    width_local = table.shape[1]
    heads_local = step_bias.shape[0]
    onehot = (token_ids[:, None] == jnp.arange(table.shape[0])[None, :]).astype(jnp.float32)
    embedded = jnp.dot(onehot, table, precision=lax.Precision.HIGHEST)
    square_sums = lax.psum(jnp.sum(embedded * embedded, axis=1), "fsdp")
    scale = lax.rsqrt(square_sums / D + 1e-05)[:, None]
    unit_rows = embedded * scale
    normed = round_keep(unit_rows * norm_gain)
    radius = conv_weight.shape[0] - 1
    padded = with_halo(normed.astype(jnp.bfloat16), (("ctx", 0),), radius)
    (fwd_x, rev_x), conv_back = jax.vjp(
        conv_pair, padded.astype(jnp.float32), conv_weight, conv_bias
    )
    fwd_half = fwd_x.astype(jnp.bfloat16)
    rev_half = rev_x.astype(jnp.bfloat16)

    def project(half):
        return (
            contract("rd,dn->rn", half, weight_b),
            contract("rd,dn->rn", half, weight_c),
            contract("rd,dn->rn", half, step_weight),
        )

    fwd_parts = project(fwd_half)
    rev_parts = project(rev_half)
    fwd_b, fwd_c, fwd_every, rev_b, rev_c, rev_every = lax.psum(
        (fwd_parts[0], fwd_parts[1], fwd_parts[2], rev_parts[0], rev_parts[1], rev_parts[2]), "fsdp"
    )
    first_head = lax.axis_index("fsdp") * heads_local
    fwd_step = lax.dynamic_slice_in_dim(fwd_every, first_head, heads_local, 1)
    rev_step = lax.dynamic_slice_in_dim(rev_every, first_head, heads_local, 1)
    fwd_terms, fwd_back = jax.vjp(local_terms, fwd_x, fwd_b, fwd_c, fwd_step, step_bias, log_rate)
    rev_terms, rev_back = jax.vjp(
        local_terms,
        mirror(rev_x),
        mirror(rev_b),
        mirror(rev_c),
        mirror(rev_step),
        step_bias,
        log_rate,
    )
    f_intra, f_final, f_decay, f_chalf, f_expc, f_entries, f_prior = fwd_terms
    r_intra, r_final, r_decay, r_chalf, r_expc, r_entries, r_prior = rev_terms
    grad_out = out_grad.astype(jnp.float32)

    def split_heads(value):
        return value.reshape(local_rows // SPAN, SPAN, heads_local, -1)

    fwd_dy = split_heads(grad_out)
    rev_dy = split_heads(mirror(grad_out))
    f_dstart = start_grad(f_chalf, f_expc, f_prior, fwd_dy)
    r_dstart = start_grad(r_chalf, r_expc, r_prior, rev_dy)
    unit_decay = jnp.ones_like(f_decay)
    zero_state = jnp.zeros_like(f_final)
    _, f_start = carried_in((f_decay, f_final), "ctx", chain_pairs, (unit_decay, zero_state), False)
    _, r_start = carried_in((r_decay, r_final), "ctx", chain_pairs, (unit_decay, zero_state), True)

    def fwd_carried(c_half, exp_cumul, entries, prior_decay):
        return carried_terms(c_half, exp_cumul, entries, prior_decay, f_start)

    def rev_carried(c_half, exp_cumul, entries, prior_decay):
        return carried_terms(c_half, exp_cumul, entries, prior_decay, r_start)

    f_carry, f_carry_back = jax.vjp(fwd_carried, f_chalf, f_expc, f_entries, f_prior)
    r_carry, r_carry_back = jax.vjp(rev_carried, r_chalf, r_expc, r_entries, r_prior)
    fwd_y = (f_intra + f_carry).reshape(local_rows, width_local)
    rev_y = mirror((r_intra + r_carry).reshape(local_rows, width_local))
    per_channel = jnp.repeat(skip_gain, width_local // heads_local)
    mixed = fwd_y + rev_y + per_channel * (fwd_x + rev_x)
    mixer_out = mixed.astype(jnp.bfloat16)
    _, f_dfinal = entering((f_decay, f_dstart), "ctx", chain_pairs, (unit_decay, zero_state))
    _, r_dfinal = carried_in(
        (r_decay, r_dstart), "ctx", chain_pairs, (unit_decay, zero_state), False
    )
    f_ddecay = jnp.sum(f_dfinal * f_start, axis=(1, 2))
    r_ddecay = jnp.sum(r_dfinal * r_start, axis=(1, 2))
    f_dc, f_de, f_dn, f_dp = f_carry_back(fwd_dy)
    r_dc, r_de, r_dn, r_dp = r_carry_back(rev_dy)
    f_dx, f_db, f_dcv, f_ds, f_dbias, f_drate = fwd_back(
        (fwd_dy, f_dfinal, f_ddecay, f_dc, f_de, f_dn, f_dp)
    )
    r_dx, r_db, r_dcv, r_ds, r_dbias, r_drate = rev_back(
        (rev_dy, r_dfinal, r_ddecay, r_dc, r_de, r_dn, r_dp)
    )
    r_dx = mirror(r_dx)
    r_db = mirror(r_db)
    r_dcv = mirror(r_dcv)
    r_ds = mirror(r_ds)
    d_skip = jnp.sum((grad_out * (fwd_x + rev_x)).reshape(local_rows, heads_local, -1), axis=(0, 2))
    direct = per_channel * grad_out
    total_fb, total_fc, total_rb, total_rc = (
        lax.psum(f_db.astype(jnp.bfloat16), "fsdp").astype(jnp.float32),
        lax.psum(f_dcv.astype(jnp.bfloat16), "fsdp").astype(jnp.float32),
        lax.psum(r_db.astype(jnp.bfloat16), "fsdp").astype(jnp.float32),
        lax.psum(r_dcv.astype(jnp.bfloat16), "fsdp").astype(jnp.float32),
    )
    fwd_steps, rev_steps = (
        lax.all_gather(f_ds.astype(jnp.bfloat16), "fsdp", axis=1, tiled=True),
        lax.all_gather(r_ds.astype(jnp.bfloat16), "fsdp", axis=1, tiled=True),
    )

    def project_back(half, d_b, d_c, s_half):
        b_half = d_b.astype(jnp.bfloat16)
        c_half = d_c.astype(jnp.bfloat16)
        into_x = (
            contract("rn,dn->rd", b_half, weight_b)
            + contract("rn,dn->rd", c_half, weight_c)
            + contract("rn,dn->rd", s_half, step_weight)
        )
        return (
            into_x,
            contract("rd,rn->dn", half, b_half),
            contract("rd,rn->dn", half, c_half),
            contract("rd,rn->dn", half, s_half),
        )

    into_f, gb_f, gc_f, gs_f = project_back(fwd_half, total_fb, total_fc, fwd_steps)
    into_r, gb_r, gc_r, gs_r = project_back(rev_half, total_rb, total_rc, rev_steps)
    d_padded, d_cw, d_cb = conv_back((f_dx + direct + into_f, r_dx + direct + into_r))
    from_above = from_behind(d_padded[:radius], "ctx", -1)
    from_below = from_behind(d_padded[local_rows + radius :], "ctx", 1)
    center = d_padded[radius : radius + local_rows]
    center = center.at[:radius].add(from_below)
    center = center.at[local_rows - radius :].add(from_above)
    grad_normed = round_keep(center)
    d_gain = jnp.sum(grad_normed * unit_rows, axis=0)
    grad_unit = grad_normed * norm_gain
    cross_sum = lax.psum(jnp.sum(grad_unit * embedded, axis=1), "fsdp")
    d_embedded = scale * grad_unit - embedded * (scale * scale * scale) * (cross_sum / D)[:, None]
    grad_embedded = d_embedded.astype(jnp.bfloat16)
    d_table = jnp.dot(onehot.T, d_embedded, precision=lax.Precision.HIGHEST)
    summed = lax.psum(
        (
            d_table,
            d_gain,
            d_cw,
            d_cb,
            gb_f + gb_r,
            gc_f + gc_r,
            gs_f + gs_r,
            f_dbias + r_dbias,
            f_drate + r_drate,
            d_skip,
        ),
        "ctx",
    )
    (
        grad_table,
        grad_gain,
        grad_cw,
        grad_cb,
        grad_wb,
        grad_wc,
        grad_sw,
        grad_sbias,
        grad_rate,
        grad_skip,
    ) = summed
    return (
        mixer_out,
        grad_embedded,
        grad_table,
        grad_gain,
        grad_cw,
        grad_cb,
        grad_wb,
        grad_wc,
        grad_sw,
        grad_sbias,
        grad_rate,
        grad_skip,
    )


def solution(mesh):
    return jax.shard_map(
        local,
        mesh=mesh,
        in_specs=(
            P("ctx"),
            P(None, "fsdp"),
            P("fsdp"),
            P(None, "fsdp"),
            P("fsdp"),
            P("fsdp", None),
            P("fsdp", None),
            P("fsdp", None),
            P("fsdp"),
            P("fsdp"),
            P("fsdp"),
            P("ctx", "fsdp"),
        ),
        out_specs=(
            P("ctx", "fsdp"),
            P("ctx", "fsdp"),
            P(None, "fsdp"),
            P("fsdp"),
            P(None, "fsdp"),
            P("fsdp"),
            P("fsdp", None),
            P("fsdp", None),
            P("fsdp", None),
            P("fsdp"),
            P("fsdp"),
            P("fsdp"),
        ),
        check_vma=False,
    )
```

profile of v0, /device:TPU:6, one launch (start us, length us, event | category | flops | bytes accessed | tf_op | source)
XLA Modules:
  0.0 1384.7 jit_solution(16640274492150675166)
XLA Ops:
  7.2 1.1 multiply_reduce_fusion.23
  8.4 26.7 %psum.154 = f32[256]{0:T(256)S(1)} all-reduce(f32[256]{0:T(256)S(1)} %get-tuple-element.955), channel_id=1, replica_groups=mesh['fsdp'=16,'ctx'=32] {'fsdp'}, use_global_device_ids=true, to_apply=%region_1.0 | all-reduce | flops 256 | bytes 2048 | tf_op jit(solution)/shard_map/psum | solution.py:182
  36.5 4.7 collective-permute-start
  41.2 2.7 collective-permute-start.1
  45.4 4.3 collective-permute-done.1
  49.9 2.1 multiply_convert_fusion.13
  54.8 57.7 %all-reduce.33 = (bf16[256,128]{1,0:T(8,128)(2,1)S(1)}, bf16[256,128]{1,0:T(8,128)(2,1)S(1)}, bf16[256,128]{1,0:T(8,128)(2,1)S(1)}, bf16[256,128]{1,0:T(8,128)(2,1)S(1)}) all-reduce(f32[256,128]{1,0:T(8,128)S(1)} %rev.34, f32[256,128]{1,0:T(8,128)S(1)} %rev.35, ...), channel_id=1, replica_groups=mesh['fsdp'=16,'ctx'=32] {'fsdp'}, use_global_device_ids=true, to_apply=%region_9.11 | all-reduce | flops 131072 | bytes 786432 | tf_op jit(solution)/shard_map/psum | solution.py:203
  112.5 77.1 %all-reduce.30.cloned.1.call-done = (f32[256,64]{0,1:T(8,128)}, f32[256,64]{0,1:T(8,128)}) async-done(((f32[256,64]{0,1:T(8,128)}, f32[256,64]{0,1:T(8,128)}), (f32[256,64]{0,1:T(8,128)}, f32[256,64]{0,1:T(8,128)})) %all-reduce.30.cloned.1.call-update) | async-done | bytes 131088 | tf_op jit(solution)/shard_map/psum | solution.py:203
  190.6 1.4 multiply_bitcast_fusion.3
  191.9 1.2 reduce-window.26
  193.3 1.2 reduce-window.30
  207.6 1.3 fusion.7
  209.8 1.3 copy.208
  211.8 73.0 %all-gather.6 = bf16[32,1,4]{2,1,0:T(2,128)(2,1)S(1)} all-gather(bf16[1,1,4]{2,1,0:T(2,128)(2,1)S(1)} %copy.178), channel_id=8, replica_groups=mesh['fsdp'=16,'ctx'=32] {'ctx'}, dimensions={0}, use_global_device_ids=true | all-gather | bytes 264 | tf_op jit(solution)/shard_map/all_gather | solution.py:26
  285.6 74.9 %all-gather.1 = bf16[32,1,4]{2,1,0:T(2,128)(2,1)S(1)} all-gather(bf16[1,1,4]{2,1,0:T(2,128)(2,1)S(1)} %copy.185), channel_id=3, replica_groups=mesh['fsdp'=16,'ctx'=32] {'ctx'}, dimensions={0}, use_global_device_ids=true | all-gather | bytes 264 | tf_op jit(solution)/shard_map/all_gather | solution.py:26
  361.3 71.9 %all-gather.4 = f32[32,1,4]{2,1,0:T(1,128)} all-gather(f32[1,1,4]{2,1,0:T(1,128)} %copy.208), channel_id=6, replica_groups=mesh['fsdp'=16,'ctx'=32] {'ctx'}, dimensions={0}, use_global_device_ids=true | all-gather | bytes 528 | tf_op jit(solution)/shard_map/all_gather | solution.py:49
  434.4 2.2 fusion.29
  436.6 2.1 fusion.25
  438.7 2.4 fusion.48
  441.4 57.6 %while.42 = (s32[]{:T(128)}, f32[4,128,64]{2,1,0:T(8,128)S(1)}, s32[]{:T(128)}, bf16[32,4]{1,0:T(8,128)(2,1)}, bf16[32,4,128,64]{2,3,1,0:T(8,128)(2,1)}, /*index=5*/s32[]{:T(128)}, s32[]{:T(128)}) while((s32[]{:T(128)}, f32[4,128,64]{2,1,0:T(8,128)S(1)}, s32[]{:T(128)}, bf16[32,4]{1,0:T(8,128)(2,1)}, ...), condition=%wide.region_8.10_spmd.clone, body=%wide.region_7.0_spmd.clone.sunk | while | flops 163848 | bytes 589977 | solution.py:44
  499.0 58.0 %while.43 = (s32[]{:T(128)}, f32[4,128,64]{2,1,0:T(8,128)S(1)}, s32[]{:T(128)}, bf16[32,4]{1,0:T(8,128)(2,1)}, bf16[32,4,128,64]{2,3,1,0:T(8,128)(2,1)}, /*index=5*/s32[]{:T(128)}, s32[]{:T(128)}, s32[]{:T(128)}, s32[]{:T(128)}) while((s32[]{:T(128)}, f32[4,128,64]{2,1,0:T(8,128)S(1)}, s32[]{:T(128)}, bf16[32,4]{1,0:T(8,128)(2,1)}, ...), condition=%wide.region_15.17_spmd.clone, body=%wide.region_14.16_spmd.clone.sunk | while | flops 163852 | bytes 590039 | solution.py:44
  557.0 88.4 %all-gather.18.cloned.1.call-done = bf16[128,128,64]{1,2,0:T(8,128)(2,1)} async-done(((bf16[4,128,64]{1,2,0:T(8,128)(2,1)}), bf16[128,128,64]{1,2,0:T(8,128)(2,1)}) %all-gather.18.cloned.1.call-update) | async-done | bytes 2097168 | tf_op jit(solution)/shard_map/all_gather | solution.py:26
  645.4 57.8 %while.44 = (s32[]{:T(128)}, f32[4,128,64]{2,1,0:T(8,128)S(1)}, s32[]{:T(128)}, bf16[32,4]{1,0:T(8,128)(2,1)}, bf16[32,4,128,64]{2,3,1,0:T(8,128)(2,1)}, /*index=5*/s32[]{:T(128)}, s32[]{:T(128)}) while((s32[]{:T(128)}, f32[4,128,64]{2,1,0:T(8,128)S(1)}, s32[]{:T(128)}, bf16[32,4]{1,0:T(8,128)(2,1)}, ...), condition=%wide.region_17.19_spmd.clone, body=%wide.region_16.18_spmd.clone.sunk | while | flops 163848 | bytes 589977 | solution.py:44
  705.9 1.4 fusion.24
  707.3 1.6 rev.39
  709.1 1.3 multiply_reduce_fusion.21
  712.2 1.5 fusion.18
  717.1 5.0 reduce-window.34
  723.2 83.8 %all-gather.20.cloned.1.call-done = f32[128,128,64]{1,2,0:T(8,128)} async-done(((f32[4,128,64]{1,2,0:T(8,128)}), f32[128,128,64]{1,2,0:T(8,128)}) %all-gather.20.cloned.1.call-update) | async-done | bytes 4194320 | tf_op jit(solution)/shard_map/all_gather | solution.py:49
  807.1 60.0 %while.45 = (s32[]{:T(128)}, f32[4,128,64]{2,1,0:T(8,128)S(1)}, s32[]{:T(128)}, f32[32,4]{1,0:T(8,128)}, f32[32,4,128,64]{2,3,1,0:T(8,128)}, /*index=5*/s32[]{:T(128)}, s32[]{:T(128)}, s32[]{:T(128)}, s32[]{:T(128)}) while((s32[]{:T(128)}, f32[4,128,64]{2,1,0:T(8,128)S(1)}, s32[]{:T(128)}, f32[32,4]{1,0:T(8,128)}, ...), condition=%wide.region_34.36_spmd.clone, body=%wide.region_33.35_spmd.clone.sunk | while | flops 131080 | bytes 917727 | solution.py:62
  868.5 1.3 fusion.28
  869.9 1.2 fusion.19
  875.4 5.0 reduce-window.36
  882.1 16.2 %all-gather.7 = bf16[16,4,256]{2,1,0:T(4,128)(2,1)S(1)} all-gather(bf16[1,4,256]{2,1,0:T(4,128)(2,1)S(1)} %bitcast.525), channel_id=1, replica_groups=mesh['fsdp'=16,'ctx'=32] {'fsdp'}, dimensions={0}, use_global_device_ids=true | all-gather | bytes 34816 | tf_op jit(solution)/shard_map/all_gather | solution.py:276
  898.4 20.3 %all-gather.8 = bf16[16,4,256]{2,1,0:T(4,128)(2,1)S(1)} all-gather(bf16[1,4,256]{2,1,0:T(4,128)(2,1)S(1)} %bitcast.526), channel_id=1, replica_groups=mesh['fsdp'=16,'ctx'=32] {'fsdp'}, dimensions={0}, use_global_device_ids=true | all-gather | bytes 34816 | tf_op jit(solution)/shard_map/all_gather | solution.py:275
  921.9 121.9 %all-reduce.32.cloned.1.call-done = (bf16[256,128]{1,0:T(8,128)(2,1)}, bf16[256,128]{1,0:T(8,128)(2,1)}, bf16[256,128]{1,0:T(8,128)(2,1)}, bf16[256,128]{1,0:T(8,128)(2,1)}) async-done(((bf16[256,128]{1,0:T(8,128)(2,1)}, bf16[256,128]{1,0:T(8,128)(2,1)}, bf16[256,128]{1,0:T(8,128)(2,1)}, bf16[256,128]{1,0:T(8,128)(2,1)}), (bf16[256,128]{1,0:T(8,128)(2,1)}, bf16[256,128]{1,0:T(8,128)(2,1)}, ...) | async-done | bytes 262160 | tf_op jit(solution)/shard_map/psum | solution.py:269
  1048.0 1.7 convolution_add_fusion.5
  1049.6 1.7 convolution_add_fusion.4
  1053.9 4.1 collective-permute-start.3
  1058.0 4.1 collective-permute-start.2
  1062.3 4.0 collective-permute-done.2
  1066.5 1.1 scatter-add.6
  1068.8 29.0 %psum.165 = f32[256]{0:T(256)S(1)} all-reduce(f32[256]{0:T(256)S(1)} %get-tuple-element.815), channel_id=1, replica_groups=mesh['fsdp'=16,'ctx'=32] {'fsdp'}, use_global_device_ids=true, to_apply=%region_51.53 | all-reduce | flops 256 | bytes 2048 | tf_op jit(solution)/shard_map/psum | solution.py:305
  1099.0 145.6 %all-reduce.18 = (f32[16,256]{1,0:T(8,128)}, f32[256]{0:T(256)}, f32[4,256]{1,0:T(4,128)}, f32[256]{0:T(256)}, f32[4]{0:T(128)}, /*index=5*/f32[4]{0:T(128)}, f32[4]{0:T(128)}) all-reduce(f32[16,256]{1,0:T(8,128)S(1)} %fusion.72, f32[256]{0:T(256)S(1)} %get-tuple-element.814, ...), channel_id=1, replica_groups=mesh['fsdp'=16,'ctx'=32] {'ctx'}, use_global_device_ids=true, to_apply=%region_52.54 | all-reduce | flops 5644 | bytes 45152 | tf_op jit(solution)/shard_map/psum | solution.py:309
  1244.6 128.6 %all-reduce.28.cloned.1.call-done = (f32[256,128]{1,0:T(8,128)}, f32[256,128]{1,0:T(8,128)}, f32[256,64]{0,1:T(8,128)}) async-done(((f32[256,128]{1,0:T(8,128)}, f32[256,128]{1,0:T(8,128)}, f32[256,64]{0,1:T(8,128)}), (f32[256,128]{1,0:T(8,128)}, f32[256,128]{1,0:T(8,128)}, f32[256,64]{0,1:T(8,128)})) %all-reduce.28.cloned.1.call-update) | async-done | bytes 327696 | tf_op jit(solution)/shard_map/psum | solution.py:309
  1373.2 1.6 copy.306
  1374.8 1.6 copy.307
  1376.4 1.5 copy.308
  (824 shorter events, 281.7 us)
Async XLA Ops:
  7.2 46.4 %copy-start = (bf16[256,128]{1,0:T(8,128)(2,1)S(1)}, bf16[256,128]{1,0:T(8,128)(2,1)}, u32[]{:S(2)}) copy-start(bf16[256,128]{1,0:T(8,128)(2,1)} %param.30) | copy-start | bytes 196612
  7.2 44.8 %copy-start.7 = (bf16[256,64]{0,1:T(8,128)(2,1)S(1)}, bf16[256,64]{0,1:T(8,128)(2,1)}, u32[]{:S(2)}) copy-start(bf16[256,64]{0,1:T(8,128)(2,1)} %param.32) | copy-start | bytes 98308
  7.2 182.5 %all-reduce.30.cloned.1.call-start = ((), (), s32[]{:S(2)}) async-start(), calls=%async_computation.5 | async-start | bytes 262144 | tf_op jit(solution)/shard_map/psum | solution.py:203
  36.5 8.9 collective-permute-start
  41.2 8.6 collective-permute-start.1
  44.7 9.4 copy-start.38
  44.7 9.4 copy-start.40
  44.7 9.4 copy-start.42
  44.7 9.4 copy-start.44
  45.4 145.2 %copy-start.59 = (f32[4]{0:T(128)}, f32[4]{0:T(128)S(1)}, u32[]{:S(2)}) copy-start(f32[4]{0:T(128)S(1)} %exp.124) | copy-start | bytes 52
  45.4 8.7 copy-start.6
  52.0 138.5 %copy-start.26 = (f32[4]{0:T(128)S(1)}, f32[4]{0:T(128)}, u32[]{:S(2)}) copy-start(f32[4]{0:T(128)} %param.33) | copy-start | bytes 52
  53.6 147.8 %copy-start.21 = (bf16[256,256]{1,0:T(8,128)(2,1)S(1)}, bf16[256,256]{1,0:T(8,128)(2,1)}, u32[]{:S(2)}) copy-start(bf16[256,256]{1,0:T(8,128)(2,1)} %param.36) | copy-start | bytes 393220
  54.8 386.6 %all-gather.14.cloned.1.call-start = ((), (), s32[]{:S(2)}) async-start(), calls=%async_computation | async-start | bytes 2162688 | tf_op jit(solution)/shard_map/all_gather | solution.py:26
  112.5 88.8 %copy-start.11 = (f32[256,128]{1,0:T(8,128)}, f32[256,128]{1,0:T(8,128)S(1)}, u32[]{:S(2)}) copy-start(f32[256,128]{1,0:T(8,128)S(1)} %convert_element_type.659) | copy-start | bytes 393220
  195.8 7.0 copy-start.30
  198.3 300.6 %all-gather.16.cloned.1.call-start = ((), (), s32[]{:S(2)}) async-start(), calls=%async_computation.1 | async-start | bytes 2162688 | tf_op jit(solution)/shard_map/all_gather | solution.py:26
  198.8 242.3 %copy-start.22 = (bf16[256,256]{0,1:T(8,128)(2,1)}, bf16[256,256]{0,1:T(8,128)(2,1)S(1)}, u32[]{:S(2)}) copy-start(bf16[256,256]{0,1:T(8,128)(2,1)S(1)} %rev.33) | copy-start | bytes 393220
  201.3 444.1 %all-gather.18.cloned.1.call-start = ((), (), s32[]{:S(2)}) async-start(), calls=%async_computation.2 | async-start | bytes 2162688 | tf_op jit(solution)/shard_map/all_gather | solution.py:26
  202.8 604.2 %all-gather.20.cloned.1.call-start = ((), (), s32[]{:S(2)}) async-start(), calls=%async_computation.3 | async-start | bytes 4325376 | tf_op jit(solution)/shard_map/all_gather | solution.py:49
  204.3 234.3 %copy-start.24 = (pred[256,256]{1,0:T(8,128)(4,1)}, pred[256,256]{1,0:T(8,128)(4,1)S(1)}, u32[]{:S(2)}) copy-start(pred[256,256]{1,0:T(8,128)(4,1)S(1)} %iota_compare_fusion) | copy-start | bytes 196612
  441.1 602.7 %all-reduce.32.cloned.1.call-start = ((), (), s32[]{:S(2)}) async-start(), calls=%async_computation.6 | async-start | bytes 524288 | tf_op jit(solution)/shard_map/psum | solution.py:269
  645.4 58.7 %copy-start.20 = (f32[256,128]{0,1:T(8,128)S(1)}, f32[256,128]{0,1:T(8,128)}, u32[]{:S(2)}) copy-start(f32[256,128]{0,1:T(8,128)} %copy.199) | copy-start | bytes 393220
  645.4 58.7 %copy-start.23 = (bf16[256,256]{0,1:T(8,128)(2,1)S(1)}, bf16[256,256]{0,1:T(8,128)(2,1)}, u32[]{:S(2)}) copy-start(bf16[256,256]{0,1:T(8,128)(2,1)} %copy-done.22) | copy-start | bytes 393220
  645.4 58.7 %copy-start.28 = (f32[256,4]{0,1:T(4,128)S(1)}, f32[256,4]{0,1:T(4,128)}, u32[]{:S(2)}) copy-start(f32[256,4]{0,1:T(4,128)} %copy-done.27) | copy-start | bytes 12292
  704.1 8.1 copy-start.31
  807.1 60.0 %copy-start.19 = (f32[256,128]{0,1:T(8,128)S(1)}, f32[256,128]{0,1:T(8,128)}, u32[]{:S(2)}) copy-start(f32[256,128]{0,1:T(8,128)} %copy.219) | copy-start | bytes 393220
  807.1 60.4 %copy-start.36 = (f32[4]{0:T(128)S(1)}, f32[4]{0:T(128)}, u32[]{:S(2)}) copy-start(f32[4]{0:T(128)} %copy-done.35) | copy-start | bytes 52
  807.1 60.6 %copy-start.65 = (f32[4]{0:T(128)S(1)}, f32[4]{0:T(128)}, u32[]{:S(2)}) copy-start(f32[4]{0:T(128)} %get-tuple-element.951) | copy-start | bytes 52
  871.1 9.8 copy-start.34
  871.1 9.8 copy-start.57
  871.1 9.8 copy-start.58
  871.1 9.8 copy-start.60
  871.2 49.0 %copy-start.61 = (f32[4]{0:T(128)S(1)}, f32[4]{0:T(128)}, u32[]{:S(2)}) copy-start(f32[4]{0:T(128)} %fusion.94) | copy-start | bytes 52
  871.2 49.0 %copy-start.64 = (f32[4]{0:T(128)S(1)}, f32[4]{0:T(128)}, u32[]{:S(2)}) copy-start(f32[4]{0:T(128)} %param.34) | copy-start | bytes 52
  898.3 153.0 %copy-start.2 = (f32[256,256]{0,1:T(8,128)S(1)}, f32[256,256]{0,1:T(8,128)}, u32[]{:S(2)}) copy-start(f32[256,256]{0,1:T(8,128)} %rev.39) | copy-start | bytes 786436
  898.3 153.0 %copy-start.48 = (f32[256]{0:T(256)S(1)}, f32[256]{0:T(256)}, u32[]{:S(2)}) copy-start(f32[256]{0:T(256)} %mul.927) | copy-start | bytes 3076
  919.9 131.6 %copy-start.5 = (f32[256,256]{0,1:T(8,128)S(1)}, f32[256,256]{0,1:T(8,128)}, u32[]{:S(2)}) copy-start(f32[256,256]{0,1:T(8,128)} %get-tuple-element.924) | copy-start | bytes 786436
  919.9 453.3 %all-reduce.28.cloned.1.call-start = ((), (), s32[]{:S(2)}) async-start(), calls=%async_computation.4 | async-start | bytes 655360 | tf_op jit(solution)/shard_map/psum | solution.py:309
  1043.8 7.5 copy-start.18
  1043.8 7.7 copy-start.14
  1044.8 6.9 copy-start.3
  1053.7 14.9 %copy-start.46 = (f32[256]{0:T(256)S(1)}, f32[256]{0:T(256)}, u32[]{:S(2)}) copy-start(f32[256]{0:T(256)} %param.27) | copy-start | bytes 3076
  1053.7 44.1 %copy-start.49 = (f32[256]{0:T(256)S(1)}, f32[256]{0:T(256)}, u32[]{:S(2)}) copy-start(f32[256]{0:T(256)} %get-tuple-element.945) | copy-start | bytes 3076
  1053.7 44.9 %copy-start.62 = (s32[256]{0:T(256)S(1)}, s32[256]{0:T(256)}, u32[]{:S(2)}) copy-start(s32[256]{0:T(256)} %param.25) | copy-start | bytes 3076
  1053.9 13.7 collective-permute-start.3
  1058.0 8.4 collective-permute-start.2
  1062.1 36.9 %copy-start.63 = (f32[4]{0:T(128)S(1)}, f32[4]{0:T(128)}, u32[]{:S(2)}) copy-start(f32[4]{0:T(128)} %add.433) | copy-start | bytes 52
  (29 other events, 100.9 us)
Sparse Core Ops, SparseCore 0:
  54.9 134.7 all-reduce.29
  198.5 152.4 all-gather.13
  354.0 144.2 all-gather.15
  501.3 144.0 all-gather.17
  648.9 158.0 all-gather.19
  920.0 123.7 all-reduce.31
  1062.3 310.9 all-reduce.27
where the time goes:
time: 1400 us; the launch traced here: 1380 us
  blocking collectives  515 us (37%)
  waiting for transfers between devices  508 us (36%)
  local copies, waits for them, and re-layouts  177 us (13%)
  other arithmetic  109 us (8%)
  matrix products  38.6 us (3%)
  starting transfers between devices  16.3 us (1%)
  between operations  15.4 us (1%)
    all_gather x2, blocking collectives, carried_in(): lax.all_gather(part.astype(kind), axis)  148 us
    psum x1, blocking collectives, local(): lax.psum((d_table, d_gain, d_cw, d_cb, gb_f + gb_r, gc_f + gc_r, gs_f + g...  146 us
    psum x1, waiting for transfers between devices, local(): lax.psum((d_table, d_gain, d_cw, d_cb, gb_f + gb_r, gc_f + gc_r, gs_f + g...  129 us
    psum x1, waiting for transfers between devices, local(): lax.psum(f_db.astype(jnp.bfloat16), 'fsdp').astype(jnp.float32)  122 us
    dynamic_slice x192, local copies, waits for them, and re-layouts, carried_turn(): part[at].astype(own.dtype)  93.5 us
    all_gather x3, waiting for transfers between devices, carried_in(): lax.all_gather(part.astype(kind), axis)  88.5 us
    all_gather x1, waiting for transfers between devices, entering(): everything = jax.tree.map(lambda part: lax.all_gather(part, axis), array)  83.8 us
    psum x1, waiting for transfers between devices, local(): lax.psum((fwd_parts[0], fwd_parts[1], fwd_parts[2], rev_parts[0], rev_par...  77.1 us
  transfers between devices with their start and end apart: 11, of which 7 were waited for; matrix products, arithmetic and copies ran while one was open for 16% of the time, Pallas kernels for 0%

commit v1 on v0

v1 whole, which is shorter than its diff:
```python
import jax
import jax.numpy as jnp
from jax import lax
from jax.sharding import PartitionSpec as P
from jax.experimental import pallas as pl
from jax.experimental.pallas import tpu as pltpu

D = 4096
ROWS = 256
HEADS = 4
STATE = 128
GROUPS = 16
SLICES = 32
F32 = jnp.float32
BF16 = jnp.bfloat16
VMEM = pltpu.VMEM


def call(kernel, outs, *args):
    shapes = tuple(jax.ShapeDtypeStruct(shape, kind) for shape, kind in outs)
    return pl.pallas_call(kernel, out_shape=shapes, name=kernel.__name__)(*args)


def iota(shape, dim):
    return lax.broadcasted_iota(jnp.int32, shape, dim)


def mm(left, right):
    return lax.dot_general(left, right, (((1,), (0,)), ((), ())), preferred_element_type=F32)


def mm_tn(left, right):
    return lax.dot_general(left, right, (((0,), (0,)), ((), ())), preferred_element_type=F32)


def mm_nt(left, right):
    return lax.dot_general(left, right, (((1,), (1,)), ((), ())), preferred_element_type=F32)


def pieces(value, count):
    parts = []
    rest = value
    for _ in range(count):
        part = rest.astype(BF16)
        parts.append(part)
        rest = rest - part.astype(F32)
    return parts


def exact(form, left, right, count, split_left):
    total = None
    for part in pieces(left if split_left else right, count):
        term = form(part, right) if split_left else form(left, part)
        total = term if total is None else total + term
    return total


def head_masks(rows):
    lane_head = iota((rows, 256), 1) // 64
    return [lane_head == h for h in range(HEADS)]


def by_head(values, masks):
    out = values[3]
    for h in range(3):
        out = jnp.where(masks[h], values[h], out)
    return out


def expand(cols, first, masks):
    wide = [jnp.broadcast_to(cols[:, first + h : first + h + 1], (ROWS, 256)) for h in range(HEADS)]
    return by_head(wide, masks)


def columns(rows):
    missing = 128 - rows.shape[0]
    return jnp.transpose(jnp.concatenate([rows, jnp.zeros((missing, ROWS), F32)], axis=0))


def inclusive_masks():
    before = iota((ROWS, ROWS), 0) <= iota((ROWS, ROWS), 1)
    after = iota((ROWS, ROWS), 0) >= iota((ROWS, ROWS), 1)
    return jnp.where(before, 1.0, 0.0).astype(BF16), jnp.where(after, 1.0, 0.0).astype(BF16)


def tokens_kernel(ids, table, scale, gain, cw, cb, wbc, swx, xf, xr, gf, gr, send, oht_ref):
    normed = (table[...] * scale[...] * gain[...]).astype(BF16).astype(F32)
    vocab = iota((16, ROWS), 0)
    hits = [jnp.where(ids[o : o + 1, :] == vocab, 1.0, 0.0) for o in range(8)]
    oht = jnp.concatenate(hits, axis=0).astype(BF16)
    oht_ref[...] = oht
    none = jnp.zeros((16, 256), F32)
    taps = [cw[k : k + 1, :] * normed for k in range(4)]
    fwd_rows = jnp.concatenate([taps[3], taps[2], taps[1], taps[0], none, none, none, none], axis=0)
    rev_rows = jnp.concatenate([none, none, none, taps[0], taps[1], taps[2], taps[3], none], axis=0)
    halves = []
    for rows, x_ref, slope_ref in ((fwd_rows, xf, gf), (rev_rows, xr, gr)):
        pre = exact(mm_tn, oht, rows, 3, False) + cb[...]
        gate = 1.0 / (1.0 + jnp.exp(-pre))
        slope_ref[...] = gate * (1.0 + pre * (1.0 - gate))
        half = (pre * gate).astype(BF16)
        x_ref[...] = half
        halves.append(half)
    for member, half in enumerate(halves):
        part = mm(half, wbc[...]).astype(BF16).reshape(GROUPS, 16, 256)
        send[:, 0:16, member * 256 : member * 256 + 256] = part
    own = iota((128, 256), 0) % 8 < 4
    steps = jnp.where(own, mm_nt(swx[...], halves[0]), mm_nt(swx[...], halves[1]))
    high, low = pieces(steps, 2)
    send[:, 16:24, 0:256] = high.reshape(GROUPS, 8, 256)
    send[:, 16:24, 256:512] = low.reshape(GROUPS, 8, 256)


def reduce_kernel(got, bc, raw):
    total = got[0].astype(F32)
    for k in range(1, GROUPS):
        total = total + got[k].astype(F32)
    half = total[0:16].astype(BF16)
    bc[...] = jnp.broadcast_to(half[None], (GROUPS, 16, 512))
    raw[...] = total[16:24, 0:256] + total[16:24, 256:512]


def states_kernel(bc, raw, bias, rate, xf, xr, dy, send, cols_ref, rows_ref):
    shifted = raw[...] + bias[...]
    step = jnp.maximum(shifted, 0.0) + jnp.log1p(jnp.exp(-jnp.abs(shifted)))
    slope = 1.0 / (1.0 + jnp.exp(-shifted))
    logdec = -step * jnp.exp(rate[...])
    before, after = inclusive_masks()
    fwd_row = iota((8, ROWS), 0) < 4
    prefix = exact(mm, logdec, before, 3, True)
    suffix = exact(mm, logdec, after, 3, True)
    cumul = jnp.where(fwd_row, prefix, suffix)
    fwd_one = iota((8, 1), 0) < 4
    ending = jnp.where(fwd_one, prefix[:, ROWS - 1 : ROWS], suffix[:, 0:1])
    closing = jnp.exp(ending - cumul)
    weight = closing * step
    grown = jnp.exp(cumul)
    rows_ref[...] = jnp.concatenate([cumul, step, weight, closing, slope, logdec], axis=0)
    cols = columns(jnp.concatenate([cumul, step, weight, grown], axis=0))
    cols_ref[...] = cols
    masks = head_masks(ROWS)
    dyf = dy[...].astype(F32)
    found = []
    for br, x in ((0, xf), (1, xr)):
        b = bc[:, br * 256 : br * 256 + 128]
        c = bc[:, br * 256 + 128 : br * 256 + 256]
        weighted = (expand(cols, 16 + 4 * br, masks) * x[...].astype(F32)).astype(BF16)
        final = mm_tn(b, weighted)
        turned = (expand(cols, 24 + 4 * br, masks) * dyf).astype(BF16)
        found.append((final, mm_tn(c, turned)))
    chains = (found[0][0], found[1][1], found[1][0], found[0][1])
    for ch, state in enumerate(chains):
        for hp in range(2):
            part = state[:, hp * 128 : hp * 128 + 128].astype(BF16).reshape(16, 8, 128)
            send[:, hp, ch * 8 : ch * 8 + 8, :] = part
    decay = jnp.exp(ending)
    left = iota((1, 128), 1) < 64
    row = iota((8, 128), 0)
    for hp in range(2):
        fd = jnp.where(left, decay[2 * hp : 2 * hp + 1], decay[2 * hp + 1 : 2 * hp + 2])
        rd = jnp.where(left, decay[4 + 2 * hp : 5 + 2 * hp], decay[5 + 2 * hp : 6 + 2 * hp])
        f_high = fd.astype(BF16).astype(F32)
        r_high = rd.astype(BF16).astype(F32)
        packed = jnp.where(row == 0, f_high, 0.0)
        packed = jnp.where(row == 1, fd - f_high, packed)
        packed = jnp.where(row == 2, r_high, packed)
        packed = jnp.where(row == 3, rd - r_high, packed)
        send[:, hp, 32:40, :] = jnp.broadcast_to(packed.astype(BF16)[None], (16, 8, 128))


def chain_kernel(got, out):
    decays = got[:, 32:40, :].astype(F32)
    fwd_decay = decays[:, 0:1, :] + decays[:, 1:2, :]
    rev_decay = decays[:, 2:3, :] + decays[:, 3:4, :]
    up_f = jnp.zeros((8, 128), F32)
    up_r = jnp.zeros((8, 128), F32)
    down_r = jnp.zeros((8, 128), F32)
    down_f = jnp.zeros((8, 128), F32)
    for i in range(SLICES):
        out[i, 0:16, :] = jnp.concatenate([up_f, up_r], axis=0).astype(BF16)
        here = got[i, 0:16, :].astype(F32)
        up_f = fwd_decay[i] * up_f + here[0:8]
        up_r = rev_decay[i] * up_r + here[8:16]
        j = SLICES - 1 - i
        out[j, 16:32, :] = jnp.concatenate([down_r, down_f], axis=0).astype(BF16)
        there = got[j, 16:32, :].astype(F32)
        down_r = rev_decay[j] * down_r + there[0:8]
        down_f = fwd_decay[j] * down_f + there[8:16]


def within_kernel(bc, cols_ref, rows_ref, xf, xr, dy, skip, y_ref, dxf, dxr, dbc, side, line):
    masks = head_masks(ROWS)
    t_at = iota((ROWS, ROWS), 0)
    s_at = iota((ROWS, ROWS), 1)
    lane = iota((ROWS, 128), 1)
    cols = cols_ref[...]
    dyh = dy[...]
    dyf = dyh.astype(F32)
    nothing = jnp.zeros((ROWS, 256), BF16)
    direct = skip[...] * dyf
    total = skip[...] * (xf[...].astype(F32) + xr[...].astype(F32))
    side_acc = jnp.zeros((ROWS, 128), F32)
    lines = []
    for br, x, dx_ref in ((0, xf, dxf), (1, xr, dxr)):
        xh = x[...]
        b = bc[:, br * 256 : br * 256 + 128]
        c = bc[:, br * 256 + 128 : br * 256 + 256]
        inner = mm_nt(c, b)
        causal = t_at >= s_at if br == 0 else t_at <= s_at
        dinner = jnp.zeros((ROWS, ROWS), F32)
        intra = []
        back = []
        for h in range(HEADS):
            at = 4 * br + h
            spread = cols[:, at : at + 1] - rows_ref[at : at + 1, :]
            decay = jnp.exp(jnp.where(causal, spread, -jnp.inf))
            step = rows_ref[8 + at : 9 + at, :]
            paced = decay * step
            mixing = (inner * paced).astype(BF16)
            intra.append(mm(mixing, xh))
            back.append(mm_tn(mixing, dyh))
            dmix = mm_nt(jnp.where(masks[h], dyh, nothing), xh)
            dinner = dinner + dmix * paced
            reach = dmix * decay * inner
            lines.append(jnp.sum(reach, axis=0, keepdims=True))
            flow = jnp.sum(reach * step, axis=1, keepdims=True)
            side_acc = jnp.where(lane == at, flow, side_acc)
        total = total + by_head(intra, masks)
        dx_ref[...] = direct + by_head(back, masks)
        dhalf = dinner.astype(BF16)
        dbc[:, br * 256 : br * 256 + 128] = mm_tn(dhalf, c)
        dbc[:, br * 256 + 128 : br * 256 + 256] = mm(dhalf, b)
    y_ref[...] = total
    side[...] = jnp.transpose(side_acc)[0:8]
    line[...] = jnp.concatenate(lines, axis=0)


def carried_kernel(
    got, bc, cols_ref, rows_ref, xf, xr, dy, y0, dxf0, dxr0, dbc0, side, line, rate,
    out, dxf, dxr, send, draw_ref, small,
):
    masks = head_masks(ROWS)
    cols = cols_ref[...]
    dyf = dy[...].astype(F32)

    def state(ch):
        halves = [
            got[:, hp, ch * 8 : ch * 8 + 8, :].astype(F32).reshape(STATE, 128) for hp in range(2)
        ]
        return jnp.concatenate(halves, axis=1)

    row_at = iota((8, 256), 0)
    lane_head = iota((8, 256), 1) // 64
    total = y0[...]
    dp = jnp.zeros((8, ROWS), F32)
    dw = jnp.zeros((8, ROWS), F32)
    d_end = jnp.zeros((8, 1), F32)
    for br, x, dx0, dx_ref, at_state, at_grad in ((0, xf, dxf0, dxf, 0, 3), (1, xr, dxr0, dxr, 2, 1)):
        start = state(at_state)
        ahead = state(at_grad)
        start_half = start.astype(BF16)
        ahead_half = ahead.astype(BF16)
        b = bc[:, br * 256 : br * 256 + 128]
        c = bc[:, br * 256 + 128 : br * 256 + 256]
        grown = expand(cols, 24 + 4 * br, masks)
        weight = expand(cols, 16 + 4 * br, masks)
        heads = jnp.where(lane_head + 4 * br == row_at, 1.0, 0.0).astype(BF16)
        carried = grown * mm(c, start_half)
        total = total + carried
        dp = dp + exact(mm_nt, heads, dyf * carried, 2, False)
        xv = x[...].astype(F32)
        toward = mm(b, ahead_half)
        dx_ref[...] = dx0[...] + weight * toward
        dw = dw + exact(mm_nt, heads, xv * toward, 2, False)
        dc = mm_nt((grown * dyf).astype(BF16), start_half)
        db = mm_nt((weight * xv).astype(BF16), ahead_half)
        at = br * 256
        send[:, :, at : at + 128] = (dbc0[:, at : at + 128] + db).astype(BF16).reshape(16, 16, 128)
        send[:, :, at + 128 : at + 256] = (
            (dbc0[:, at + 128 : at + 256] + dc).astype(BF16).reshape(16, 16, 128)
        )
        both = jnp.sum(start * ahead, axis=0, keepdims=True)
        spread = jnp.where(lane_head + 4 * br == row_at, both, 0.0)
        d_end = d_end + jnp.sum(spread, axis=1, keepdims=True)
    out[...] = total.astype(BF16)
    cumul = rows_ref[0:8]
    step = rows_ref[8:16]
    weight = rows_ref[16:24]
    closing = rows_ref[24:32]
    slope = rows_ref[32:40]
    logdec = rows_ref[40:48]
    at = iota((8, ROWS), 1)
    row = iota((8, ROWS), 0)
    last = at == jnp.where(row < 4, ROWS - 1, 0)
    pull = dw * weight
    ending = jnp.sum(jnp.where(last, cumul, 0.0), axis=1, keepdims=True)
    d_end = jnp.exp(ending) * d_end + jnp.sum(pull, axis=1, keepdims=True)
    dcumul = side[...] - step * line[...] + dp - pull + jnp.where(last, d_end, 0.0)
    before, after = inclusive_masks()
    prefix = exact(mm, dcumul, before, 3, True)
    suffix = exact(mm, dcumul, after, 3, True)
    dlog = jnp.where(row < 4, suffix, prefix)
    dstep = line[...] + dw * closing - dlog * jnp.exp(rate[...])
    draw = dstep * slope
    draw_ref[...] = draw.astype(BF16)
    d_bias = jnp.sum(draw, axis=1, keepdims=True)
    d_rate = jnp.sum(dlog * logdec, axis=1, keepdims=True)
    first = iota((1, 256), 1)
    bias_row = jnp.zeros((1, 256), F32)
    rate_row = jnp.zeros((1, 256), F32)
    for h in range(HEADS):
        bias_row = jnp.where(first == 64 * h, d_bias[h : h + 1] + d_bias[h + 4 : h + 5], bias_row)
        rate_row = jnp.where(first == 64 * h, d_rate[h : h + 1] + d_rate[h + 4 : h + 5], rate_row)
    skip_row = jnp.sum(dyf * (xf[...].astype(F32) + xr[...].astype(F32)), axis=0, keepdims=True)
    none = jnp.zeros((5, 256), F32)
    small[...] = jnp.concatenate([skip_row, bias_row, rate_row, none], axis=0)


def total_kernel(got, draw, send):
    total = got[0].astype(F32)
    for k in range(1, GROUPS):
        total = total + got[k].astype(F32)
    send[:, 0:16, :] = jnp.broadcast_to(total.astype(BF16)[None], (GROUPS, 16, 512))
    padded = jnp.concatenate([draw[...].astype(F32), jnp.zeros((8, 256), F32)], axis=1)
    send[:, 16:24, :] = jnp.broadcast_to(padded.astype(BF16)[None], (GROUPS, 8, 512))


def project_back_kernel(
    got, xf, xr, gf, gr, dxf, dxr, wbc, sw, oht, table, scale, gain, small,
    dpf, dpr, to_prev, to_next, grads, lines,
):
    dbc = got[:, 0:16, :].reshape(ROWS, 512)
    draw = got[:, 16:24, 0:256].astype(F32).reshape(128, 256).astype(BF16)
    pick_row = iota((128, 64), 0)
    pick_col = iota((128, 64), 1)
    wanted = pick_row // 8 * 4 + pick_row % 4
    normed = (table[...] * scale[...] * gain[...]).astype(BF16).astype(F32)
    taps = [jnp.zeros((1, 256), F32)] * 4
    bias_row = jnp.zeros((1, 256), F32)
    wide = jnp.zeros((256, 256), F32)
    thin = jnp.zeros((256, 64), F32)
    for br, x, slope, dx, out in ((0, xf, gf, dxf, dpf), (1, xr, gr, dxr, dpr)):
        mine = (wanted == pick_col) & ((pick_row % 8 < 4) == (br == 0))
        dstep = mm_tn(draw, jnp.where(mine, 1.0, 0.0).astype(BF16)).astype(BF16)
        half = dbc[:, br * 256 : br * 256 + 256]
        into = mm_nt(half, wbc[...]) + mm_nt(dstep, sw[...])
        whole = (dx[...] + into).astype(BF16).astype(F32)
        dpre = whole * slope[...]
        out[...] = dpre
        wide = wide + mm_tn(x[...], half)
        thin = thin + mm_tn(x[...], dstep)
        sums = exact(mm, oht[...], dpre, 2, False)
        for k in range(4):
            o = 3 - k if br == 0 else 3 + k
            part = jnp.sum(normed * sums[16 * o : 16 * o + 16], axis=0, keepdims=True)
            taps[k] = taps[k] + part
        bias_row = bias_row + jnp.sum(dpre, axis=0, keepdims=True)
    to_prev[...] = dpf[0:8]
    to_next[...] = dpr[ROWS - 8 : ROWS]
    grads[:, 0:256] = wide
    grads[:, 256:384] = jnp.concatenate([thin, jnp.zeros((256, 64), F32)], axis=1)
    lines[...] = jnp.concatenate(taps + [bias_row, small[0:3]], axis=0)


def normed_kernel(
    dpf, dpr, from_next, from_prev, cw, gain, table, oht, grads, lines,
    gn_ref, cross, send, ahead, behind,
):
    ahead[0:ROWS] = dpf[...]
    ahead[ROWS : ROWS + 8] = from_next[...]
    behind[0:8] = from_prev[...]
    behind[8 : ROWS + 8] = dpr[...]
    dn = jnp.zeros((ROWS, 256), F32)
    for k in range(4):
        dn = dn + cw[k : k + 1] * (ahead[k : k + ROWS] + behind[8 - k : 8 - k + ROWS])
    gn = dn.astype(BF16)
    gn_ref[...] = gn
    own = oht[48:64]
    sums = mm(own, gn)
    rated = exact(mm_tn, own, table[...] * gain[...], 3, False)
    ones = jnp.ones((8, 256), BF16)
    cross[...] = jnp.broadcast_to(
        exact(mm_nt, ones, gn.astype(F32) * rated, 3, False)[None], (GROUPS, 8, ROWS)
    )
    stacked = jnp.concatenate(
        [jnp.zeros((64, 256), F32), sums, lines[...], jnp.zeros((40, 256), F32)], axis=0
    )
    last = grads[:, 256:384] + jnp.transpose(stacked)
    send[:, 0:8, :] = grads[:, 0:128].astype(BF16).reshape(SLICES, 8, 128)
    send[:, 8:16, :] = grads[:, 128:256].astype(BF16).reshape(SLICES, 8, 128)
    send[:, 16:24, :] = last.astype(BF16).reshape(SLICES, 8, 128)


def embedded_kernel(got, gn, gain, table, scale, oht, out, counts):
    total = got[0]
    for k in range(1, GROUPS):
        total = total + got[k]
    cross = columns(total)[:, 0:1]
    own = oht[48:64]
    unit = scale[...]
    turned = exact(mm_tn, own, unit * gain[...], 3, False)
    shrunk = exact(mm_tn, own, table[...] * (unit * unit * unit / D), 3, False)
    out[...] = (turned * gn[...].astype(F32) - shrunk * cross).astype(BF16)
    counts[...] = exact(mm_nt, own, total, 3, False)


def gather_kernel(got, send):
    total = got[0].astype(F32)
    for k in range(1, SLICES):
        total = total + got[k].astype(F32)
    send[...] = jnp.broadcast_to(total.astype(BF16)[None], (SLICES, 24, 128))


def finish_kernel(got, counts, table, scale, gain, gt, gg, gcw, gcb, gwb, gwc, gsw, heads):
    gwb[...] = got[:, 0:8, :].astype(F32).reshape(256, 128)
    gwc[...] = got[:, 8:16, :].astype(F32).reshape(256, 128)
    last = got[:, 16:24, :].astype(F32).reshape(256, 128)
    gsw[...] = last[:, 0:64]
    rows = jnp.transpose(last)
    sums = rows[64:80]
    crossed = counts[0]
    for k in range(1, SLICES):
        crossed = crossed + counts[k]
    unit = scale[...]
    shrunk = table[...] * (unit * unit * unit / D) * crossed[:, 0:1]
    gt[...] = unit * gain[...] * sums - shrunk
    gg[...] = jnp.sum(table[...] * unit * sums, axis=0, keepdims=True)
    gcw[...] = rows[80:84]
    gcb[...] = rows[84:85]
    lane = iota((8, 256), 1)
    tail = rows[80:88]
    picked = iota((8, 128), 1)
    result = jnp.zeros((8, 128), F32)
    for h in range(HEADS):
        part = jnp.sum(jnp.where(lane // 64 == h, tail, 0.0), axis=1, keepdims=True)
        result = jnp.where(picked == h, part, result)
    heads[...] = result


def swap(value, axis):
    return lax.all_to_all(value, axis, 0, 0, tiled=True)


def local(
    token_ids,
    table,
    norm_gain,
    conv_weight,
    conv_bias,
    weight_b,
    weight_c,
    step_weight,
    step_bias,
    log_rate,
    skip_gain,
    out_grad,
):
    size = lax.axis_size("ctx")
    up = [(i, i + 1) for i in range(size - 1)]
    down = [(i + 1, i) for i in range(size - 1)]
    marked = token_ids + 1
    before = lax.ppermute(marked[-3:], "ctx", up)
    after = lax.ppermute(marked[:3], "ctx", down)
    squares = jnp.sum(table * table, axis=1)
    spread = jnp.broadcast_to(squares[None, None, :], (GROUPS, 1, 16))
    spread = jnp.pad(spread, ((0, 0), (0, 0), (0, 112)))
    square_sums = jnp.sum(swap(spread, "fsdp"), axis=(0, 1))[:16]
    scale = lax.rsqrt(square_sums / D + 1e-05)[:, None]
    reach = jnp.concatenate([before, marked, after]) - 1
    ids = jnp.stack([reach[o : o + ROWS] for o in range(7)] + [jnp.full((ROWS,), -1, jnp.int32)])
    gain = norm_gain[None]
    wbc = jnp.concatenate([weight_b, weight_c], axis=1)
    heads_first = jnp.transpose(step_weight).reshape(GROUPS, HEADS, 256)
    swx = jnp.concatenate([heads_first, heads_first], axis=1).reshape(128, 256)
    bias = jnp.tile(step_bias, 2)[:, None]
    rate = jnp.tile(log_rate, 2)[:, None]
    skip = jnp.repeat(skip_gain, 64)[None]

    square = ((ROWS, 256), F32)
    half_square = ((ROWS, 256), BF16)
    xf, xr, gf, gr, part, oht = call(
        tokens_kernel,
        (
            half_square,
            half_square,
            square,
            square,
            ((GROUPS, 24, 512), BF16),
            ((128, 256), BF16),
        ),
        ids, table, scale, gain, conv_weight, conv_bias[None], wbc, swx,
    )
    bc, raw = call(
        reduce_kernel, (((GROUPS, 16, 512), BF16), ((8, 256), F32)), swap(part, "fsdp")
    )
    bc = swap(bc, "fsdp").reshape(ROWS, 512)
    states, cols, rows = call(
        states_kernel,
        (((16, 2, 40, 128), BF16), ((ROWS, 128), F32), ((48, ROWS), F32)),
        bc, raw, bias, rate, xf, xr, out_grad,
    )
    arrived = swap(states.reshape(SLICES, 40, 128), "ctx")
    y0, dxf0, dxr0, dbc0, side, line = call(
        within_kernel,
        (square, square, square, ((ROWS, 512), F32), ((8, ROWS), F32), ((8, ROWS), F32)),
        bc, cols, rows, xf, xr, out_grad, skip,
    )
    (entering,) = call(chain_kernel, (((SLICES, 32, 128), BF16),), arrived)
    entering = swap(entering, "ctx").reshape(16, 2, 32, 128)
    mixer_out, dxf, dxr, dpart, draw, small = call(
        carried_kernel,
        (
            half_square,
            square,
            square,
            ((GROUPS, 16, 512), BF16),
            ((8, 256), BF16),
            ((8, 256), F32),
        ),
        entering, bc, cols, rows, xf, xr, out_grad, y0, dxf0, dxr0, dbc0, side, line, rate,
    )
    (totals,) = call(total_kernel, (((GROUPS, 24, 512), BF16),), swap(dpart, "fsdp"), draw)
    edge = ((8, 256), F32)
    dpf, dpr, to_prev, to_next, grads, lines = call(
        project_back_kernel,
        (square, square, edge, edge, ((256, 384), F32), edge),
        swap(totals, "fsdp"), xf, xr, gf, gr, dxf, dxr, wbc, step_weight, oht, table, scale, gain, small,
    )
    from_next = lax.ppermute(to_prev, "ctx", down)
    from_prev = lax.ppermute(to_next, "ctx", up)
    gn, cross, gsend = pl.pallas_call(
        normed_kernel,
        out_shape=(
            jax.ShapeDtypeStruct((ROWS, 256), BF16),
            jax.ShapeDtypeStruct((GROUPS, 8, ROWS), F32),
            jax.ShapeDtypeStruct((SLICES, 24, 128), BF16),
        ),
        scratch_shapes=[VMEM((ROWS + 8, 256), F32), VMEM((ROWS + 8, 256), F32)],
        name="normed_kernel",
    )(dpf, dpr, from_next, from_prev, conv_weight, gain, table, oht, grads, lines)
    grad_embedded, counts = call(
        embedded_kernel,
        (half_square, ((16, 8), F32)),
        swap(cross, "fsdp"), gn, gain, table, scale, oht,
    )
    (gathered,) = call(gather_kernel, (((SLICES, 24, 128), BF16),), swap(gsend, "ctx"))
    counts = jnp.broadcast_to(counts[None], (SLICES, 16, 8))
    outs = call(
        finish_kernel,
        (
            ((16, 256), F32),
            ((1, 256), F32),
            ((4, 256), F32),
            ((1, 256), F32),
            ((256, 128), F32),
            ((256, 128), F32),
            ((256, 64), F32),
            ((8, 128), F32),
        ),
        swap(gathered, "ctx"), swap(counts, "ctx"), table, scale, gain,
    )
    gt, gg, gcw, gcb, gwb, gwc, gsw, heads = outs
    return (
        mixer_out,
        grad_embedded,
        gt,
        gg[0],
        gcw,
        gcb[0],
        gwb,
        gwc,
        gsw,
        heads[6, :HEADS],
        heads[7, :HEADS],
        heads[5, :HEADS],
    )


def solution(mesh):
    return jax.shard_map(
        local,
        mesh=mesh,
        in_specs=(
            P("ctx"),
            P(None, "fsdp"),
            P("fsdp"),
            P(None, "fsdp"),
            P("fsdp"),
            P("fsdp", None),
            P("fsdp", None),
            P("fsdp", None),
            P("fsdp"),
            P("fsdp"),
            P("fsdp"),
            P("ctx", "fsdp"),
        ),
        out_specs=(
            P("ctx", "fsdp"),
            P("ctx", "fsdp"),
            P(None, "fsdp"),
            P("fsdp"),
            P(None, "fsdp"),
            P("fsdp"),
            P("fsdp", None),
            P("fsdp", None),
            P("fsdp", None),
            P("fsdp"),
            P("fsdp"),
            P("fsdp"),
        ),
        check_vma=False,
    )
```

time: 1400 us -> 262 us (0.19)
  blocking collectives: 515 us -> 78.5 us
  waiting for transfers between devices: 508 us -> 74.3 us
  local copies, waits for them, and re-layouts: 177 us -> 15.3 us
  other arithmetic: 109 us -> 2.96 us
  starting transfers between devices: 16.3 us -> 57.3 us
  matrix products: 38.6 us -> 0 us
  Pallas kernels: 0 us -> 30.8 us
  between operations: 15.4 us -> 0.87 us
    psum x3 -> x0, waiting for transfers between devices: 328 us -> none  [the longest x1 129 us: local(): lax.psum((d_table, d_gain, d_cw, d_cb, gb_f + gb_r, gc_f + gc_r, gs_f + g...]
    psum x4 -> x0, blocking collectives: 259 us -> none  [the longest x1 146 us: local(): lax.psum((d_table, d_gain, d_cw, d_cb, gb_f + gb_r, gc_f + gc_r, gs_f + g...]
    all_gather x5 -> x0, blocking collectives: 256 us -> none  [the longest x2 148 us: carried_in(): lax.all_gather(part.astype(kind), axis)]
    all_gather x4 -> x0, waiting for transfers between devices: 172 us -> none  [the longest x3 88.5 us: carried_in(): lax.all_gather(part.astype(kind), axis)]
    dynamic_slice x257 -> x0, local copies, waits for them, and re-layouts: 127 us -> none  [the longest x192 93.5 us: carried_turn(): part[at].astype(own.dtype)]
    all_to_all x0 -> x4, blocking collectives: none -> 78.5 us  [swap(): return lax.all_to_all(value, axis, 0, 0, tiled=True)]
    all_to_all x0 -> x7, waiting for transfers between devices: none -> 72.5 us  [swap(): return lax.all_to_all(value, axis, 0, 0, tiled=True)]
    convert_element_type x103 -> x0, other arithmetic: 69.4 us -> none  [the longest x96 66.2 us: carried_turn(): part[at].astype(own.dtype)]
  transfers between devices with their start and end apart: 11 -> 11, of which waited for: 7 -> 8; matrix products, arithmetic and copies ran while one was open for 16% -> 4% of each run, Pallas kernels for 0% -> 3%
where the time goes in v1:
time: 262 us; the launch traced here: 260 us
  blocking collectives  78.5 us (30%)
  waiting for transfers between devices  74.3 us (28%)
  starting transfers between devices  57.3 us (22%)
  Pallas kernels  30.8 us (12%)
  local copies, waits for them, and re-layouts  15.3 us (6%)
  other arithmetic  2.96 us (1%)
    all_to_all x4, blocking collectives, swap(): return lax.all_to_all(value, axis, 0, 0, tiled=True)  78.5 us
    all_to_all x7, waiting for transfers between devices, swap(): return lax.all_to_all(value, axis, 0, 0, tiled=True)  72.5 us
    all_to_all x7, starting transfers between devices, swap(): return lax.all_to_all(value, axis, 0, 0, tiled=True)  41.7 us
    pallas_call x11, Pallas kernels, call(): return pl.pallas_call(kernel, out_shape=shapes, name=kernel.__name__)(*args)  28.1 us
    unnamed x32, local copies, waits for them, and re-layouts  7.71 us
    ppermute x1, starting transfers between devices, local(): from_prev = lax.ppermute(to_next, 'ctx', up)  5.4 us
  transfers between devices with their start and end apart: 11, of which 8 were waited for; matrix products, arithmetic and copies ran while one was open for 4% of the time, Pallas kernels for 3%

profile of v1, /device:TPU:6, one launch (start us, length us, event | category | flops | bytes accessed | tf_op | source)
XLA Modules:
  0.0 260.0 jit_solution(4107580059589879315)
XLA Ops:
  1.4 4.7 %collective-permute-start = (s32[3]{0:T(128)S(1)}, s32[3]{0:T(128)S(1)}, u32[]{:S(2)}, u32[]{:S(2)}) collective-permute-start(s32[3]{0:T(128)S(1)} %get-tuple-element.154), channel_id=1, source_target_pairs={{0,1},{1,2},{2,3},{3,4},{4,5},{5,6},{6,7},{7,8},{8,9},{9,10},{10,1... | collective-permute-start | bytes 44 | tf_op jit(solution)/shard_map/ppermute | solution.py:462
  6.1 2.7 %collective-permute-start.1 = (s32[3]{0:T(128)S(1)}, s32[3]{0:T(128)S(1)}, u32[]{:S(2)}, u32[]{:S(2)}) collective-permute-start(s32[3]{0:T(128)S(1)} %get-tuple-element.155), channel_id=1, source_target_pairs={{1,0},{2,1},{3,2},{4,3},{5,4},{6,5},{7,6},{8,7},{9,8},{10,9},{11,1... | collective-permute-start | bytes 44 | tf_op jit(solution)/shard_map/ppermute | solution.py:463
  8.7 0.8 multiply_reduce_fusion
  10.2 5.9 %all-to-all-start = ((f32[16,1,128]{2,1,0:T(1,128)}), f32[16,1,128]{2,1,0:T(1,128)S(1)}, u32[]{:S(2)}, u32[]{:S(2)}) async-start(f32[16,1,128]{2,1,0:T(1,128)} %pad.7), calls=%async_computation | async-start | bytes 16384 | tf_op jit(solution)/shard_map/all_to_all | solution.py:441
  16.1 0.9 constant_dynamic-update-slice_fusion.1
  18.7 2.1 all-to-all-done
  21.5 2.6 tokens_kernel.1
  24.1 13.8 %all_to_all.55.got = bf16[16,24,512]{2,1,0:T(8,128)(2,1)} all-to-all(bf16[16,24,512]{2,1,0:T(8,128)(2,1)} %get-tuple-element.54), channel_id=1, replica_groups=mesh['fsdp'=16,'ctx'=32] {'fsdp'}, dimensions={0} | all-to-all | bytes 786432 | tf_op jit(solution)/shard_map/all_to_all | solution.py:441
  37.9 1.7 reduce_kernel.1
  39.6 4.7 %all-to-all-start.2 = ((bf16[16,16,512]{2,1,0:T(8,128)(2,1)}), bf16[16,16,512]{2,1,0:T(8,128)(2,1)S(1)}, u32[]{:S(2)}, u32[]{:S(2)}) async-start(bf16[16,16,512]{2,1,0:T(8,128)(2,1)} %get-tuple-element.55), calls=%async_computation.2 | async-start | bytes 524288 | tf_op jit(solution)/shard_map/all_to_all | solution.py:441
  45.7 5.4 %all-to-all-done.2 = bf16[16,16,512]{2,1,0:T(8,128)(2,1)S(1)} async-done(((bf16[16,16,512]{2,1,0:T(8,128)(2,1)}), bf16[16,16,512]{2,1,0:T(8,128)(2,1)S(1)}, u32[]{:S(2)}, u32[]{:S(2)}) %all-to-all-start.2) | async-done | bytes 262176 | tf_op jit(solution)/shard_map/all_to_all | solution.py:441
  51.1 0.7 copy-done
  51.8 3.3 %states_kernel.1 = (bf16[16,2,40,128]{3,2,1,0:T(8,128)(2,1)}, f32[256,128]{1,0:T(8,128)}, f32[48,256]{1,0:T(8,128)}) custom-call(bf16[256,512]{1,0:T(8,128)(2,1)} %bitcast.29, f32[8,256]{1,0:T(8,128)} %get-tuple-element.56.raw, f32[8,1]{1,0:T(8,128)} %broadcast_in_dim_tile.8.bias, f32[8,1]{1,0:T(8,128)} %broadcast_in_dim_tile.9.rate, ...), custom_call_target="tpu_custom_call" | custom-call | tf_op jit(solution)/shard_map/states_kernel/pallas_call | solution.py:21
  55.1 43.5 %all_to_all.56.got = bf16[32,40,128]{2,1,0:T(8,128)(2,1)} all-to-all(bf16[32,40,128]{2,1,0:T(8,128)(2,1)} %bitcast.34), channel_id=1, replica_groups=mesh['fsdp'=16,'ctx'=32] {'ctx'}, dimensions={0} | all-to-all | bytes 655360 | tf_op jit(solution)/shard_map/all_to_all | solution.py:441
  98.6 1.8 chain_kernel.1
  100.3 5.3 %all-to-all-start.4 = ((bf16[32,32,128]{2,1,0:T(8,128)(2,1)}), bf16[32,32,128]{2,1,0:T(8,128)(2,1)S(1)}, u32[]{:S(2)}, u32[]{:S(2)}) async-start(bf16[32,32,128]{2,1,0:T(8,128)(2,1)} %chain_kernel.1), calls=%async_computation.4 | async-start | bytes 524288 | tf_op jit(solution)/shard_map/all_to_all | solution.py:441
  106.3 4.2 %within_kernel.1 = (f32[256,256]{1,0:T(8,128)}, f32[256,256]{1,0:T(8,128)}, f32[256,256]{1,0:T(8,128)}, f32[256,512]{1,0:T(8,128)}, f32[8,256]{1,0:T(8,128)}, /*index=5*/f32[8,256]{1,0:T(8,128)}) custom-call(bf16[256,512]{1,0:T(8,128)(2,1)} %bitcast.30, f32[256,128]{1,0:T(8,128)} %get-tuple-element.60.cols_ref, f32[48,256]{1,0:T(8,128)} %get-tuple-element.61.rows_ref, ...), custom_call_target="tpu_custom_call" | custom-call | tf_op jit(solution)/shard_map/within_kernel/pallas_call | solution.py:21
  110.5 16.3 %all-to-all-done.4 = bf16[32,32,128]{2,1,0:T(8,128)(2,1)S(1)} async-done(((bf16[32,32,128]{2,1,0:T(8,128)(2,1)}), bf16[32,32,128]{2,1,0:T(8,128)(2,1)S(1)}, u32[]{:S(2)}, u32[]{:S(2)}) %all-to-all-start.4) | async-done | bytes 262176 | tf_op jit(solution)/shard_map/all_to_all | solution.py:441
  126.8 0.7 copy-done.2
  127.5 3.9 %carried_kernel.1 = (bf16[256,256]{1,0:T(8,128)(2,1)}, f32[256,256]{1,0:T(8,128)}, f32[256,256]{1,0:T(8,128)}, bf16[16,16,512]{2,1,0:T(8,128)(2,1)}, bf16[8,256]{1,0:T(8,128)(2,1)}, /*index=5*/f32[8,256]{1,0:T(8,128)}) custom-call(bf16[16,2,32,128]{3,2,1,0:T(8,128)(2,1)} %bitcast.32, bf16[256,512]{1,0:T(8,128)(2,1)} %bitcast.31, ...), custom_call_target="tpu_custom_call" | custom-call | tf_op jit(solution)/shard_map/carried_kernel/pallas_call | solution.py:21
  131.5 11.0 %all_to_all.57.got = bf16[16,16,512]{2,1,0:T(8,128)(2,1)} all-to-all(bf16[16,16,512]{2,1,0:T(8,128)(2,1)} %get-tuple-element.69), channel_id=1, replica_groups=mesh['fsdp'=16,'ctx'=32] {'fsdp'}, dimensions={0} | all-to-all | bytes 524288 | tf_op jit(solution)/shard_map/all_to_all | solution.py:441
  142.4 1.7 total_kernel.1
  144.1 4.7 %all-to-all-start.6 = ((bf16[16,24,512]{2,1,0:T(8,128)(2,1)}), bf16[16,24,512]{2,1,0:T(8,128)(2,1)S(1)}, u32[]{:S(2)}, u32[]{:S(2)}) async-start(bf16[16,24,512]{2,1,0:T(8,128)(2,1)} %total_kernel.1), calls=%async_computation.6 | async-start | bytes 786432 | tf_op jit(solution)/shard_map/all_to_all | solution.py:441
  148.9 0.7 copy.60.sw
  149.6 7.6 %all-to-all-done.6.got = bf16[16,24,512]{2,1,0:T(8,128)(2,1)S(1)} async-done(((bf16[16,24,512]{2,1,0:T(8,128)(2,1)}), bf16[16,24,512]{2,1,0:T(8,128)(2,1)S(1)}, u32[]{:S(2)}, u32[]{:S(2)}) %all-to-all-start.6) | async-done | bytes 393248 | tf_op jit(solution)/shard_map/all_to_all | solution.py:441
  157.2 0.8 copy-done.1
  158.0 3.2 %project_back_kernel.1 = (f32[256,256]{1,0:T(8,128)}, f32[256,256]{1,0:T(8,128)}, f32[8,256]{1,0:T(8,128)}, f32[8,256]{1,0:T(8,128)}, f32[256,384]{1,0:T(8,128)}, /*index=5*/f32[8,256]{1,0:T(8,128)}) custom-call(bf16[16,24,512]{2,1,0:T(8,128)(2,1)} %copy-done.1, bf16[256,256]{1,0:T(8,128)(2,1)} %get-tuple-element.57.xf, ...), custom_call_target="tpu_custom_call" | custom-call | tf_op jit(solution)/shard_map/project_back_kernel/pallas_call | solution.py:21
  161.2 2.8 %collective-permute-start.2 = (f32[8,256]{1,0:T(8,128)}, f32[8,256]{1,0:T(8,128)S(1)}, u32[]{:S(2)}, u32[]{:S(2)}) collective-permute-start(f32[8,256]{1,0:T(8,128)} %get-tuple-element.79), channel_id=1, source_target_pairs={{1,0},{2,1},{3,2},{4,3},{5,4},{6,5},{7,6},{8,7},{9,8},{10,9},{11,1... | collective-permute-start | bytes 24584 | tf_op jit(solution)/shard_map/ppermute | solution.py:529
  164.1 5.4 %collective-permute-start.3 = (f32[8,256]{1,0:T(8,128)}, f32[8,256]{1,0:T(8,128)S(1)}, u32[]{:S(2)}, u32[]{:S(2)}) collective-permute-start(f32[8,256]{1,0:T(8,128)} %get-tuple-element.80), channel_id=1, source_target_pairs={{0,1},{1,2},{2,3},{3,4},{4,5},{5,6},{6,7},{7,8},{8,9},{9,10},{10,1... | collective-permute-start | bytes 24584 | tf_op jit(solution)/shard_map/ppermute | solution.py:530
  169.5 1.8 collective-permute-done.3.from_prev
  171.9 2.7 %normed_kernel.1 = (bf16[256,256]{1,0:T(8,128)(2,1)}, f32[16,8,256]{2,1,0:T(8,128)}, bf16[32,24,128]{2,1,0:T(8,128)(2,1)}) custom-call(f32[256,256]{1,0:T(8,128)} %get-tuple-element.77.dpf, f32[256,256]{1,0:T(8,128)} %get-tuple-element.78.dpr, f32[8,256]{1,0:T(8,128)} %copy-done.8, f32[8,256]{1,0:T(8,128)} %copy-done.9, f32[4,256]{1,0:T(4,128)} %cw.3, ...), custom_call_target="tpu_custom_call" | custom-call | tf_op jit(solution)/shard_map/normed_kernel/pallas_call | solution.py:531
  174.6 10.2 %all_to_all.58.got = f32[16,8,256]{2,1,0:T(8,128)} all-to-all(f32[16,8,256]{2,1,0:T(8,128)} %get-tuple-element.83), channel_id=1, replica_groups=mesh['fsdp'=16,'ctx'=32] {'fsdp'}, dimensions={0} | all-to-all | bytes 262144 | tf_op jit(solution)/shard_map/all_to_all | solution.py:441
  184.9 9.6 %all-to-all-start.8 = ((bf16[32,24,128]{2,1,0:T(8,128)(2,1)}), bf16[32,24,128]{2,1,0:T(8,128)(2,1)S(1)}, u32[]{:S(2)}, u32[]{:S(2)}) async-start(bf16[32,24,128]{2,1,0:T(8,128)(2,1)} %get-tuple-element.86), calls=%async_computation.8 | async-start | bytes 393216 | tf_op jit(solution)/shard_map/all_to_all | solution.py:441
  194.5 2.1 embedded_kernel.1
  196.6 0.8 copy.63
  197.4 0.7 reshape.50
  198.1 15.5 %all-to-all-done.8.got = bf16[32,24,128]{2,1,0:T(8,128)(2,1)S(1)} async-done(((bf16[32,24,128]{2,1,0:T(8,128)(2,1)}), bf16[32,24,128]{2,1,0:T(8,128)(2,1)S(1)}, u32[]{:S(2)}, u32[]{:S(2)}) %all-to-all-start.8) | async-done | bytes 196640 | tf_op jit(solution)/shard_map/all_to_all | solution.py:441
  213.5 5.1 %all-to-all-start.10 = ((f32[32,1,128]{2,1,0:T(1,128)}), f32[32,1,128]{2,1,0:T(1,128)S(1)}, u32[]{:S(2)}, u32[]{:S(2)}) async-start(f32[32,1,128]{2,1,0:T(1,128)} %reshape.50), calls=%async_computation.10 | async-start | bytes 32768 | tf_op jit(solution)/shard_map/all_to_all | solution.py:441
  218.6 1.7 gather_kernel.1
  220.3 10.4 %all-to-all-done.10 = f32[32,1,128]{2,1,0:T(1,128)S(1)} async-done(((f32[32,1,128]{2,1,0:T(1,128)}), f32[32,1,128]{2,1,0:T(1,128)S(1)}, u32[]{:S(2)}, u32[]{:S(2)}) %all-to-all-start.10) | async-done | bytes 16416 | tf_op jit(solution)/shard_map/all_to_all | solution.py:441
  230.7 6.3 %all-to-all-start.9 = ((bf16[32,24,128]{2,1,0:T(8,128)(2,1)}), bf16[32,24,128]{2,1,0:T(8,128)(2,1)S(1)}, u32[]{:S(2)}, u32[]{:S(2)}) async-start(bf16[32,24,128]{2,1,0:T(8,128)(2,1)} %gather_kernel.1), calls=%async_computation.9 | async-start | bytes 393216 | tf_op jit(solution)/shard_map/all_to_all | solution.py:441
  237.6 0.7 reduce
  238.4 0.8 copy.64.counts
  239.2 15.3 %all-to-all-done.9.got = bf16[32,24,128]{2,1,0:T(8,128)(2,1)S(1)} async-done(((bf16[32,24,128]{2,1,0:T(8,128)(2,1)}), bf16[32,24,128]{2,1,0:T(8,128)(2,1)S(1)}, u32[]{:S(2)}, u32[]{:S(2)}) %all-to-all-start.9) | async-done | bytes 196640 | tf_op jit(solution)/shard_map/all_to_all | solution.py:441
  254.5 0.7 copy-done.5
  255.2 1.9 finish_kernel.1
  257.0 1.6 copy.66
  258.7 1.3 slice_bitcast_fusion
  (48 shorter events, 7.0 us)
Async XLA Ops:
  1.4 16.5 %collective-permute-start = (s32[3]{0:T(128)S(1)}, s32[3]{0:T(128)S(1)}, u32[]{:S(2)}, u32[]{:S(2)}) collective-permute-start(s32[3]{0:T(128)S(1)} %get-tuple-element.154), channel_id=1, source_target_pairs={{0,1},{1,2},{2,3},{3,4},{4,5},{5,6},{6,7},{7,8},{8,9},{9,10},{10,1... | collective-permute-start | bytes 44 | tf_op jit(solution)/shard_map/ppermute | solution.py:462
  6.1 11.9 %collective-permute-start.1 = (s32[3]{0:T(128)S(1)}, s32[3]{0:T(128)S(1)}, u32[]{:S(2)}, u32[]{:S(2)}) collective-permute-start(s32[3]{0:T(128)S(1)} %get-tuple-element.155), channel_id=1, source_target_pairs={{1,0},{2,1},{3,2},{4,3},{5,4},{6,5},{7,6},{8,7},{9,8},{10,9},{11,1... | collective-permute-start | bytes 44 | tf_op jit(solution)/shard_map/ppermute | solution.py:463
  10.2 10.6 %all-to-all-start = ((f32[16,1,128]{2,1,0:T(1,128)}), f32[16,1,128]{2,1,0:T(1,128)S(1)}, u32[]{:S(2)}, u32[]{:S(2)}) async-start(f32[16,1,128]{2,1,0:T(1,128)} %pad.7), calls=%async_computation | async-start | bytes 16384 | tf_op jit(solution)/shard_map/all_to_all | solution.py:441
  16.1 0.9 copy-start.6
  17.0 0.8 copy-start.7
  17.9 3.6 %copy-start.3 = (bf16[256,256]{1,0:T(8,128)(2,1)}, bf16[256,256]{1,0:T(8,128)(2,1)S(1)}, u32[]{:S(2)}) copy-start(bf16[256,256]{1,0:T(8,128)(2,1)S(1)} %constant_dynamic-update-slice_fusion.wbc) | copy-start | bytes 393220
  39.6 4.7 %copy-start.11 = (f32[4]{0:T(128)S(1)}, f32[4]{0:T(128)}, u32[]{:S(2)}) copy-start(f32[4]{0:T(128)} %param.21) | copy-start | bytes 52
  39.6 11.5 %all-to-all-start.2 = ((bf16[16,16,512]{2,1,0:T(8,128)(2,1)}), bf16[16,16,512]{2,1,0:T(8,128)(2,1)S(1)}, u32[]{:S(2)}, u32[]{:S(2)}) async-start(bf16[16,16,512]{2,1,0:T(8,128)(2,1)} %get-tuple-element.55), calls=%async_computation.2 | async-start | bytes 524288 | tf_op jit(solution)/shard_map/all_to_all | solution.py:441
  44.4 0.7 copy-start.12
  51.1 0.7 copy-start
  100.3 5.3 %copy-start.10 = (f32[4]{0:T(128)S(1)}, f32[4]{0:T(128)}, u32[]{:S(2)}) copy-start(f32[4]{0:T(128)} %param.22) | copy-start | bytes 52
  100.3 26.5 %all-to-all-start.4 = ((bf16[32,32,128]{2,1,0:T(8,128)(2,1)}), bf16[32,32,128]{2,1,0:T(8,128)(2,1)S(1)}, u32[]{:S(2)}, u32[]{:S(2)}) async-start(bf16[32,32,128]{2,1,0:T(8,128)(2,1)} %chain_kernel.1), calls=%async_computation.4 | async-start | bytes 524288 | tf_op jit(solution)/shard_map/all_to_all | solution.py:441
  126.8 0.7 copy-start.2
  144.1 13.1 %all-to-all-start.6 = ((bf16[16,24,512]{2,1,0:T(8,128)(2,1)}), bf16[16,24,512]{2,1,0:T(8,128)(2,1)S(1)}, u32[]{:S(2)}, u32[]{:S(2)}) async-start(bf16[16,24,512]{2,1,0:T(8,128)(2,1)} %total_kernel.1), calls=%async_computation.6 | async-start | bytes 786432 | tf_op jit(solution)/shard_map/all_to_all | solution.py:441
  157.2 0.8 copy-start.1
  161.2 8.3 %collective-permute-start.2 = (f32[8,256]{1,0:T(8,128)}, f32[8,256]{1,0:T(8,128)S(1)}, u32[]{:S(2)}, u32[]{:S(2)}) collective-permute-start(f32[8,256]{1,0:T(8,128)} %get-tuple-element.79), channel_id=1, source_target_pairs={{1,0},{2,1},{3,2},{4,3},{5,4},{6,5},{7,6},{8,7},{9,8},{10,9},{11,1... | collective-permute-start | bytes 24584 | tf_op jit(solution)/shard_map/ppermute | solution.py:529
  164.1 7.3 %collective-permute-start.3 = (f32[8,256]{1,0:T(8,128)}, f32[8,256]{1,0:T(8,128)S(1)}, u32[]{:S(2)}, u32[]{:S(2)}) collective-permute-start(f32[8,256]{1,0:T(8,128)} %get-tuple-element.80), channel_id=1, source_target_pairs={{0,1},{1,2},{2,3},{3,4},{4,5},{5,6},{6,7},{7,8},{8,9},{9,10},{10,1... | collective-permute-start | bytes 24584 | tf_op jit(solution)/shard_map/ppermute | solution.py:530
  169.5 1.8 copy-start.8
  171.3 0.6 copy-start.9
  184.9 28.7 %all-to-all-start.8 = ((bf16[32,24,128]{2,1,0:T(8,128)(2,1)}), bf16[32,24,128]{2,1,0:T(8,128)(2,1)S(1)}, u32[]{:S(2)}, u32[]{:S(2)}) async-start(bf16[32,24,128]{2,1,0:T(8,128)(2,1)} %get-tuple-element.86), calls=%async_computation.8 | async-start | bytes 393216 | tf_op jit(solution)/shard_map/all_to_all | solution.py:441
  213.5 5.1 %copy-start.4 = (bf16[32,24,128]{2,1,0:T(8,128)(2,1)}, bf16[32,24,128]{2,1,0:T(8,128)(2,1)S(1)}, u32[]{:S(2)}) copy-start(bf16[32,24,128]{2,1,0:T(8,128)(2,1)S(1)} %all-to-all-done.8.got) | copy-start | bytes 589828
  213.5 17.2 %all-to-all-start.10 = ((f32[32,1,128]{2,1,0:T(1,128)}), f32[32,1,128]{2,1,0:T(1,128)S(1)}, u32[]{:S(2)}, u32[]{:S(2)}) async-start(f32[32,1,128]{2,1,0:T(1,128)} %reshape.50), calls=%async_computation.10 | async-start | bytes 32768 | tf_op jit(solution)/shard_map/all_to_all | solution.py:441
  230.7 23.7 %all-to-all-start.9 = ((bf16[32,24,128]{2,1,0:T(8,128)(2,1)}), bf16[32,24,128]{2,1,0:T(8,128)(2,1)S(1)}, u32[]{:S(2)}, u32[]{:S(2)}) async-start(bf16[32,24,128]{2,1,0:T(8,128)(2,1)} %gather_kernel.1), calls=%async_computation.9 | async-start | bytes 393216 | tf_op jit(solution)/shard_map/all_to_all | solution.py:441
  254.5 0.7 copy-start.5

commit v2 on v1

--- a/solution.py
+++ b/solution.py
@@ -16,9 +16,18 @@
 VMEM = pltpu.VMEM
 
 
-def call(kernel, outs, *args):
-    shapes = tuple(jax.ShapeDtypeStruct(shape, kind) for shape, kind in outs)
-    return pl.pallas_call(kernel, out_shape=shapes, name=kernel.__name__)(*args)
+def call(kernel, outs, *args, final=(), scratch=()):
+    shapes = tuple(
+        jax.ShapeDtypeStruct(shape, kind) if i in final else VMEM(shape, kind)
+        for i, (shape, kind) in enumerate(outs)
+    )
+    near = [pltpu.with_memory_space_constraint(arg, VMEM) for arg in args]
+    return pl.pallas_call(
+        kernel,
+        out_shape=shapes,
+        scratch_shapes=scratch,
+        compiler_params=pltpu.CompilerParams(vmem_limit_bytes=24 << 20),
+    )(*near)
 
 
 def iota(shape, dim):
@@ -83,10 +92,39 @@
     return jnp.where(before, 1.0, 0.0).astype(BF16), jnp.where(after, 1.0, 0.0).astype(BF16)
 
 
-def tokens_kernel(ids, table, scale, gain, cw, cb, wbc, swx, xf, xr, gf, gr, send, oht_ref):
-    normed = (table[...] * scale[...] * gain[...]).astype(BF16).astype(F32)
-    vocab = iota((16, ROWS), 0)
-    hits = [jnp.where(ids[o : o + 1, :] == vocab, 1.0, 0.0) for o in range(8)]
+def squares_kernel(table, send):
+    squares = jnp.concatenate([table[...] * table[...], jnp.zeros((112, 256), F32)], axis=0)
+    sums = exact(mm_nt, jnp.ones((8, 256), BF16), squares, 3, False)
+    send[...] = jnp.broadcast_to(sums[0:1][None], (GROUPS, 1, 128))
+
+
+def tokens_kernel(
+    ids, ids_prev, ids_next, got, table, gain, cw, cb, wbc, swx,
+    xf, xr, gf, gr, send, oht_ref, scale,
+):
+    total = got[0]
+    for k in range(1, GROUPS):
+        total = total + got[k]
+    unit = lax.rsqrt(total / D + 1e-05)
+    spread = jnp.transpose(jnp.broadcast_to(unit, (128, 128)))[0:16]
+    scale[...] = spread
+    unit = spread[:, 0:1]
+    normed = (table[...] * unit * gain[...]).astype(BF16).astype(F32)
+    vocab = iota((16, ROWS), 0) + 1
+    lane = iota((1, ROWS), 1)
+    here = ids[...]
+    hits = []
+    for o in range(7):
+        d = o - 3
+        if d == 0:
+            moved = here
+        elif d > 0:
+            ahead = pltpu.roll(ids_next[...], ROWS - d, 1)
+            moved = jnp.where(lane < ROWS - d, pltpu.roll(here, ROWS - d, 1), ahead)
+        else:
+            moved = jnp.where(lane >= -d, pltpu.roll(here, -d, 1), pltpu.roll(ids_prev[...], -d, 1))
+        hits.append(jnp.where(moved == vocab, 1.0, 0.0))
+    hits.append(jnp.zeros((16, ROWS), F32))
     oht = jnp.concatenate(hits, axis=0).astype(BF16)
     oht_ref[...] = oht
     none = jnp.zeros((16, 256), F32)
@@ -120,7 +158,10 @@
     raw[...] = total[16:24, 0:256] + total[16:24, 256:512]
 
 
-def states_kernel(bc, raw, bias, rate, xf, xr, dy, send, cols_ref, rows_ref):
+def steps_kernel(
+    raw, bias, rate, xf, xr, dy,
+    cols_ref, rows_ref, weight_ref, grown_ref, weighted_ref, turned_ref, packed_ref,
+):
     shifted = raw[...] + bias[...]
     step = jnp.maximum(shifted, 0.0) + jnp.log1p(jnp.exp(-jnp.abs(shifted)))
     slope = 1.0 / (1.0 + jnp.exp(-shifted))
@@ -140,19 +181,13 @@
     cols_ref[...] = cols
     masks = head_masks(ROWS)
     dyf = dy[...].astype(F32)
-    found = []
     for br, x in ((0, xf), (1, xr)):
-        b = bc[:, br * 256 : br * 256 + 128]
-        c = bc[:, br * 256 + 128 : br * 256 + 256]
-        weighted = (expand(cols, 16 + 4 * br, masks) * x[...].astype(F32)).astype(BF16)
-        final = mm_tn(b, weighted)
-        turned = (expand(cols, 24 + 4 * br, masks) * dyf).astype(BF16)
-        found.append((final, mm_tn(c, turned)))
-    chains = (found[0][0], found[1][1], found[1][0], found[0][1])
-    for ch, state in enumerate(chains):
-        for hp in range(2):
-            part = state[:, hp * 128 : hp * 128 + 128].astype(BF16).reshape(16, 8, 128)
-            send[:, hp, ch * 8 : ch * 8 + 8, :] = part
+        weight_wide = expand(cols, 16 + 4 * br, masks)
+        grown_wide = expand(cols, 24 + 4 * br, masks)
+        weight_ref[br] = weight_wide
+        grown_ref[br] = grown_wide
+        weighted_ref[br] = (weight_wide * x[...].astype(F32)).astype(BF16)
+        turned_ref[br] = (grown_wide * dyf).astype(BF16)
     decay = jnp.exp(ending)
     left = iota((1, 128), 1) < 64
     row = iota((8, 128), 0)
@@ -165,7 +200,22 @@
         packed = jnp.where(row == 1, fd - f_high, packed)
         packed = jnp.where(row == 2, r_high, packed)
         packed = jnp.where(row == 3, rd - r_high, packed)
-        send[:, hp, 32:40, :] = jnp.broadcast_to(packed.astype(BF16)[None], (16, 8, 128))
+        packed_ref[hp] = packed
+
+
+def states_kernel(bc, weighted, turned, packed, send):
+    found = []
+    for br in range(2):
+        b = bc[:, br * 256 : br * 256 + 128]
+        c = bc[:, br * 256 + 128 : br * 256 + 256]
+        found.append((mm_tn(b, weighted[br]), mm_tn(c, turned[br])))
+    chains = (found[0][0], found[1][1], found[1][0], found[0][1])
+    for ch, state in enumerate(chains):
+        for hp in range(2):
+            part = state[:, hp * 128 : hp * 128 + 128].astype(BF16).reshape(16, 8, 128)
+            send[:, hp, ch * 8 : ch * 8 + 8, :] = part
+    for hp in range(2):
+        send[:, hp, 32:40, :] = jnp.broadcast_to(packed[hp].astype(BF16)[None], (16, 8, 128))
 
 
 def chain_kernel(got, out):
@@ -236,11 +286,10 @@
 
 
 def carried_kernel(
-    got, bc, cols_ref, rows_ref, xf, xr, dy, y0, dxf0, dxr0, dbc0, side, line, rate,
+    got, bc, weight_ref, grown_ref, weighted, turned, rows_ref, xf, xr, dy,
+    y0, dxf0, dxr0, dbc0, side, line, rate,
     out, dxf, dxr, send, draw_ref, small,
 ):
-    masks = head_masks(ROWS)
-    cols = cols_ref[...]
     dyf = dy[...].astype(F32)
 
     def state(ch):
@@ -262,18 +311,16 @@
         ahead_half = ahead.astype(BF16)
         b = bc[:, br * 256 : br * 256 + 128]
         c = bc[:, br * 256 + 128 : br * 256 + 256]
-        grown = expand(cols, 24 + 4 * br, masks)
-        weight = expand(cols, 16 + 4 * br, masks)
         heads = jnp.where(lane_head + 4 * br == row_at, 1.0, 0.0).astype(BF16)
-        carried = grown * mm(c, start_half)
+        carried = grown_ref[br] * mm(c, start_half)
         total = total + carried
         dp = dp + exact(mm_nt, heads, dyf * carried, 2, False)
         xv = x[...].astype(F32)
         toward = mm(b, ahead_half)
-        dx_ref[...] = dx0[...] + weight * toward
+        dx_ref[...] = dx0[...] + weight_ref[br] * toward
         dw = dw + exact(mm_nt, heads, xv * toward, 2, False)
-        dc = mm_nt((grown * dyf).astype(BF16), start_half)
-        db = mm_nt((weight * xv).astype(BF16), ahead_half)
+        dc = mm_nt(turned[br], start_half)
+        db = mm_nt(weighted[br], ahead_half)
         at = br * 256
         send[:, :, at : at + 128] = (dbc0[:, at : at + 128] + db).astype(BF16).reshape(16, 16, 128)
         send[:, :, at + 128 : at + 256] = (
@@ -326,24 +373,25 @@
 
 
 def project_back_kernel(
-    got, xf, xr, gf, gr, dxf, dxr, wbc, sw, oht, table, scale, gain, small,
-    dpf, dpr, to_prev, to_next, grads, lines,
+    got, xf, xr, gf, gr, dxf, dxr, wbc, swt, oht, table, scale, gain, cw, small,
+    dpf, dpr, to_prev, to_next, send, cpart,
 ):
     dbc = got[:, 0:16, :].reshape(ROWS, 512)
     draw = got[:, 16:24, 0:256].astype(F32).reshape(128, 256).astype(BF16)
     pick_row = iota((128, 64), 0)
     pick_col = iota((128, 64), 1)
     wanted = pick_row // 8 * 4 + pick_row % 4
-    normed = (table[...] * scale[...] * gain[...]).astype(BF16).astype(F32)
+    normed = (table[...] * scale[:, 0:1] * gain[...]).astype(BF16).astype(F32)
     taps = [jnp.zeros((1, 256), F32)] * 4
     bias_row = jnp.zeros((1, 256), F32)
     wide = jnp.zeros((256, 256), F32)
     thin = jnp.zeros((256, 64), F32)
+    ids_sum = jnp.zeros((16, 256), F32)
     for br, x, slope, dx, out in ((0, xf, gf, dxf, dpf), (1, xr, gr, dxr, dpr)):
         mine = (wanted == pick_col) & ((pick_row % 8 < 4) == (br == 0))
         dstep = mm_tn(draw, jnp.where(mine, 1.0, 0.0).astype(BF16)).astype(BF16)
         half = dbc[:, br * 256 : br * 256 + 256]
-        into = mm_nt(half, wbc[...]) + mm_nt(dstep, sw[...])
+        into = mm_nt(half, wbc[...]) + mm(dstep, swt[...])
         whole = (dx[...] + into).astype(BF16).astype(F32)
         dpre = whole * slope[...]
         out[...] = dpre
@@ -352,19 +400,31 @@
         sums = exact(mm, oht[...], dpre, 2, False)
         for k in range(4):
             o = 3 - k if br == 0 else 3 + k
-            part = jnp.sum(normed * sums[16 * o : 16 * o + 16], axis=0, keepdims=True)
+            block = sums[16 * o : 16 * o + 16]
+            ids_sum = ids_sum + cw[k : k + 1] * block
+            part = jnp.sum(normed * block, axis=0, keepdims=True)
             taps[k] = taps[k] + part
         bias_row = bias_row + jnp.sum(dpre, axis=0, keepdims=True)
     to_prev[...] = dpf[0:8]
     to_next[...] = dpr[ROWS - 8 : ROWS]
-    grads[:, 0:256] = wide
-    grads[:, 256:384] = jnp.concatenate([thin, jnp.zeros((256, 64), F32)], axis=1)
-    lines[...] = jnp.concatenate(taps + [bias_row, small[0:3]], axis=0)
+    shared = table[...] * gain[...] * ids_sum
+    placed = jnp.concatenate(
+        [jnp.zeros((88, 256), F32), shared, jnp.zeros((24, 256), F32)], axis=0
+    )
+    cpart[...] = exact(mm_nt, jnp.ones((8, 256), BF16), placed, 3, False)[0:1]
+    stacked = jnp.concatenate(
+        [jnp.zeros((64, 256), F32), ids_sum] + taps + [bias_row, small[0:3], jnp.zeros((40, 256), F32)],
+        axis=0,
+    )
+    last = jnp.concatenate([thin, jnp.zeros((256, 64), F32)], axis=1) + jnp.transpose(stacked)
+    send[:, 0:8, :] = wide[:, 0:128].astype(BF16).reshape(SLICES, 8, 128)
+    send[:, 8:16, :] = wide[:, 128:256].astype(BF16).reshape(SLICES, 8, 128)
+    send[:, 16:24, :] = last.astype(BF16).reshape(SLICES, 8, 128)
 
 
 def normed_kernel(
-    dpf, dpr, from_next, from_prev, cw, gain, table, oht, grads, lines,
-    gn_ref, cross, send, ahead, behind,
+    dpf, dpr, from_next, from_prev, cw, gain, table, oht, cpart,
+    gn_ref, cross, ahead, behind,
 ):
     ahead[0:ROWS] = dpf[...]
     ahead[ROWS : ROWS + 8] = from_next[...]
@@ -375,73 +435,72 @@
         dn = dn + cw[k : k + 1] * (ahead[k : k + ROWS] + behind[8 - k : 8 - k + ROWS])
     gn = dn.astype(BF16)
     gn_ref[...] = gn
-    own = oht[48:64]
-    sums = mm(own, gn)
-    rated = exact(mm_tn, own, table[...] * gain[...], 3, False)
+    rated = exact(mm_tn, oht[48:64], table[...] * gain[...], 3, False)
     ones = jnp.ones((8, 256), BF16)
-    cross[...] = jnp.broadcast_to(
-        exact(mm_nt, ones, gn.astype(F32) * rated, 3, False)[None], (GROUPS, 8, ROWS)
-    )
-    stacked = jnp.concatenate(
-        [jnp.zeros((64, 256), F32), sums, lines[...], jnp.zeros((40, 256), F32)], axis=0
-    )
-    last = grads[:, 256:384] + jnp.transpose(stacked)
-    send[:, 0:8, :] = grads[:, 0:128].astype(BF16).reshape(SLICES, 8, 128)
-    send[:, 8:16, :] = grads[:, 128:256].astype(BF16).reshape(SLICES, 8, 128)
-    send[:, 16:24, :] = last.astype(BF16).reshape(SLICES, 8, 128)
-
-
-def embedded_kernel(got, gn, gain, table, scale, oht, out, counts):
+    row = exact(mm_nt, ones, gn.astype(F32) * rated, 3, False)[0:1]
+    row = jnp.concatenate([row, cpart[...]], axis=1)
+    cross[...] = jnp.broadcast_to(row[None], (GROUPS, 1, 384))
+
+
+def embedded_kernel(got, gn, gain, table, scale, oht, out):
     total = got[0]
     for k in range(1, GROUPS):
         total = total + got[k]
-    cross = columns(total)[:, 0:1]
+    cross = columns(jnp.broadcast_to(total[:, 0:256], (8, ROWS)))[:, 0:1]
     own = oht[48:64]
-    unit = scale[...]
+    unit = scale[:, 0:1]
     turned = exact(mm_tn, own, unit * gain[...], 3, False)
     shrunk = exact(mm_tn, own, table[...] * (unit * unit * unit / D), 3, False)
     out[...] = (turned * gn[...].astype(F32) - shrunk * cross).astype(BF16)
-    counts[...] = exact(mm_nt, own, total, 3, False)
-
-
-def gather_kernel(got, send):
+
+
+def gather_kernel(got, cross, send):
     total = got[0].astype(F32)
     for k in range(1, SLICES):
         total = total + got[k].astype(F32)
+    here = cross[0]
+    for k in range(1, GROUPS):
+        here = here + cross[k]
+    here = here[:, 256:384]
+    high = here.astype(BF16).astype(F32)
+    row = iota((24, 128), 0)
+    total = total + jnp.where(row == 16, high, 0.0) + jnp.where(row == 17, here - high, 0.0)
     send[...] = jnp.broadcast_to(total.astype(BF16)[None], (SLICES, 24, 128))
 
 
-def finish_kernel(got, counts, table, scale, gain, gt, gg, gcw, gcb, gwb, gwc, gsw, heads):
+def finish_kernel(got, table, scale, gain, gt, gg, gcw, gcb, gwb, gwc, gswt, gsb, glr, gsg):
     gwb[...] = got[:, 0:8, :].astype(F32).reshape(256, 128)
     gwc[...] = got[:, 8:16, :].astype(F32).reshape(256, 128)
-    last = got[:, 16:24, :].astype(F32).reshape(256, 128)
-    gsw[...] = last[:, 0:64]
-    rows = jnp.transpose(last)
+    rows = jnp.transpose(got[:, 16:24, :].astype(F32).reshape(256, 128))
+    gswt[...] = rows[0:64]
     sums = rows[64:80]
-    crossed = counts[0]
-    for k in range(1, SLICES):
-        crossed = crossed + counts[k]
-    unit = scale[...]
-    shrunk = table[...] * (unit * unit * unit / D) * crossed[:, 0:1]
-    gt[...] = unit * gain[...] * sums - shrunk
+    crossed = jnp.sum(rows[88:104], axis=1, keepdims=True)
+    unit = scale[:, 0:1]
+    gt[...] = unit * gain[...] * sums - table[...] * (unit * unit * unit / D) * crossed
     gg[...] = jnp.sum(table[...] * unit * sums, axis=0, keepdims=True)
     gcw[...] = rows[80:84]
     gcb[...] = rows[84:85]
     lane = iota((8, 256), 1)
     tail = rows[80:88]
-    picked = iota((8, 128), 1)
-    result = jnp.zeros((8, 128), F32)
+    picked = iota((8, 4), 1)
+    result = jnp.zeros((8, 4), F32)
     for h in range(HEADS):
         part = jnp.sum(jnp.where(lane // 64 == h, tail, 0.0), axis=1, keepdims=True)
         result = jnp.where(picked == h, part, result)
-    heads[...] = result
+    gsg[...] = result[5:6]
+    gsb[...] = result[6:7]
+    glr[...] = result[7:8]
 
 
 def swap(value, axis):
     return lax.all_to_all(value, axis, 0, 0, tiled=True)
 
 
-def local(
+def shift(value, pairs):
+    return lax.ppermute(value, "ctx", pairs)
+
+
+def mixer(
     token_ids,
     table,
     norm_gain,
@@ -458,27 +517,24 @@
     size = lax.axis_size("ctx")
     up = [(i, i + 1) for i in range(size - 1)]
     down = [(i + 1, i) for i in range(size - 1)]
-    marked = token_ids + 1
-    before = lax.ppermute(marked[-3:], "ctx", up)
-    after = lax.ppermute(marked[:3], "ctx", down)
-    squares = jnp.sum(table * table, axis=1)
-    spread = jnp.broadcast_to(squares[None, None, :], (GROUPS, 1, 16))
-    spread = jnp.pad(spread, ((0, 0), (0, 0), (0, 112)))
-    square_sums = jnp.sum(swap(spread, "fsdp"), axis=(0, 1))[:16]
-    scale = lax.rsqrt(square_sums / D + 1e-05)[:, None]
-    reach = jnp.concatenate([before, marked, after]) - 1
-    ids = jnp.stack([reach[o : o + ROWS] for o in range(7)] + [jnp.full((ROWS,), -1, jnp.int32)])
+    edge = ((8, 256), F32)
+    square = ((ROWS, 256), F32)
+    half_square = ((ROWS, 256), BF16)
+    (squares,) = call(squares_kernel, (((GROUPS, 1, 128), F32),), table)
+    squares = swap(squares, "fsdp")
+    marked = token_ids[None] + 1
+    ids_prev = shift(marked, up)
+    ids_next = shift(marked, down)
     gain = norm_gain[None]
     wbc = jnp.concatenate([weight_b, weight_c], axis=1)
-    heads_first = jnp.transpose(step_weight).reshape(GROUPS, HEADS, 256)
+    swt = jnp.transpose(step_weight)
+    heads_first = swt.reshape(GROUPS, HEADS, 256)
     swx = jnp.concatenate([heads_first, heads_first], axis=1).reshape(128, 256)
     bias = jnp.tile(step_bias, 2)[:, None]
     rate = jnp.tile(log_rate, 2)[:, None]
     skip = jnp.repeat(skip_gain, 64)[None]
 
-    square = ((ROWS, 256), F32)
-    half_square = ((ROWS, 256), BF16)
-    xf, xr, gf, gr, part, oht = call(
+    xf, xr, gf, gr, part, oht, scale = call(
         tokens_kernel,
         (
             half_square,
@@ -487,17 +543,21 @@
             square,
             ((GROUPS, 24, 512), BF16),
             ((128, 256), BF16),
+            ((16, 128), F32),
         ),
-        ids, table, scale, gain, conv_weight, conv_bias[None], wbc, swx,
-    )
-    bc, raw = call(
-        reduce_kernel, (((GROUPS, 16, 512), BF16), ((8, 256), F32)), swap(part, "fsdp")
-    )
+        marked, ids_prev, ids_next, squares, table, gain, conv_weight, conv_bias[None], wbc, swx,
+    )
+    bc, raw = call(reduce_kernel, (((GROUPS, 16, 512), BF16), ((8, 256), F32)), swap(part, "fsdp"))
     bc = swap(bc, "fsdp").reshape(ROWS, 512)
-    states, cols, rows = call(
-        states_kernel,
-        (((16, 2, 40, 128), BF16), ((ROWS, 128), F32), ((48, ROWS), F32)),
-        bc, raw, bias, rate, xf, xr, out_grad,
+    pair = ((2, ROWS, 256), F32)
+    half_pair = ((2, ROWS, 256), BF16)
+    cols, rows, weight, grown, weighted, turned, packed = call(
+        steps_kernel,
+        (((ROWS, 128), F32), ((48, ROWS), F32), pair, pair, half_pair, half_pair, ((2, 8, 128), F32)),
+        raw, bias, rate, xf, xr, out_grad,
+    )
+    (states,) = call(
+        states_kernel, (((16, 2, 40, 128), BF16),), bc, weighted, turned, packed
     )
     arrived = swap(states.reshape(SLICES, 40, 128), "ctx")
     y0, dxf0, dxr0, dbc0, side, line = call(
@@ -515,36 +575,33 @@
             square,
             ((GROUPS, 16, 512), BF16),
             ((8, 256), BF16),
-            ((8, 256), F32),
+            edge,
         ),
-        entering, bc, cols, rows, xf, xr, out_grad, y0, dxf0, dxr0, dbc0, side, line, rate,
+        entering, bc, weight, grown, weighted, turned, rows, xf, xr, out_grad,
+        y0, dxf0, dxr0, dbc0, side, line, rate,
+        final=(0,),
     )
     (totals,) = call(total_kernel, (((GROUPS, 24, 512), BF16),), swap(dpart, "fsdp"), draw)
-    edge = ((8, 256), F32)
-    dpf, dpr, to_prev, to_next, grads, lines = call(
+    dpf, dpr, to_prev, to_next, gsend, cpart = call(
         project_back_kernel,
-        (square, square, edge, edge, ((256, 384), F32), edge),
-        swap(totals, "fsdp"), xf, xr, gf, gr, dxf, dxr, wbc, step_weight, oht, table, scale, gain, small,
-    )
-    from_next = lax.ppermute(to_prev, "ctx", down)
-    from_prev = lax.ppermute(to_next, "ctx", up)
-    gn, cross, gsend = pl.pallas_call(
+        (square, square, edge, edge, ((SLICES, 24, 128), BF16), ((1, 128), F32)),
+        swap(totals, "fsdp"), xf, xr, gf, gr, dxf, dxr, wbc, swt, oht, table, scale, gain,
+        conv_weight, small,
+    )
+    from_next = shift(to_prev, down)
+    from_prev = shift(to_next, up)
+    reduced = swap(gsend, "ctx")
+    gn, cross = call(
         normed_kernel,
-        out_shape=(
-            jax.ShapeDtypeStruct((ROWS, 256), BF16),
-            jax.ShapeDtypeStruct((GROUPS, 8, ROWS), F32),
-            jax.ShapeDtypeStruct((SLICES, 24, 128), BF16),
-        ),
-        scratch_shapes=[VMEM((ROWS + 8, 256), F32), VMEM((ROWS + 8, 256), F32)],
-        name="normed_kernel",
-    )(dpf, dpr, from_next, from_prev, conv_weight, gain, table, oht, grads, lines)
-    grad_embedded, counts = call(
-        embedded_kernel,
-        (half_square, ((16, 8), F32)),
-        swap(cross, "fsdp"), gn, gain, table, scale, oht,
-    )
-    (gathered,) = call(gather_kernel, (((SLICES, 24, 128), BF16),), swap(gsend, "ctx"))
-    counts = jnp.broadcast_to(counts[None], (SLICES, 16, 8))
+        (half_square, ((GROUPS, 1, 384), F32)),
+        dpf, dpr, from_next, from_prev, conv_weight, gain, table, oht, cpart,
+        scratch=[VMEM((ROWS + 8, 256), F32), VMEM((ROWS + 8, 256), F32)],
+    )
+    crossed = swap(cross, "fsdp")
+    (gathered,) = call(gather_kernel, (((SLICES, 24, 128), BF16),), reduced, crossed)
+    (grad_embedded,) = call(
+        embedded_kernel, (half_square,), crossed, gn, gain, table, scale, oht, final=(0,)
+    )
     outs = call(
         finish_kernel,
         (
@@ -554,12 +611,15 @@
             ((1, 256), F32),
             ((256, 128), F32),
             ((256, 128), F32),
-            ((256, 64), F32),
-            ((8, 128), F32),
+            ((64, 256), F32),
+            ((1, 4), F32),
+            ((1, 4), F32),
+            ((1, 4), F32),
         ),
-        swap(gathered, "ctx"), swap(counts, "ctx"), table, scale, gain,
-    )
-    gt, gg, gcw, gcb, gwb, gwc, gsw, heads = outs
+        swap(gathered, "ctx"), table, scale, gain,
+        final=range(10),
+    )
+    gt, gg, gcw, gcb, gwb, gwc, gswt, gsb, glr, gsg = outs
     return (
         mixer_out,
         grad_embedded,
@@ -569,16 +629,16 @@
         gcb[0],
         gwb,
         gwc,
-        gsw,
-        heads[6, :HEADS],
-        heads[7, :HEADS],
-        heads[5, :HEADS],
+        jnp.transpose(gswt),
+        gsb[0],
+        glr[0],
+        gsg[0],
     )
 
 
 def solution(mesh):
     return jax.shard_map(
-        local,
+        mixer,
         mesh=mesh,
         in_specs=(
             P("ctx"),

time: 262 us -> 222 us (0.85)
  blocking collectives: 78.5 us -> 115 us
  waiting for transfers between devices: 74.3 us -> 39 us
  starting transfers between devices: 57.3 us -> 37.5 us
  Pallas kernels: 30.8 us -> 13.4 us
    all_to_all x4 -> x6, blocking collectives: 78.5 us -> 115 us  [swap(): return lax.all_to_all(value, axis, 0, 0, tiled=True)]
    all_to_all x7 -> x4, waiting for transfers between devices: 72.5 us -> 37.7 us  [swap(): return lax.all_to_all(value, axis, 0, 0, tiled=True)]
    all_to_all x7 -> x4, starting transfers between devices: 41.7 us -> 21 us  [swap(): return lax.all_to_all(value, axis, 0, 0, tiled=True)]
    pallas_call x12 -> x14, Pallas kernels: 30.8 us -> 13.4 us  [call(): pl.pallas_call(kernel, out_shape=shapes, scratch_shapes=scratch, compiler...]
    unnamed x32 -> x59, local copies, waits for them, and re-layouts: 7.71 us -> 14.1 us
  transfers between devices with their start and end apart: 11 -> 8, of which waited for: 8 -> 5; matrix products, arithmetic and copies ran while one was open for 4% -> 0% of each run, Pallas kernels for 3% -> 2%
where the time goes in v2:
time: 222 us; the launch traced here: 221 us
  blocking collectives  115 us (52%)
  waiting for transfers between devices  39 us (18%)
  starting transfers between devices  37.5 us (17%)
  local copies, waits for them, and re-layouts  15 us (7%)
  Pallas kernels  13.4 us (6%)
    all_to_all x6, blocking collectives, swap(): return lax.all_to_all(value, axis, 0, 0, tiled=True)  115 us
    all_to_all x4, waiting for transfers between devices, swap(): return lax.all_to_all(value, axis, 0, 0, tiled=True)  37.7 us
    all_to_all x4, starting transfers between devices, swap(): return lax.all_to_all(value, axis, 0, 0, tiled=True)  21 us
    ppermute x4, starting transfers between devices, shift(): return lax.ppermute(value, 'ctx', pairs)  16.5 us
    unnamed x59, local copies, waits for them, and re-layouts  14.1 us
    pallas_call x14, Pallas kernels, call(): pl.pallas_call(kernel, out_shape=shapes, scratch_shapes=scratch, compiler...  13.4 us
  transfers between devices with their start and end apart: 8, of which 5 were waited for; matrix products, arithmetic and copies ran while one was open for 0% of the time, Pallas kernels for 2%

profile of v2, /device:TPU:6, one launch (start us, length us, event | category | flops | bytes accessed | tf_op | source)
XLA Modules:
  0.0 221.3 jit_solution(2897260399150803067)
XLA Ops:
  0.6 0.7 broadcast_add_fusion
  1.3 3.3 %collective-permute-start.1 = (s32[1,256]{1,0:T(1,128)S(1)}, s32[1,256]{1,0:T(1,128)S(1)}, u32[]{:S(2)}, u32[]{:S(2)}) collective-permute-start(s32[1,256]{1,0:T(1,128)S(1)} %bitcast.27), channel_id=1, source_target_pairs={{1,0},{2,1},{3,2},{4,3},{5,4},{6,5},{7,6},{8,7},{9,8},{10,9},{11,1... | collective-permute-start | bytes 3080 | tf_op jit(solution)/shard_map/ppermute | solution.py:500
  4.6 4.9 %collective-permute-start = (s32[1,256]{1,0:T(1,128)S(1)}, s32[1,256]{1,0:T(1,128)S(1)}, u32[]{:S(2)}, u32[]{:S(2)}) collective-permute-start(s32[1,256]{1,0:T(1,128)S(1)} %bitcast.28), channel_id=1, source_target_pairs={{0,1},{1,2},{2,3},{3,4},{4,5},{5,6},{6,7},{7,8},{8,9},{9,10},{10,1... | collective-permute-start | bytes 3080 | tf_op jit(solution)/shard_map/ppermute | solution.py:500
  9.6 0.7 copy-done.1
  10.3 0.8 shard_map.211
  11.1 5.9 %all-to-all-start = ((f32[16,1,128]{2,1,0:T(1,128)}), f32[16,1,128]{2,1,0:T(1,128)S(1)}, u32[]{:S(2)}, u32[]{:S(2)}) async-start(f32[16,1,128]{2,1,0:T(1,128)} %shard_map.211), calls=%async_computation | async-start | bytes 16384 | tf_op jit(solution)/shard_map/all_to_all | solution.py:496
  17.1 0.8 copy-done.24
  17.9 0.8 copy-done.25
  18.7 2.9 %all-to-all-done.got = f32[16,1,128]{2,1,0:T(1,128)S(1)} async-done(((f32[16,1,128]{2,1,0:T(1,128)}), f32[16,1,128]{2,1,0:T(1,128)S(1)}, u32[]{:S(2)}, u32[]{:S(2)}) %all-to-all-start) | async-done | bytes 8224 | tf_op jit(solution)/shard_map/all_to_all | solution.py:496
  21.7 0.7 copy-done.16
  22.3 0.8 shard_map.212
  23.2 0.7 copy-done.3
  23.9 12.2 %all_to_all.50.got = bf16[16,24,512]{2,1,0:T(8,128)(2,1)S(1)} all-to-all(bf16[16,24,512]{2,1,0:T(8,128)(2,1)S(1)} %get-tuple-element.58), channel_id=1, replica_groups=mesh['fsdp'=16,'ctx'=32] {'fsdp'}, dimensions={0} | all-to-all | bytes 786432 | tf_op jit(solution)/shard_map/all_to_all | solution.py:496
  36.1 0.8 shard_map.213
  36.9 4.7 %all-to-all-start.2 = ((bf16[16,16,512]{2,1,0:T(8,128)(2,1)}), bf16[16,16,512]{2,1,0:T(8,128)(2,1)S(1)}, u32[]{:S(2)}, u32[]{:S(2)}) async-start(bf16[16,16,512]{2,1,0:T(8,128)(2,1)} %get-tuple-element.59), calls=%async_computation.2 | async-start | bytes 524288 | tf_op jit(solution)/shard_map/all_to_all | solution.py:496
  42.4 1.2 shard_map.214
  43.5 0.6 copy-done.13
  44.2 4.2 %all-to-all-done.2 = bf16[16,16,512]{2,1,0:T(8,128)(2,1)S(1)} async-done(((bf16[16,16,512]{2,1,0:T(8,128)(2,1)}), bf16[16,16,512]{2,1,0:T(8,128)(2,1)S(1)}, u32[]{:S(2)}, u32[]{:S(2)}) %all-to-all-start.2) | async-done | bytes 262176 | tf_op jit(solution)/shard_map/all_to_all | solution.py:496
  48.6 42.6 %all_to_all.51.got = bf16[32,40,128]{2,1,0:T(8,128)(2,1)S(1)} all-to-all(bf16[32,40,128]{2,1,0:T(8,128)(2,1)S(1)} %bitcast.18), channel_id=1, replica_groups=mesh['fsdp'=16,'ctx'=32] {'ctx'}, dimensions={0} | all-to-all | bytes 655360 | tf_op jit(solution)/shard_map/all_to_all | solution.py:496
  91.3 0.8 shard_map.216
  92.1 5.3 %all-to-all-start.4 = ((bf16[32,32,128]{2,1,0:T(8,128)(2,1)}), bf16[32,32,128]{2,1,0:T(8,128)(2,1)S(1)}, u32[]{:S(2)}, u32[]{:S(2)}) async-start(bf16[32,32,128]{2,1,0:T(8,128)(2,1)} %shard_map.216), calls=%async_computation.4 | async-start | bytes 524288 | tf_op jit(solution)/shard_map/all_to_all | solution.py:496
  98.1 0.7 copy-done.22
  98.7 0.9 copy-done.14
  99.6 2.3 %shard_map.217 = (f32[256,256]{1,0:T(8,128)S(1)}, f32[256,256]{1,0:T(8,128)S(1)}, f32[256,256]{1,0:T(8,128)S(1)}, f32[256,512]{1,0:T(8,128)S(1)}, f32[8,256]{1,0:T(8,128)S(1)}, /*index=5*/f32[8,256]{1,0:T(8,128)S(1)}) custom-call(bf16[256,512]{1,0:T(8,128)(2,1)S(1)} %bitcast.16, f32[256,128]{1,0:T(8,128)S(1)} %copy-done.14, ...), custom_call_target="tpu_custom_call" | custom-call | tf_op jit(solution)/shard_map/pallas_call | solution.py:25
  101.9 0.7 copy-done.5
  102.7 0.7 copy-done.7
  103.4 0.7 copy-done.9
  105.3 13.3 %all-to-all-done.4 = bf16[32,32,128]{2,1,0:T(8,128)(2,1)S(1)} async-done(((bf16[32,32,128]{2,1,0:T(8,128)(2,1)}), bf16[32,32,128]{2,1,0:T(8,128)(2,1)S(1)}, u32[]{:S(2)}, u32[]{:S(2)}) %all-to-all-start.4) | async-done | bytes 262176 | tf_op jit(solution)/shard_map/all_to_all | solution.py:496
  118.6 0.7 copy-done.21
  119.3 0.9 copy-done.6
  120.2 0.9 copy-done.8
  121.2 0.9 copy-done.10
  122.1 1.9 shard_map.218
  124.0 10.6 %all_to_all.52.got = bf16[16,16,512]{2,1,0:T(8,128)(2,1)S(1)} all-to-all(bf16[16,16,512]{2,1,0:T(8,128)(2,1)S(1)} %get-tuple-element.77), channel_id=1, replica_groups=mesh['fsdp'=16,'ctx'=32] {'fsdp'}, dimensions={0} | all-to-all | bytes 524288 | tf_op jit(solution)/shard_map/all_to_all | solution.py:496
  134.7 12.3 %all_to_all.53.got = bf16[16,24,512]{2,1,0:T(8,128)(2,1)S(1)} all-to-all(bf16[16,24,512]{2,1,0:T(8,128)(2,1)S(1)} %shard_map.219), channel_id=1, replica_groups=mesh['fsdp'=16,'ctx'=32] {'fsdp'}, dimensions={0} | all-to-all | bytes 786432 | tf_op jit(solution)/shard_map/all_to_all | solution.py:496
  147.0 0.7 copy-done.17
  147.7 1.2 shard_map.220
  148.9 2.5 %collective-permute-start.2 = (f32[8,256]{1,0:T(8,128)S(1)}, f32[8,256]{1,0:T(8,128)S(1)}, u32[]{:S(2)}, u32[]{:S(2)}) collective-permute-start(f32[8,256]{1,0:T(8,128)S(1)} %get-tuple-element.88), channel_id=1, source_target_pairs={{1,0},{2,1},{3,2},{4,3},{5,4},{6,5},{7,6},{8,7},{9,8},{10,9},{11,1... | collective-permute-start | bytes 24584 | tf_op jit(solution)/shard_map/ppermute | solution.py:500
  151.4 5.7 %collective-permute-start.3 = (f32[8,256]{1,0:T(8,128)S(1)}, f32[8,256]{1,0:T(8,128)S(1)}, u32[]{:S(2)}, u32[]{:S(2)}) collective-permute-start(f32[8,256]{1,0:T(8,128)S(1)} %get-tuple-element.89), channel_id=1, source_target_pairs={{0,1},{1,2},{2,3},{3,4},{4,5},{5,6},{6,7},{7,8},{8,9},{9,10},{10,1... | collective-permute-start | bytes 24584 | tf_op jit(solution)/shard_map/ppermute | solution.py:500
  157.2 1.3 collective-permute-done.3.from_prev
  158.5 0.7 shard_map.221
  159.3 8.5 %all_to_all.54.got.cross = f32[16,1,384]{2,1,0:T(1,128)S(1)} all-to-all(f32[16,1,384]{2,1,0:T(1,128)S(1)} %get-tuple-element.91), channel_id=1, replica_groups=mesh['fsdp'=16,'ctx'=32] {'fsdp'}, dimensions={0} | all-to-all | bytes 49152 | tf_op jit(solution)/shard_map/all_to_all | solution.py:496
  167.8 28.4 %all_to_all.55.got = bf16[32,24,128]{2,1,0:T(8,128)(2,1)S(1)} all-to-all(bf16[32,24,128]{2,1,0:T(8,128)(2,1)S(1)} %get-tuple-element.93), channel_id=1, replica_groups=mesh['fsdp'=16,'ctx'=32] {'ctx'}, dimensions={0} | all-to-all | bytes 393216 | tf_op jit(solution)/shard_map/all_to_all | solution.py:496
  196.2 0.7 shard_map.223
  196.9 5.1 %all-to-all-start.9 = ((bf16[32,24,128]{2,1,0:T(8,128)(2,1)}), bf16[32,24,128]{2,1,0:T(8,128)(2,1)S(1)}, u32[]{:S(2)}, u32[]{:S(2)}) async-start(bf16[32,24,128]{2,1,0:T(8,128)(2,1)} %shard_map.223), calls=%async_computation.9 | async-start | bytes 393216 | tf_op jit(solution)/shard_map/all_to_all | solution.py:496
  202.0 1.1 shard_map.222
  203.1 17.3 %all-to-all-done.9.got = bf16[32,24,128]{2,1,0:T(8,128)(2,1)S(1)} async-done(((bf16[32,24,128]{2,1,0:T(8,128)(2,1)}), bf16[32,24,128]{2,1,0:T(8,128)(2,1)S(1)}, u32[]{:S(2)}, u32[]{:S(2)}) %all-to-all-start.9) | async-done | bytes 196640 | tf_op jit(solution)/shard_map/all_to_all | solution.py:496
  220.4 0.8 shard_map.224
  (57 shorter events, 3.1 us)
Async XLA Ops:
  1.3 17.4 %collective-permute-start.1 = (s32[1,256]{1,0:T(1,128)S(1)}, s32[1,256]{1,0:T(1,128)S(1)}, u32[]{:S(2)}, u32[]{:S(2)}) collective-permute-start(s32[1,256]{1,0:T(1,128)S(1)} %bitcast.27), channel_id=1, source_target_pairs={{1,0},{2,1},{3,2},{4,3},{5,4},{6,5},{7,6},{8,7},{9,8},{10,9},{11,1... | collective-permute-start | bytes 3080 | tf_op jit(solution)/shard_map/ppermute | solution.py:500
  4.6 14.1 %collective-permute-start = (s32[1,256]{1,0:T(1,128)S(1)}, s32[1,256]{1,0:T(1,128)S(1)}, u32[]{:S(2)}, u32[]{:S(2)}) collective-permute-start(s32[1,256]{1,0:T(1,128)S(1)} %bitcast.28), channel_id=1, source_target_pairs={{0,1},{1,2},{2,3},{3,4},{4,5},{5,6},{6,7},{7,8},{8,9},{9,10},{10,1... | collective-permute-start | bytes 3080 | tf_op jit(solution)/shard_map/ppermute | solution.py:500
  9.6 0.7 copy-start.1
  10.3 6.7 %copy-start.11 = (bf16[256,64]{0,1:T(8,128)(2,1)S(1)}, bf16[256,64]{0,1:T(8,128)(2,1)}, u32[]{:S(2)}) copy-start(bf16[256,64]{0,1:T(8,128)(2,1)} %param.19) | copy-start | bytes 98308
  11.1 10.6 %all-to-all-start = ((f32[16,1,128]{2,1,0:T(1,128)}), f32[16,1,128]{2,1,0:T(1,128)S(1)}, u32[]{:S(2)}, u32[]{:S(2)}) async-start(f32[16,1,128]{2,1,0:T(1,128)} %shard_map.211), calls=%async_computation | async-start | bytes 16384 | tf_op jit(solution)/shard_map/all_to_all | solution.py:496
  17.0 0.8 copy-start.24
  17.9 0.8 copy-start.25
  18.7 3.0 %copy-start.2 = (f32[16,256]{1,0:T(8,128)S(1)}, f32[16,256]{1,0:T(8,128)}, u32[]{:S(2)}) copy-start(f32[16,256]{1,0:T(8,128)} %table.11) | copy-start | bytes 49156
  18.7 3.0 %copy-start.15 = (f32[4,256]{1,0:T(4,128)S(1)}, f32[4,256]{1,0:T(4,128)}, u32[]{:S(2)}) copy-start(f32[4,256]{1,0:T(4,128)} %cw.5) | copy-start | bytes 12292
  18.7 3.0 %copy-start.23 = (f32[256]{0:T(256)S(1)}, f32[256]{0:T(256)}, u32[]{:S(2)}) copy-start(f32[256]{0:T(256)} %param.16) | copy-start | bytes 3076
  21.7 0.7 copy-start.16
  23.2 0.7 copy-start.3
  36.9 4.7 %copy-start.27 = (f32[4]{0:T(128)S(1)}, f32[4]{0:T(128)}, u32[]{:S(2)}) copy-start(f32[4]{0:T(128)} %param.21) | copy-start | bytes 52
  36.9 5.5 %copy-start = (bf16[256,256]{1,0:T(8,128)(2,1)S(1)}, bf16[256,256]{1,0:T(8,128)(2,1)}, u32[]{:S(2)}) copy-start(bf16[256,256]{1,0:T(8,128)(2,1)} %dy.5) | copy-start | bytes 393220
  36.9 11.5 %all-to-all-start.2 = ((bf16[16,16,512]{2,1,0:T(8,128)(2,1)}), bf16[16,16,512]{2,1,0:T(8,128)(2,1)S(1)}, u32[]{:S(2)}, u32[]{:S(2)}) async-start(bf16[16,16,512]{2,1,0:T(8,128)(2,1)} %get-tuple-element.59), calls=%async_computation.2 | async-start | bytes 524288 | tf_op jit(solution)/shard_map/all_to_all | solution.py:496
  41.6 0.7 copy-start.28
  43.5 0.7 copy-start.13
  92.1 5.3 %copy-start.26 = (f32[4]{0:T(128)S(1)}, f32[4]{0:T(128)}, u32[]{:S(2)}) copy-start(f32[4]{0:T(128)} %param.22) | copy-start | bytes 52
  92.1 26.5 %all-to-all-start.4 = ((bf16[32,32,128]{2,1,0:T(8,128)(2,1)}), bf16[32,32,128]{2,1,0:T(8,128)(2,1)S(1)}, u32[]{:S(2)}, u32[]{:S(2)}) async-start(bf16[32,32,128]{2,1,0:T(8,128)(2,1)} %shard_map.216), calls=%async_computation.4 | async-start | bytes 524288 | tf_op jit(solution)/shard_map/all_to_all | solution.py:496
  98.1 0.7 copy-start.22
  98.7 0.9 copy-start.14
  101.9 0.7 copy-start.5
  102.7 0.7 copy-start.7
  103.4 0.7 copy-start.9
  104.1 0.6 copy-start.18
  104.7 0.6 copy-start.20
  118.6 0.7 copy-start.21
  118.6 0.7 copy-start.19
  119.3 0.9 copy-start.6
  120.2 0.9 copy-start.8
  121.2 0.9 copy-start.10
  134.7 12.3 %copy-start.4 = (f32[256,256]{1,0:T(8,128)S(1)}, f32[256,256]{1,0:T(8,128)}, u32[]{:S(2)}) copy-start(f32[256,256]{1,0:T(8,128)} %copy-done.3) | copy-start | bytes 786436
  134.7 12.3 %copy-start.12 = (bf16[256,64]{0,1:T(8,128)(2,1)S(1)}, bf16[256,64]{0,1:T(8,128)(2,1)}, u32[]{:S(2)}) copy-start(bf16[256,64]{0,1:T(8,128)(2,1)} %param.19) | copy-start | bytes 98308
  147.0 0.7 copy-start.17
  148.9 8.3 %collective-permute-start.2 = (f32[8,256]{1,0:T(8,128)S(1)}, f32[8,256]{1,0:T(8,128)S(1)}, u32[]{:S(2)}, u32[]{:S(2)}) collective-permute-start(f32[8,256]{1,0:T(8,128)S(1)} %get-tuple-element.88), channel_id=1, source_target_pairs={{1,0},{2,1},{3,2},{4,3},{5,4},{6,5},{7,6},{8,7},{9,8},{10,9},{11,1... | collective-permute-start | bytes 24584 | tf_op jit(solution)/shard_map/ppermute | solution.py:500
  151.4 7.1 %collective-permute-start.3 = (f32[8,256]{1,0:T(8,128)S(1)}, f32[8,256]{1,0:T(8,128)S(1)}, u32[]{:S(2)}, u32[]{:S(2)}) collective-permute-start(f32[8,256]{1,0:T(8,128)S(1)} %get-tuple-element.89), channel_id=1, source_target_pairs={{0,1},{1,2},{2,3},{3,4},{4,5},{5,6},{6,7},{7,8},{8,9},{9,10},{10,1... | collective-permute-start | bytes 24584 | tf_op jit(solution)/shard_map/ppermute | solution.py:500
  196.9 23.5 %all-to-all-start.9 = ((bf16[32,24,128]{2,1,0:T(8,128)(2,1)}), bf16[32,24,128]{2,1,0:T(8,128)(2,1)S(1)}, u32[]{:S(2)}, u32[]{:S(2)}) async-start(bf16[32,24,128]{2,1,0:T(8,128)(2,1)} %shard_map.223), calls=%async_computation.9 | async-start | bytes 393216 | tf_op jit(solution)/shard_map/all_to_all | solution.py:496

commit v3 on v2

--- a/solution.py
+++ b/solution.py
@@ -10,7 +10,10 @@
 HEADS = 4
 STATE = 128
 GROUPS = 16
-SLICES = 32
+NEAR = 8
+FAR = 4
+CTX = ("zh", "zl", "xh")
+BESIDE = ("zl", "xh")
 F32 = jnp.float32
 BF16 = jnp.bfloat16
 VMEM = pltpu.VMEM
@@ -99,7 +102,7 @@
 
 
 def tokens_kernel(
-    ids, ids_prev, ids_next, got, table, gain, cw, cb, wbc, swx,
+    ids, ids_prev, ids_next, got, table, gain, cw, cb, wb, wc, swt,
     xf, xr, gf, gr, send, oht_ref, scale,
 ):
     total = got[0]
@@ -140,10 +143,15 @@
         x_ref[...] = half
         halves.append(half)
     for member, half in enumerate(halves):
-        part = mm(half, wbc[...]).astype(BF16).reshape(GROUPS, 16, 256)
-        send[:, 0:16, member * 256 : member * 256 + 256] = part
+        for side, weight in ((0, wb), (128, wc)):
+            at = member * 256 + side
+            part = mm(half, weight[...]).astype(BF16).reshape(GROUPS, 16, 128)
+            send[:, 0:16, at : at + 128] = part
     own = iota((128, 256), 0) % 8 < 4
-    steps = jnp.where(own, mm_nt(swx[...], halves[0]), mm_nt(swx[...], halves[1]))
+    place = iota((128, 64), 0)
+    chosen = jnp.where(place // 8 * 4 + place % 4 == iota((128, 64), 1), 1.0, 0.0).astype(BF16)
+    swx = mm(chosen, swt[...]).astype(BF16)
+    steps = jnp.where(own, mm_nt(swx, halves[0]), mm_nt(swx, halves[1]))
     high, low = pieces(steps, 2)
     send[:, 16:24, 0:256] = high.reshape(GROUPS, 8, 256)
     send[:, 16:24, 256:512] = low.reshape(GROUPS, 8, 256)
@@ -160,7 +168,7 @@
 
 def steps_kernel(
     raw, bias, rate, xf, xr, dy,
-    cols_ref, rows_ref, weight_ref, grown_ref, weighted_ref, turned_ref, packed_ref,
+    cols_ref, rows_ref, weighted_ref, turned_ref, packed_ref,
 ):
     shifted = raw[...] + bias[...]
     step = jnp.maximum(shifted, 0.0) + jnp.log1p(jnp.exp(-jnp.abs(shifted)))
@@ -184,23 +192,31 @@
     for br, x in ((0, xf), (1, xr)):
         weight_wide = expand(cols, 16 + 4 * br, masks)
         grown_wide = expand(cols, 24 + 4 * br, masks)
-        weight_ref[br] = weight_wide
-        grown_ref[br] = grown_wide
         weighted_ref[br] = (weight_wide * x[...].astype(F32)).astype(BF16)
         turned_ref[br] = (grown_wide * dyf).astype(BF16)
     decay = jnp.exp(ending)
-    left = iota((1, 128), 1) < 64
-    row = iota((8, 128), 0)
-    for hp in range(2):
-        fd = jnp.where(left, decay[2 * hp : 2 * hp + 1], decay[2 * hp + 1 : 2 * hp + 2])
-        rd = jnp.where(left, decay[4 + 2 * hp : 5 + 2 * hp], decay[5 + 2 * hp : 6 + 2 * hp])
-        f_high = fd.astype(BF16).astype(F32)
-        r_high = rd.astype(BF16).astype(F32)
-        packed = jnp.where(row == 0, f_high, 0.0)
-        packed = jnp.where(row == 1, fd - f_high, packed)
-        packed = jnp.where(row == 2, r_high, packed)
-        packed = jnp.where(row == 3, rd - r_high, packed)
-        packed_ref[hp] = packed
+    lane_head = iota((1, 256), 1) // 64
+    fwd_decay = jnp.zeros((1, 256), F32)
+    rev_decay = jnp.zeros((1, 256), F32)
+    for h in range(HEADS):
+        fwd_decay = jnp.where(lane_head == h, decay[h : h + 1], fwd_decay)
+        rev_decay = jnp.where(lane_head == h, decay[h + 4 : h + 5], rev_decay)
+    packed_ref[...] = split_decays(fwd_decay, rev_decay)
+
+
+def split_decays(fwd_decay, rev_decay):
+    row = iota((8, 256), 0)
+    f_high = fwd_decay.astype(BF16).astype(F32)
+    r_high = rev_decay.astype(BF16).astype(F32)
+    packed = jnp.where(row == 0, f_high, 0.0)
+    packed = jnp.where(row == 1, fwd_decay - f_high, packed)
+    packed = jnp.where(row == 2, r_high, packed)
+    return jnp.where(row == 3, rev_decay - r_high, packed)
+
+
+def join_decays(packed):
+    rows = packed.astype(F32)
+    return rows[0:1] + rows[1:2], rows[2:3] + rows[3:4]
 
 
 def states_kernel(bc, weighted, turned, packed, send):
@@ -211,31 +227,55 @@
         found.append((mm_tn(b, weighted[br]), mm_tn(c, turned[br])))
     chains = (found[0][0], found[1][1], found[1][0], found[0][1])
     for ch, state in enumerate(chains):
-        for hp in range(2):
-            part = state[:, hp * 128 : hp * 128 + 128].astype(BF16).reshape(16, 8, 128)
-            send[:, hp, ch * 8 : ch * 8 + 8, :] = part
-    for hp in range(2):
-        send[:, hp, 32:40, :] = jnp.broadcast_to(packed[hp].astype(BF16)[None], (16, 8, 128))
-
-
-def chain_kernel(got, out):
-    decays = got[:, 32:40, :].astype(F32)
-    fwd_decay = decays[:, 0:1, :] + decays[:, 1:2, :]
-    rev_decay = decays[:, 2:3, :] + decays[:, 3:4, :]
-    up_f = jnp.zeros((8, 128), F32)
-    up_r = jnp.zeros((8, 128), F32)
-    down_r = jnp.zeros((8, 128), F32)
-    down_f = jnp.zeros((8, 128), F32)
-    for i in range(SLICES):
-        out[i, 0:16, :] = jnp.concatenate([up_f, up_r], axis=0).astype(BF16)
-        here = got[i, 0:16, :].astype(F32)
-        up_f = fwd_decay[i] * up_f + here[0:8]
-        up_r = rev_decay[i] * up_r + here[8:16]
-        j = SLICES - 1 - i
-        out[j, 16:32, :] = jnp.concatenate([down_r, down_f], axis=0).astype(BF16)
-        there = got[j, 16:32, :].astype(F32)
-        down_r = rev_decay[j] * down_r + there[0:8]
-        down_f = fwd_decay[j] * down_f + there[8:16]
+        send[:, ch * 16 : ch * 16 + 16, :] = state.astype(BF16).reshape(NEAR, 16, 256)
+    send[:, 64:72, :] = jnp.broadcast_to(packed[...].astype(BF16)[None], (NEAR, 8, 256))
+
+
+def advance(state, decay_first, decay_second, piece):
+    return decay_first * state[0] + piece[0:16], decay_second * state[1] + piece[16:32]
+
+
+def group_kernel(got, send):
+    nothing = jnp.zeros((16, 256), F32)
+    up = (nothing, nothing)
+    down = (nothing, nothing)
+    fwd_all = jnp.ones((1, 256), F32)
+    rev_all = jnp.ones((1, 256), F32)
+    for i in range(NEAR):
+        fwd_decay, rev_decay = join_decays(got[i, 64:72, :])
+        fwd_all = fwd_all * fwd_decay
+        rev_all = rev_all * rev_decay
+        up = advance(up, fwd_decay, rev_decay, got[i, 0:32, :].astype(F32))
+        j = NEAR - 1 - i
+        fwd_decay, rev_decay = join_decays(got[j, 64:72, :])
+        down = advance(down, rev_decay, fwd_decay, got[j, 32:64, :].astype(F32))
+    totals = jnp.concatenate([up[0], up[1], down[0], down[1], split_decays(fwd_all, rev_all)], axis=0)
+    send[...] = jnp.broadcast_to(totals.astype(BF16)[None], (FAR, 72, 256))
+
+
+def chain_kernel(got, far, group, out):
+    here = group[...]
+    nothing = jnp.zeros((16, 256), F32)
+    up = (nothing, nothing)
+    down = (nothing, nothing)
+    for g in range(FAR):
+        fwd_decay, rev_decay = join_decays(far[g, 64:72, :])
+        moved = advance(up, fwd_decay, rev_decay, far[g, 0:32, :].astype(F32))
+        up = tuple(jnp.where(here > g, new, old) for new, old in zip(moved, up))
+        k = FAR - 1 - g
+        fwd_decay, rev_decay = join_decays(far[k, 64:72, :])
+        moved = advance(down, rev_decay, fwd_decay, far[k, 32:64, :].astype(F32))
+        down = tuple(jnp.where(here < k, new, old) for new, old in zip(moved, down))
+    for i in range(NEAR):
+        out[i, 0:16, :] = up[0].astype(BF16)
+        out[i, 16:32, :] = up[1].astype(BF16)
+        fwd_decay, rev_decay = join_decays(got[i, 64:72, :])
+        up = advance(up, fwd_decay, rev_decay, got[i, 0:32, :].astype(F32))
+        j = NEAR - 1 - i
+        out[j, 32:48, :] = down[0].astype(BF16)
+        out[j, 48:64, :] = down[1].astype(BF16)
+        fwd_decay, rev_decay = join_decays(got[j, 64:72, :])
+        down = advance(down, rev_decay, fwd_decay, got[j, 32:64, :].astype(F32))
 
 
 def within_kernel(bc, cols_ref, rows_ref, xf, xr, dy, skip, y_ref, dxf, dxr, dbc, side, line):
@@ -286,17 +326,17 @@
 
 
 def carried_kernel(
-    got, bc, weight_ref, grown_ref, weighted, turned, rows_ref, xf, xr, dy,
+    got, bc, cols_ref, weighted, turned, rows_ref, xf, xr, dy,
     y0, dxf0, dxr0, dbc0, side, line, rate,
     out, dxf, dxr, send, draw_ref, small,
 ):
     dyf = dy[...].astype(F32)
 
+    masks = head_masks(ROWS)
+    cols = cols_ref[...]
+
     def state(ch):
-        halves = [
-            got[:, hp, ch * 8 : ch * 8 + 8, :].astype(F32).reshape(STATE, 128) for hp in range(2)
-        ]
-        return jnp.concatenate(halves, axis=1)
+        return got[:, ch * 16 : ch * 16 + 16, :].reshape(STATE, 256)
 
     row_at = iota((8, 256), 0)
     lane_head = iota((8, 256), 1) // 64
@@ -305,19 +345,17 @@
     dw = jnp.zeros((8, ROWS), F32)
     d_end = jnp.zeros((8, 1), F32)
     for br, x, dx0, dx_ref, at_state, at_grad in ((0, xf, dxf0, dxf, 0, 3), (1, xr, dxr0, dxr, 2, 1)):
-        start = state(at_state)
-        ahead = state(at_grad)
-        start_half = start.astype(BF16)
-        ahead_half = ahead.astype(BF16)
+        start_half = state(at_state)
+        ahead_half = state(at_grad)
         b = bc[:, br * 256 : br * 256 + 128]
         c = bc[:, br * 256 + 128 : br * 256 + 256]
         heads = jnp.where(lane_head + 4 * br == row_at, 1.0, 0.0).astype(BF16)
-        carried = grown_ref[br] * mm(c, start_half)
+        carried = expand(cols, 24 + 4 * br, masks) * mm(c, start_half)
         total = total + carried
         dp = dp + exact(mm_nt, heads, dyf * carried, 2, False)
         xv = x[...].astype(F32)
         toward = mm(b, ahead_half)
-        dx_ref[...] = dx0[...] + weight_ref[br] * toward
+        dx_ref[...] = dx0[...] + expand(cols, 16 + 4 * br, masks) * toward
         dw = dw + exact(mm_nt, heads, xv * toward, 2, False)
         dc = mm_nt(turned[br], start_half)
         db = mm_nt(weighted[br], ahead_half)
@@ -326,7 +364,7 @@
         send[:, :, at + 128 : at + 256] = (
             (dbc0[:, at + 128 : at + 256] + dc).astype(BF16).reshape(16, 16, 128)
         )
-        both = jnp.sum(start * ahead, axis=0, keepdims=True)
+        both = jnp.sum(start_half.astype(F32) * ahead_half.astype(F32), axis=0, keepdims=True)
         spread = jnp.where(lane_head + 4 * br == row_at, both, 0.0)
         d_end = d_end + jnp.sum(spread, axis=1, keepdims=True)
     out[...] = total.astype(BF16)
@@ -373,7 +411,7 @@
 
 
 def project_back_kernel(
-    got, xf, xr, gf, gr, dxf, dxr, wbc, swt, oht, table, scale, gain, cw, small,
+    got, xf, xr, gf, gr, dxf, dxr, wb, wc, swt, oht, table, scale, gain, cw, small,
     dpf, dpr, to_prev, to_next, send, cpart,
 ):
     dbc = got[:, 0:16, :].reshape(ROWS, 512)
@@ -391,7 +429,8 @@
         mine = (wanted == pick_col) & ((pick_row % 8 < 4) == (br == 0))
         dstep = mm_tn(draw, jnp.where(mine, 1.0, 0.0).astype(BF16)).astype(BF16)
         half = dbc[:, br * 256 : br * 256 + 256]
-        into = mm_nt(half, wbc[...]) + mm(dstep, swt[...])
+        into = mm_nt(half[:, 0:128], wb[...]) + mm_nt(half[:, 128:256], wc[...])
+        into = into + mm(dstep, swt[...])
         whole = (dx[...] + into).astype(BF16).astype(F32)
         dpre = whole * slope[...]
         out[...] = dpre
@@ -417,9 +456,9 @@
         axis=0,
     )
     last = jnp.concatenate([thin, jnp.zeros((256, 64), F32)], axis=1) + jnp.transpose(stacked)
-    send[:, 0:8, :] = wide[:, 0:128].astype(BF16).reshape(SLICES, 8, 128)
-    send[:, 8:16, :] = wide[:, 128:256].astype(BF16).reshape(SLICES, 8, 128)
-    send[:, 16:24, :] = last.astype(BF16).reshape(SLICES, 8, 128)
+    send[:, 0:32, :] = wide[:, 0:128].astype(BF16).reshape(NEAR, 32, 128)
+    send[:, 32:64, :] = wide[:, 128:256].astype(BF16).reshape(NEAR, 32, 128)
+    send[:, 64:96, :] = last.astype(BF16).reshape(NEAR, 32, 128)
 
 
 def normed_kernel(
@@ -454,24 +493,31 @@
     out[...] = (turned * gn[...].astype(F32) - shrunk * cross).astype(BF16)
 
 
-def gather_kernel(got, cross, send):
+def near_kernel(got, cross, send):
     total = got[0].astype(F32)
-    for k in range(1, SLICES):
+    for k in range(1, NEAR):
         total = total + got[k].astype(F32)
     here = cross[0]
     for k in range(1, GROUPS):
         here = here + cross[k]
     here = here[:, 256:384]
     high = here.astype(BF16).astype(F32)
-    row = iota((24, 128), 0)
-    total = total + jnp.where(row == 16, high, 0.0) + jnp.where(row == 17, here - high, 0.0)
-    send[...] = jnp.broadcast_to(total.astype(BF16)[None], (SLICES, 24, 128))
+    row = iota((96, 128), 0)
+    total = total + jnp.where(row == 64, high, 0.0) + jnp.where(row == 65, here - high, 0.0)
+    send[...] = jnp.broadcast_to(total.astype(BF16)[None], (FAR, 96, 128))
+
+
+def far_kernel(got, send):
+    total = got[0].astype(F32)
+    for k in range(1, FAR):
+        total = total + got[k].astype(F32)
+    send[...] = jnp.broadcast_to(total.astype(BF16)[None], (NEAR, 96, 128))
 
 
 def finish_kernel(got, table, scale, gain, gt, gg, gcw, gcb, gwb, gwc, gswt, gsb, glr, gsg):
-    gwb[...] = got[:, 0:8, :].astype(F32).reshape(256, 128)
-    gwc[...] = got[:, 8:16, :].astype(F32).reshape(256, 128)
-    rows = jnp.transpose(got[:, 16:24, :].astype(F32).reshape(256, 128))
+    gwb[...] = got[:, 0:32, :].astype(F32).reshape(256, 128)
+    gwc[...] = got[:, 32:64, :].astype(F32).reshape(256, 128)
+    rows = jnp.transpose(got[:, 64:96, :].astype(F32).reshape(256, 128))
     gswt[...] = rows[0:64]
     sums = rows[64:80]
     crossed = jnp.sum(rows[88:104], axis=1, keepdims=True)
@@ -497,7 +543,7 @@
 
 
 def shift(value, pairs):
-    return lax.ppermute(value, "ctx", pairs)
+    return lax.ppermute(value, CTX, pairs)
 
 
 def mixer(
@@ -514,7 +560,7 @@
     skip_gain,
     out_grad,
 ):
-    size = lax.axis_size("ctx")
+    size = lax.axis_size(CTX)
     up = [(i, i + 1) for i in range(size - 1)]
     down = [(i + 1, i) for i in range(size - 1)]
     edge = ((8, 256), F32)
@@ -526,10 +572,8 @@
     ids_prev = shift(marked, up)
     ids_next = shift(marked, down)
     gain = norm_gain[None]
-    wbc = jnp.concatenate([weight_b, weight_c], axis=1)
+    group = lax.axis_index("zh").reshape(1, 1)
     swt = jnp.transpose(step_weight)
-    heads_first = swt.reshape(GROUPS, HEADS, 256)
-    swx = jnp.concatenate([heads_first, heads_first], axis=1).reshape(128, 256)
     bias = jnp.tile(step_bias, 2)[:, None]
     rate = jnp.tile(log_rate, 2)[:, None]
     skip = jnp.repeat(skip_gain, 64)[None]
@@ -545,28 +589,30 @@
             ((128, 256), BF16),
             ((16, 128), F32),
         ),
-        marked, ids_prev, ids_next, squares, table, gain, conv_weight, conv_bias[None], wbc, swx,
+        marked, ids_prev, ids_next, squares, table, gain, conv_weight, conv_bias[None],
+        weight_b, weight_c, swt,
     )
     bc, raw = call(reduce_kernel, (((GROUPS, 16, 512), BF16), ((8, 256), F32)), swap(part, "fsdp"))
     bc = swap(bc, "fsdp").reshape(ROWS, 512)
-    pair = ((2, ROWS, 256), F32)
     half_pair = ((2, ROWS, 256), BF16)
-    cols, rows, weight, grown, weighted, turned, packed = call(
+    cols, rows, weighted, turned, packed = call(
         steps_kernel,
-        (((ROWS, 128), F32), ((48, ROWS), F32), pair, pair, half_pair, half_pair, ((2, 8, 128), F32)),
+        (((ROWS, 128), F32), ((48, ROWS), F32), half_pair, half_pair, edge),
         raw, bias, rate, xf, xr, out_grad,
     )
     (states,) = call(
-        states_kernel, (((16, 2, 40, 128), BF16),), bc, weighted, turned, packed
-    )
-    arrived = swap(states.reshape(SLICES, 40, 128), "ctx")
+        states_kernel, (((NEAR, 72, 256), BF16),), bc, weighted, turned, packed
+    )
+    arrived = swap(states, BESIDE)
     y0, dxf0, dxr0, dbc0, side, line = call(
         within_kernel,
         (square, square, square, ((ROWS, 512), F32), ((8, ROWS), F32), ((8, ROWS), F32)),
         bc, cols, rows, xf, xr, out_grad, skip,
     )
-    (entering,) = call(chain_kernel, (((SLICES, 32, 128), BF16),), arrived)
-    entering = swap(entering, "ctx").reshape(16, 2, 32, 128)
+    (groups,) = call(group_kernel, (((FAR, 72, 256), BF16),), arrived)
+    groups = swap(groups, "zh")
+    (entering,) = call(chain_kernel, (((NEAR, 64, 256), BF16),), arrived, groups, group)
+    entering = swap(entering, BESIDE)
     mixer_out, dxf, dxr, dpart, draw, small = call(
         carried_kernel,
         (
@@ -577,20 +623,20 @@
             ((8, 256), BF16),
             edge,
         ),
-        entering, bc, weight, grown, weighted, turned, rows, xf, xr, out_grad,
+        entering, bc, cols, weighted, turned, rows, xf, xr, out_grad,
         y0, dxf0, dxr0, dbc0, side, line, rate,
         final=(0,),
     )
     (totals,) = call(total_kernel, (((GROUPS, 24, 512), BF16),), swap(dpart, "fsdp"), draw)
     dpf, dpr, to_prev, to_next, gsend, cpart = call(
         project_back_kernel,
-        (square, square, edge, edge, ((SLICES, 24, 128), BF16), ((1, 128), F32)),
-        swap(totals, "fsdp"), xf, xr, gf, gr, dxf, dxr, wbc, swt, oht, table, scale, gain,
-        conv_weight, small,
+        (square, square, edge, edge, ((NEAR, 96, 128), BF16), ((1, 128), F32)),
+        swap(totals, "fsdp"), xf, xr, gf, gr, dxf, dxr, weight_b,
+        weight_c, swt, oht, table, scale, gain, conv_weight, small,
     )
     from_next = shift(to_prev, down)
     from_prev = shift(to_next, up)
-    reduced = swap(gsend, "ctx")
+    reduced = swap(gsend, BESIDE)
     gn, cross = call(
         normed_kernel,
         (half_square, ((GROUPS, 1, 384), F32)),
@@ -598,7 +644,9 @@
         scratch=[VMEM((ROWS + 8, 256), F32), VMEM((ROWS + 8, 256), F32)],
     )
     crossed = swap(cross, "fsdp")
-    (gathered,) = call(gather_kernel, (((SLICES, 24, 128), BF16),), reduced, crossed)
+    (summed,) = call(near_kernel, (((FAR, 96, 128), BF16),), reduced, crossed)
+    summed = swap(summed, "zh")
+    (gathered,) = call(far_kernel, (((NEAR, 96, 128), BF16),), summed)
     (grad_embedded,) = call(
         embedded_kernel, (half_square,), crossed, gn, gain, table, scale, oht, final=(0,)
     )
@@ -616,7 +664,7 @@
             ((1, 4), F32),
             ((1, 4), F32),
         ),
-        swap(gathered, "ctx"), table, scale, gain,
+        swap(gathered, BESIDE), table, scale, gain,
         final=range(10),
     )
     gt, gg, gcw, gcb, gwb, gwc, gswt, gsb, glr, gsg = outs
@@ -637,11 +685,13 @@
 
 
 def solution(mesh):
+    devices = mesh.devices.reshape(mesh.shape["fsdp"], FAR, 4, 2)
+    mesh = jax.sharding.Mesh(devices, ("fsdp",) + CTX)
     return jax.shard_map(
         mixer,
         mesh=mesh,
         in_specs=(
-            P("ctx"),
+            P(CTX),
             P(None, "fsdp"),
             P("fsdp"),
             P(None, "fsdp"),
@@ -652,11 +702,11 @@
             P("fsdp"),
             P("fsdp"),
             P("fsdp"),
-            P("ctx", "fsdp"),
+            P(CTX, "fsdp"),
         ),
         out_specs=(
-            P("ctx", "fsdp"),
-            P("ctx", "fsdp"),
+            P(CTX, "fsdp"),
+            P(CTX, "fsdp"),
             P(None, "fsdp"),
             P("fsdp"),
             P(None, "fsdp"),

time: 222 us -> 209 us (0.941); the launches traced: 221 us -> 205 us
  blocking collectives: 115 us -> 92.3 us
  starting transfers between devices: 37.5 us -> 52.5 us
  local copies, waits for them, and re-layouts: 15 us -> 7.68 us
    all_to_all x6 -> x7, blocking collectives: 115 us -> 92.3 us  [swap(): return lax.all_to_all(value, axis, 0, 0, tiled=True)]
    all_to_all x4 -> x5, starting transfers between devices: 21 us -> 35.8 us  [swap(): return lax.all_to_all(value, axis, 0, 0, tiled=True)]
    all_to_all x4 -> x5, waiting for transfers between devices: 37.7 us -> 27.9 us  [swap(): return lax.all_to_all(value, axis, 0, 0, tiled=True)]
    ppermute x4, waiting for transfers between devices: 1.34 us -> 9.26 us  [shift(): return lax.ppermute(value, CTX, pairs)]
    unnamed x59 -> x34, local copies, waits for them, and re-layouts: 14.1 us -> 7.37 us
    pallas_call x14 -> x16, Pallas kernels: 13.4 us -> 14.2 us  [call(): pl.pallas_call(kernel, out_shape=shapes, scratch_shapes=scratch, compiler...]
  transfers between devices with their start and end apart: 8 -> 9, of which waited for: 5 -> 6; matrix products, arithmetic and copies ran while one was open for 0% -> 0% of each run, Pallas kernels for 2% -> 2%
where the time goes in v3:
time: 209 us; the launch traced here: 205 us
  blocking collectives  92.3 us (44%)
  starting transfers between devices  52.5 us (25%)
  waiting for transfers between devices  37.2 us (18%)
  Pallas kernels  14.2 us (7%)
  local copies, waits for them, and re-layouts  7.68 us (4%)
    all_to_all x7, blocking collectives, swap(): return lax.all_to_all(value, axis, 0, 0, tiled=True)  92.3 us
    all_to_all x5, starting transfers between devices, swap(): return lax.all_to_all(value, axis, 0, 0, tiled=True)  35.8 us
    all_to_all x5, waiting for transfers between devices, swap(): return lax.all_to_all(value, axis, 0, 0, tiled=True)  27.9 us
    ppermute x4, starting transfers between devices, shift(): return lax.ppermute(value, CTX, pairs)  16.7 us
    pallas_call x16, Pallas kernels, call(): pl.pallas_call(kernel, out_shape=shapes, scratch_shapes=scratch, compiler...  14.2 us
    ppermute x4, waiting for transfers between devices, shift(): return lax.ppermute(value, CTX, pairs)  9.26 us
    unnamed x34, local copies, waits for them, and re-layouts  7.37 us
  transfers between devices with their start and end apart: 9, of which 6 were waited for; matrix products, arithmetic and copies ran while one was open for 0% of the time, Pallas kernels for 2%

profile of v3, /device:TPU:6, one launch (start us, length us, event | category | flops | bytes accessed | tf_op | source)
XLA Modules:
  0.0 205.4 jit_solution(7140473647504931021)
XLA Ops:
  0.7 0.7 copy-done.1
  1.4 0.8 shard_map.211
  2.1 6.1 %all-to-all-start = ((f32[16,1,128]{2,1,0:T(1,128)}), f32[16,1,128]{2,1,0:T(1,128)S(1)}, u32[]{:S(2)}, u32[]{:S(2)}) async-start(f32[16,1,128]{2,1,0:T(1,128)} %shard_map.211), calls=%async_computation | async-start | bytes 16384 | tf_op jit(solution)/shard_map/all_to_all | solution.py:542
  8.2 0.7 broadcast_add_fusion
  8.9 6.5 %collective-permute-start.1 = (s32[1,256]{1,0:T(1,128)S(1)}, s32[1,256]{1,0:T(1,128)S(1)}, u32[]{:S(2)}, u32[]{:S(2)}) collective-permute-start(s32[1,256]{1,0:T(1,128)S(1)} %bitcast.22), channel_id=1, source_target_pairs={{1,0},{2,1},{3,2},{4,3},{5,4},{6,5},{7,6},{8,7},{9,8},{10,9},{11,1... | collective-permute-start | bytes 3080 | tf_op jit(solution)/shard_map/ppermute | solution.py:546
  15.4 1.9 collective-permute-start
  17.3 5.0 %collective-permute-done.ids_prev = s32[1,256]{1,0:T(1,128)S(1)} collective-permute-done((s32[1,256]{1,0:T(1,128)S(1)}, s32[1,256]{1,0:T(1,128)S(1)}, u32[]{:S(2)}, u32[]{:S(2)}) %collective-permute-start) | collective-permute-done | bytes 1056 | tf_op jit(solution)/shard_map/ppermute | solution.py:546
  22.4 0.7 copy-done.12
  23.1 0.8 copy-done.5
  23.9 0.8 copy-done.7
  24.7 0.7 copy-done.10
  25.4 0.7 copy-done.13
  26.1 0.9 shard_map.212
  27.0 13.9 %all_to_all.60.got = bf16[16,24,512]{2,1,0:T(8,128)(2,1)S(1)} all-to-all(bf16[16,24,512]{2,1,0:T(8,128)(2,1)S(1)} %get-tuple-element.56), channel_id=1, replica_groups=mesh['fsdp'=16,'zh'=4,'zl'=4,'xh'=2] {'fsdp'}, dimensions={0} | all-to-all | bytes 786432 | tf_op jit(solution)/shard_map/all_to_all | solution.py:542
  40.9 0.8 shard_map.213
  41.7 4.7 %all-to-all-start.2 = ((bf16[16,16,512]{2,1,0:T(8,128)(2,1)}), bf16[16,16,512]{2,1,0:T(8,128)(2,1)S(1)}, u32[]{:S(2)}, u32[]{:S(2)}) async-start(bf16[16,16,512]{2,1,0:T(8,128)(2,1)} %get-tuple-element.57), calls=%async_computation.2 | async-start | bytes 524288 | tf_op jit(solution)/shard_map/all_to_all | solution.py:542
  46.5 0.6 copy-done.16
  47.1 1.2 shard_map.214
  48.3 4.8 %all-to-all-done.2 = bf16[16,16,512]{2,1,0:T(8,128)(2,1)S(1)} async-done(((bf16[16,16,512]{2,1,0:T(8,128)(2,1)}), bf16[16,16,512]{2,1,0:T(8,128)(2,1)S(1)}, u32[]{:S(2)}, u32[]{:S(2)}) %all-to-all-start.2) | async-done | bytes 262176 | tf_op jit(solution)/shard_map/all_to_all | solution.py:542
  53.1 0.3 shard_map.215
  53.4 15.2 %all_to_all.61.got = bf16[8,72,256]{2,1,0:T(8,128)(2,1)S(1)} all-to-all(bf16[8,72,256]{2,1,0:T(8,128)(2,1)S(1)} %shard_map.215), channel_id=1, replica_groups=mesh['fsdp'=16,'zh'=4,'zl'=4,'xh'=2] {'zl','xh'}, dimensions={0} | all-to-all | bytes 589824 | tf_op jit(solution)/shard_map/all_to_all | solution.py:542
  68.5 0.7 shard_map.216
  69.3 12.4 %all-to-all-start.4 = ((bf16[4,72,256]{2,1,0:T(8,128)(2,1)}), bf16[4,72,256]{2,1,0:T(8,128)(2,1)S(1)}, u32[]{:S(2)}, u32[]{:S(2)}) async-start(bf16[4,72,256]{2,1,0:T(8,128)(2,1)} %shard_map.216), calls=%async_computation.4 | async-start | bytes 294912 | tf_op jit(solution)/shard_map/all_to_all | solution.py:542
  81.7 15.3 %all-to-all-done.4.far = bf16[4,72,256]{2,1,0:T(8,128)(2,1)S(1)} async-done(((bf16[4,72,256]{2,1,0:T(8,128)(2,1)}), bf16[4,72,256]{2,1,0:T(8,128)(2,1)S(1)}, u32[]{:S(2)}, u32[]{:S(2)}) %all-to-all-start.4) | async-done | bytes 147488 | tf_op jit(solution)/shard_map/all_to_all | solution.py:542
  97.0 0.9 shard_map.217
  97.9 6.0 %all-to-all-start.5 = ((bf16[8,64,256]{2,1,0:T(8,128)(2,1)}), bf16[8,64,256]{2,1,0:T(8,128)(2,1)S(1)}, u32[]{:S(2)}, u32[]{:S(2)}) async-start(bf16[8,64,256]{2,1,0:T(8,128)(2,1)} %shard_map.217), calls=%async_computation.5 | async-start | bytes 524288 | tf_op jit(solution)/shard_map/all_to_all | solution.py:542
  103.9 0.1 broadcast_in_dim_reshape.3.skip
  104.0 2.3 %shard_map.218 = (f32[256,256]{1,0:T(8,128)S(1)}, f32[256,256]{1,0:T(8,128)S(1)}, f32[256,256]{1,0:T(8,128)S(1)}, f32[256,512]{1,0:T(8,128)S(1)}, f32[8,256]{1,0:T(8,128)S(1)}, /*index=5*/f32[8,256]{1,0:T(8,128)S(1)}) custom-call(bf16[256,512]{1,0:T(8,128)(2,1)S(1)} %bitcast.13, f32[256,128]{1,0:T(8,128)S(1)} %get-tuple-element.64.cols_ref, ...), custom_call_target="tpu_custom_call" | custom-call | tf_op jit(solution)/shard_map/pallas_call | solution.py:28
  106.3 0.7 copy-done.3
  107.0 3.1 %all-to-all-done.5.got = bf16[8,64,256]{2,1,0:T(8,128)(2,1)S(1)} async-done(((bf16[8,64,256]{2,1,0:T(8,128)(2,1)}), bf16[8,64,256]{2,1,0:T(8,128)(2,1)S(1)}, u32[]{:S(2)}, u32[]{:S(2)}) %all-to-all-start.5) | async-done | bytes 262176 | tf_op jit(solution)/shard_map/all_to_all | solution.py:542
  110.1 0.9 copy-done.4
  111.0 1.9 shard_map.219
  113.0 10.8 %all_to_all.62.got = bf16[16,16,512]{2,1,0:T(8,128)(2,1)S(1)} all-to-all(bf16[16,16,512]{2,1,0:T(8,128)(2,1)S(1)} %get-tuple-element.73), channel_id=1, replica_groups=mesh['fsdp'=16,'zh'=4,'zl'=4,'xh'=2] {'fsdp'}, dimensions={0} | all-to-all | bytes 524288 | tf_op jit(solution)/shard_map/all_to_all | solution.py:542
  123.8 12.3 %all_to_all.63.got = bf16[16,24,512]{2,1,0:T(8,128)(2,1)S(1)} all-to-all(bf16[16,24,512]{2,1,0:T(8,128)(2,1)S(1)} %shard_map.220), channel_id=1, replica_groups=mesh['fsdp'=16,'zh'=4,'zl'=4,'xh'=2] {'fsdp'}, dimensions={0} | all-to-all | bytes 786432 | tf_op jit(solution)/shard_map/all_to_all | solution.py:542
  136.1 0.7 copy-done.11
  136.8 1.1 shard_map.221
  137.9 5.5 %collective-permute-start.2 = (f32[8,256]{1,0:T(8,128)S(1)}, f32[8,256]{1,0:T(8,128)S(1)}, u32[]{:S(2)}, u32[]{:S(2)}) collective-permute-start(f32[8,256]{1,0:T(8,128)S(1)} %get-tuple-element.84), channel_id=1, source_target_pairs={{1,0},{2,1},{3,2},{4,3},{5,4},{6,5},{7,6},{8,7},{9,8},{10,9},{11,1... | collective-permute-start | bytes 24584 | tf_op jit(solution)/shard_map/ppermute | solution.py:546
  143.4 2.8 %collective-permute-start.3 = (f32[8,256]{1,0:T(8,128)S(1)}, f32[8,256]{1,0:T(8,128)S(1)}, u32[]{:S(2)}, u32[]{:S(2)}) collective-permute-start(f32[8,256]{1,0:T(8,128)S(1)} %get-tuple-element.85), channel_id=1, source_target_pairs={{0,1},{1,2},{2,3},{3,4},{4,5},{5,6},{6,7},{7,8},{8,9},{9,10},{10,1... | collective-permute-start | bytes 24584 | tf_op jit(solution)/shard_map/ppermute | solution.py:546
  146.2 4.2 %collective-permute-done.3.from_prev = f32[8,256]{1,0:T(8,128)S(1)} collective-permute-done((f32[8,256]{1,0:T(8,128)S(1)}, f32[8,256]{1,0:T(8,128)S(1)}, u32[]{:S(2)}, u32[]{:S(2)}) %collective-permute-start.3) | collective-permute-done | bytes 8224 | tf_op jit(solution)/shard_map/ppermute | solution.py:546
  150.4 0.7 shard_map.222
  151.2 8.0 %all_to_all.64.got.cross = f32[16,1,384]{2,1,0:T(1,128)S(1)} all-to-all(f32[16,1,384]{2,1,0:T(1,128)S(1)} %get-tuple-element.87), channel_id=1, replica_groups=mesh['fsdp'=16,'zh'=4,'zl'=4,'xh'=2] {'fsdp'}, dimensions={0} | all-to-all | bytes 49152 | tf_op jit(solution)/shard_map/all_to_all | solution.py:542
  159.1 12.7 %all_to_all.65.got = bf16[8,96,128]{2,1,0:T(8,128)(2,1)S(1)} all-to-all(bf16[8,96,128]{2,1,0:T(8,128)(2,1)S(1)} %get-tuple-element.89), channel_id=1, replica_groups=mesh['fsdp'=16,'zh'=4,'zl'=4,'xh'=2] {'zl','xh'}, dimensions={0} | all-to-all | bytes 393216 | tf_op jit(solution)/shard_map/all_to_all | solution.py:542
  171.8 19.6 %all_to_all.66.got = bf16[4,96,128]{2,1,0:T(8,128)(2,1)S(1)} all-to-all(bf16[4,96,128]{2,1,0:T(8,128)(2,1)S(1)} %shard_map.224), channel_id=1, replica_groups=mesh['fsdp'=16,'zh'=4,'zl'=4,'xh'=2] {'zh'}, dimensions={0} | all-to-all | bytes 196608 | tf_op jit(solution)/shard_map/all_to_all | solution.py:542
  191.4 0.7 shard_map.225
  192.1 6.6 %all-to-all-start.11 = ((bf16[8,96,128]{2,1,0:T(8,128)(2,1)}), bf16[8,96,128]{2,1,0:T(8,128)(2,1)S(1)}, u32[]{:S(2)}, u32[]{:S(2)}) async-start(bf16[8,96,128]{2,1,0:T(8,128)(2,1)} %shard_map.225), calls=%async_computation.11 | async-start | bytes 393216 | tf_op jit(solution)/shard_map/all_to_all | solution.py:542
  198.7 1.1 shard_map.223
  199.8 4.7 %all-to-all-done.11.got = bf16[8,96,128]{2,1,0:T(8,128)(2,1)S(1)} async-done(((bf16[8,96,128]{2,1,0:T(8,128)(2,1)}), bf16[8,96,128]{2,1,0:T(8,128)(2,1)S(1)}, u32[]{:S(2)}, u32[]{:S(2)}) %all-to-all-start.11) | async-done | bytes 196640 | tf_op jit(solution)/shard_map/all_to_all | solution.py:542
  204.5 0.8 shard_map.226
  (34 shorter events, 0.4 us)
Async XLA Ops:
  0.6 0.7 copy-start.1
  1.4 21.0 %copy-start.9 = (bf16[256,64]{0,1:T(8,128)(2,1)S(1)}, bf16[256,64]{0,1:T(8,128)(2,1)}, u32[]{:S(2)}) copy-start(bf16[256,64]{0,1:T(8,128)(2,1)} %param.19) | copy-start | bytes 98308
  2.1 20.3 %copy-start.2 = (f32[16,256]{1,0:T(8,128)S(1)}, f32[16,256]{1,0:T(8,128)}, u32[]{:S(2)}) copy-start(f32[16,256]{1,0:T(8,128)} %table.11) | copy-start | bytes 49156
  2.1 20.2 %all-to-all-start = ((f32[16,1,128]{2,1,0:T(1,128)}), f32[16,1,128]{2,1,0:T(1,128)S(1)}, u32[]{:S(2)}, u32[]{:S(2)}) async-start(f32[16,1,128]{2,1,0:T(1,128)} %shard_map.211), calls=%async_computation | async-start | bytes 16384 | tf_op jit(solution)/shard_map/all_to_all | solution.py:542
  8.9 8.4 %collective-permute-start.1 = (s32[1,256]{1,0:T(1,128)S(1)}, s32[1,256]{1,0:T(1,128)S(1)}, u32[]{:S(2)}, u32[]{:S(2)}) collective-permute-start(s32[1,256]{1,0:T(1,128)S(1)} %bitcast.22), channel_id=1, source_target_pairs={{1,0},{2,1},{3,2},{4,3},{5,4},{6,5},{7,6},{8,7},{9,8},{10,9},{11,1... | collective-permute-start | bytes 3080 | tf_op jit(solution)/shard_map/ppermute | solution.py:546
  15.4 7.0 %collective-permute-start = (s32[1,256]{1,0:T(1,128)S(1)}, s32[1,256]{1,0:T(1,128)S(1)}, u32[]{:S(2)}, u32[]{:S(2)}) collective-permute-start(s32[1,256]{1,0:T(1,128)S(1)} %bitcast.23), channel_id=1, source_target_pairs={{0,1},{1,2},{2,3},{3,4},{4,5},{5,6},{6,7},{7,8},{8,9},{9,10},{10,1... | collective-permute-start | bytes 3080 | tf_op jit(solution)/shard_map/ppermute | solution.py:546
  22.4 0.7 copy-start.12
  23.1 0.8 copy-start.5
  23.9 0.8 copy-start.7
  24.7 0.7 copy-start.10
  25.4 0.7 copy-start.13
  41.7 4.7 %copy-start.15 = (f32[4]{0:T(128)S(1)}, f32[4]{0:T(128)}, u32[]{:S(2)}) copy-start(f32[4]{0:T(128)} %param.21) | copy-start | bytes 52
  41.7 5.4 %copy-start = (bf16[256,256]{1,0:T(8,128)(2,1)S(1)}, bf16[256,256]{1,0:T(8,128)(2,1)}, u32[]{:S(2)}) copy-start(bf16[256,256]{1,0:T(8,128)(2,1)} %dy.5) | copy-start | bytes 393220
  41.7 11.4 %all-to-all-start.2 = ((bf16[16,16,512]{2,1,0:T(8,128)(2,1)}), bf16[16,16,512]{2,1,0:T(8,128)(2,1)S(1)}, u32[]{:S(2)}, u32[]{:S(2)}) async-start(bf16[16,16,512]{2,1,0:T(8,128)(2,1)} %get-tuple-element.57), calls=%async_computation.2 | async-start | bytes 524288 | tf_op jit(solution)/shard_map/all_to_all | solution.py:542
  46.4 0.7 copy-start.16
  69.3 27.7 %all-to-all-start.4 = ((bf16[4,72,256]{2,1,0:T(8,128)(2,1)}), bf16[4,72,256]{2,1,0:T(8,128)(2,1)S(1)}, u32[]{:S(2)}, u32[]{:S(2)}) async-start(bf16[4,72,256]{2,1,0:T(8,128)(2,1)} %shard_map.216), calls=%async_computation.4 | async-start | bytes 294912 | tf_op jit(solution)/shard_map/all_to_all | solution.py:542
  97.9 6.0 %copy-start.14 = (f32[4]{0:T(128)S(1)}, f32[4]{0:T(128)}, u32[]{:S(2)}) copy-start(f32[4]{0:T(128)} %param.22) | copy-start | bytes 52
  97.9 12.2 %all-to-all-start.5 = ((bf16[8,64,256]{2,1,0:T(8,128)(2,1)}), bf16[8,64,256]{2,1,0:T(8,128)(2,1)S(1)}, u32[]{:S(2)}, u32[]{:S(2)}) async-start(bf16[8,64,256]{2,1,0:T(8,128)(2,1)} %shard_map.217), calls=%async_computation.5 | async-start | bytes 524288 | tf_op jit(solution)/shard_map/all_to_all | solution.py:542
  106.3 0.7 copy-start.3
  110.1 1.0 copy-start.4
  123.8 12.3 %copy-start.6 = (bf16[256,128]{1,0:T(8,128)(2,1)S(1)}, bf16[256,128]{1,0:T(8,128)(2,1)}, u32[]{:S(2)}) copy-start(bf16[256,128]{1,0:T(8,128)(2,1)} %wb.3) | copy-start | bytes 196612
  123.8 12.3 %copy-start.8 = (bf16[256,128]{1,0:T(8,128)(2,1)S(1)}, bf16[256,128]{1,0:T(8,128)(2,1)}, u32[]{:S(2)}) copy-start(bf16[256,128]{1,0:T(8,128)(2,1)} %wc.3) | copy-start | bytes 196612
  136.1 0.7 copy-start.11
  137.9 8.3 %collective-permute-start.2 = (f32[8,256]{1,0:T(8,128)S(1)}, f32[8,256]{1,0:T(8,128)S(1)}, u32[]{:S(2)}, u32[]{:S(2)}) collective-permute-start(f32[8,256]{1,0:T(8,128)S(1)} %get-tuple-element.84), channel_id=1, source_target_pairs={{1,0},{2,1},{3,2},{4,3},{5,4},{6,5},{7,6},{8,7},{9,8},{10,9},{11,1... | collective-permute-start | bytes 24584 | tf_op jit(solution)/shard_map/ppermute | solution.py:546
  143.4 7.0 %collective-permute-start.3 = (f32[8,256]{1,0:T(8,128)S(1)}, f32[8,256]{1,0:T(8,128)S(1)}, u32[]{:S(2)}, u32[]{:S(2)}) collective-permute-start(f32[8,256]{1,0:T(8,128)S(1)} %get-tuple-element.85), channel_id=1, source_target_pairs={{0,1},{1,2},{2,3},{3,4},{4,5},{5,6},{6,7},{7,8},{8,9},{9,10},{10,1... | collective-permute-start | bytes 24584 | tf_op jit(solution)/shard_map/ppermute | solution.py:546
  192.1 12.4 %all-to-all-start.11 = ((bf16[8,96,128]{2,1,0:T(8,128)(2,1)}), bf16[8,96,128]{2,1,0:T(8,128)(2,1)S(1)}, u32[]{:S(2)}, u32[]{:S(2)}) async-start(bf16[8,96,128]{2,1,0:T(8,128)(2,1)} %shard_map.225), calls=%async_computation.11 | async-start | bytes 393216 | tf_op jit(solution)/shard_map/all_to_all | solution.py:542

commit v4 on v3

--- a/solution.py
+++ b/solution.py
@@ -19,18 +19,19 @@
 VMEM = pltpu.VMEM
 
 
-def call(kernel, outs, *args, final=(), scratch=()):
+def call(kernel, outs, *args, final=(), scratch=(), near=True):
     shapes = tuple(
         jax.ShapeDtypeStruct(shape, kind) if i in final else VMEM(shape, kind)
         for i, (shape, kind) in enumerate(outs)
     )
-    near = [pltpu.with_memory_space_constraint(arg, VMEM) for arg in args]
+    space = VMEM if near else pltpu.HBM
+    args = [pltpu.with_memory_space_constraint(arg, space) for arg in args]
     return pl.pallas_call(
         kernel,
         out_shape=shapes,
         scratch_shapes=scratch,
         compiler_params=pltpu.CompilerParams(vmem_limit_bytes=24 << 20),
-    )(*near)
+    )(*args)
 
 
 def iota(shape, dim):
@@ -101,8 +102,33 @@
     send[...] = jnp.broadcast_to(sums[0:1][None], (GROUPS, 1, 128))
 
 
+def fetch_kernel(
+    table, gain, cw, cb, wb, wc, swt, step_bias, log_rate, skip_gain, dy,
+    table_v, gain_v, cw_v, cb_v, wb_v, wc_v, swt_v, swx, bias, rate, skip, dy_v,
+):
+    table_v[...] = table[...]
+    gain_v[...] = gain[...]
+    cw_v[...] = cw[...]
+    cb_v[...] = cb[...]
+    wb_v[...] = wb[...]
+    wc_v[...] = wc[...]
+    swt_v[...] = swt[...]
+    dy_v[...] = dy[...]
+    place = iota((128, 64), 0)
+    chosen = jnp.where(place // 8 * 4 + place % 4 == iota((128, 64), 1), 1.0, 0.0).astype(BF16)
+    swx[...] = mm(chosen, swt[...]).astype(BF16)
+    own = iota((8, HEADS), 0) % HEADS == iota((8, HEADS), 1)
+    for source, column in ((step_bias, bias), (log_rate, rate)):
+        column[...] = jnp.sum(jnp.where(own, source[...], 0.0), axis=1, keepdims=True)
+    lane_head = iota((1, 256), 1) // 64
+    row = jnp.zeros((1, 256), F32)
+    for h in range(HEADS):
+        row = jnp.where(lane_head == h, skip_gain[:, h : h + 1], row)
+    skip[...] = row
+
+
 def tokens_kernel(
-    ids, ids_prev, ids_next, got, table, gain, cw, cb, wb, wc, swt,
+    ids, ids_prev, ids_next, place, got, table, gain, cw, cb, wb, wc, swx,
     xf, xr, gf, gr, send, oht_ref, scale,
 ):
     total = got[0]
@@ -113,19 +139,21 @@
     scale[...] = spread
     unit = spread[:, 0:1]
     normed = (table[...] * unit * gain[...]).astype(BF16).astype(F32)
-    vocab = iota((16, ROWS), 0) + 1
+    vocab = iota((16, ROWS), 0)
     lane = iota((1, ROWS), 1)
     here = ids[...]
+    following = jnp.where(place[...] == FAR * NEAR - 1, -1, ids_next[...])
+    preceding = jnp.where(place[...] == 0, -1, ids_prev[...])
     hits = []
     for o in range(7):
         d = o - 3
         if d == 0:
             moved = here
         elif d > 0:
-            ahead = pltpu.roll(ids_next[...], ROWS - d, 1)
+            ahead = pltpu.roll(following, ROWS - d, 1)
             moved = jnp.where(lane < ROWS - d, pltpu.roll(here, ROWS - d, 1), ahead)
         else:
-            moved = jnp.where(lane >= -d, pltpu.roll(here, -d, 1), pltpu.roll(ids_prev[...], -d, 1))
+            moved = jnp.where(lane >= -d, pltpu.roll(here, -d, 1), pltpu.roll(preceding, -d, 1))
         hits.append(jnp.where(moved == vocab, 1.0, 0.0))
     hits.append(jnp.zeros((16, ROWS), F32))
     oht = jnp.concatenate(hits, axis=0).astype(BF16)
@@ -148,10 +176,7 @@
             part = mm(half, weight[...]).astype(BF16).reshape(GROUPS, 16, 128)
             send[:, 0:16, at : at + 128] = part
     own = iota((128, 256), 0) % 8 < 4
-    place = iota((128, 64), 0)
-    chosen = jnp.where(place // 8 * 4 + place % 4 == iota((128, 64), 1), 1.0, 0.0).astype(BF16)
-    swx = mm(chosen, swt[...]).astype(BF16)
-    steps = jnp.where(own, mm_nt(swx, halves[0]), mm_nt(swx, halves[1]))
+    steps = jnp.where(own, mm_nt(swx[...], halves[0]), mm_nt(swx[...], halves[1]))
     high, low = pieces(steps, 2)
     send[:, 16:24, 0:256] = high.reshape(GROUPS, 8, 256)
     send[:, 16:24, 256:512] = low.reshape(GROUPS, 8, 256)
@@ -253,8 +278,8 @@
     send[...] = jnp.broadcast_to(totals.astype(BF16)[None], (FAR, 72, 256))
 
 
-def chain_kernel(got, far, group, out):
-    here = group[...]
+def chain_kernel(got, far, place, out):
+    here = place[...] // NEAR
     nothing = jnp.zeros((16, 256), F32)
     up = (nothing, nothing)
     down = (nothing, nothing)
@@ -318,8 +343,8 @@
         total = total + by_head(intra, masks)
         dx_ref[...] = direct + by_head(back, masks)
         dhalf = dinner.astype(BF16)
-        dbc[:, br * 256 : br * 256 + 128] = mm_tn(dhalf, c)
-        dbc[:, br * 256 + 128 : br * 256 + 256] = mm(dhalf, b)
+        dbc[:, br * 256 : br * 256 + 128] = mm_tn(dhalf, c).astype(BF16)
+        dbc[:, br * 256 + 128 : br * 256 + 256] = mm(dhalf, b).astype(BF16)
     y_ref[...] = total
     side[...] = jnp.transpose(side_acc)[0:8]
     line[...] = jnp.concatenate(lines, axis=0)
@@ -410,9 +435,15 @@
     send[:, 16:24, :] = jnp.broadcast_to(padded.astype(BF16)[None], (GROUPS, 8, 512))
 
 
+def split_row(value, rows):
+    row = iota((rows, 128), 0) % 32
+    high = value.astype(BF16).astype(F32)
+    return jnp.where(row == 0, high, 0.0) + jnp.where(row == 1, value - high, 0.0)
+
+
 def project_back_kernel(
     got, xf, xr, gf, gr, dxf, dxr, wb, wc, swt, oht, table, scale, gain, cw, small,
-    dpf, dpr, to_prev, to_next, send, cpart,
+    dpf, dpr, to_prev, to_next, send,
 ):
     dbc = got[:, 0:16, :].reshape(ROWS, 512)
     draw = got[:, 16:24, 0:256].astype(F32).reshape(128, 256).astype(BF16)
@@ -450,35 +481,38 @@
     placed = jnp.concatenate(
         [jnp.zeros((88, 256), F32), shared, jnp.zeros((24, 256), F32)], axis=0
     )
-    cpart[...] = exact(mm_nt, jnp.ones((8, 256), BF16), placed, 3, False)[0:1]
+    crossed = exact(mm_nt, jnp.ones((8, 256), BF16), placed, 3, False)[0:1]
     stacked = jnp.concatenate(
         [jnp.zeros((64, 256), F32), ids_sum] + taps + [bias_row, small[0:3], jnp.zeros((40, 256), F32)],
         axis=0,
     )
     last = jnp.concatenate([thin, jnp.zeros((256, 64), F32)], axis=1) + jnp.transpose(stacked)
+    last = last + split_row(crossed, 256)
     send[:, 0:32, :] = wide[:, 0:128].astype(BF16).reshape(NEAR, 32, 128)
     send[:, 32:64, :] = wide[:, 128:256].astype(BF16).reshape(NEAR, 32, 128)
     send[:, 64:96, :] = last.astype(BF16).reshape(NEAR, 32, 128)
 
 
-def normed_kernel(
-    dpf, dpr, from_next, from_prev, cw, gain, table, oht, cpart,
-    gn_ref, cross, ahead, behind,
-):
+def ahead_kernel(dpf, from_next, cw, part, ahead):
     ahead[0:ROWS] = dpf[...]
     ahead[ROWS : ROWS + 8] = from_next[...]
+    total = cw[0:1] * ahead[0:ROWS]
+    for k in range(1, 4):
+        total = total + cw[k : k + 1] * ahead[k : k + ROWS]
+    part[...] = total
+
+
+def normed_kernel(part, dpr, from_prev, cw, gain, table, oht, gn_ref, cross, behind):
     behind[0:8] = from_prev[...]
     behind[8 : ROWS + 8] = dpr[...]
-    dn = jnp.zeros((ROWS, 256), F32)
+    dn = part[...]
     for k in range(4):
-        dn = dn + cw[k : k + 1] * (ahead[k : k + ROWS] + behind[8 - k : 8 - k + ROWS])
+        dn = dn + cw[k : k + 1] * behind[8 - k : 8 - k + ROWS]
     gn = dn.astype(BF16)
     gn_ref[...] = gn
     rated = exact(mm_tn, oht[48:64], table[...] * gain[...], 3, False)
     ones = jnp.ones((8, 256), BF16)
-    row = exact(mm_nt, ones, gn.astype(F32) * rated, 3, False)[0:1]
-    row = jnp.concatenate([row, cpart[...]], axis=1)
-    cross[...] = jnp.broadcast_to(row[None], (GROUPS, 1, 384))
+    cross[...] = exact(mm_nt, ones, gn.astype(F32) * rated, 3, False)[0:1]
 
 
 def embedded_kernel(got, gn, gain, table, scale, oht, out):
@@ -493,34 +527,40 @@
     out[...] = (turned * gn[...].astype(F32) - shrunk * cross).astype(BF16)
 
 
-def near_kernel(got, cross, send):
+def near_kernel(got, send):
     total = got[0].astype(F32)
     for k in range(1, NEAR):
         total = total + got[k].astype(F32)
-    here = cross[0]
-    for k in range(1, GROUPS):
-        here = here + cross[k]
-    here = here[:, 256:384]
-    high = here.astype(BF16).astype(F32)
-    row = iota((96, 128), 0)
-    total = total + jnp.where(row == 64, high, 0.0) + jnp.where(row == 65, here - high, 0.0)
+    last = total[64:96]
+    lane = iota((32, 128), 1)
+    crossed = jnp.where((lane >= 88) & (lane < 104), last, 0.0)
+    last = last - crossed + split_row(jnp.sum(crossed, axis=0, keepdims=True), 32)
+    total = jnp.concatenate([total[0:64], last], axis=0)
     send[...] = jnp.broadcast_to(total.astype(BF16)[None], (FAR, 96, 128))
 
 
-def far_kernel(got, send):
+def far_kernel(got, cross, send, payload):
     total = got[0].astype(F32)
     for k in range(1, FAR):
         total = total + got[k].astype(F32)
     send[...] = jnp.broadcast_to(total.astype(BF16)[None], (NEAR, 96, 128))
-
-
-def finish_kernel(got, table, scale, gain, gt, gg, gcw, gcb, gwb, gwc, gswt, gsb, glr, gsg):
+    lane = iota((1, 128), 1)
+    both = total[64:65] + total[65:66]
+    crossed = jnp.where((lane >= 88) & (lane < 104), both, 0.0)
+    row = jnp.concatenate([cross[...], crossed], axis=1)
+    payload[...] = jnp.broadcast_to(row[None], (GROUPS, 1, 384))
+
+
+def finish_kernel(got, cross, table, scale, gain, gt, gg, gcw, gcb, gwb, gwc, gswt, gsb, glr, gsg):
     gwb[...] = got[:, 0:32, :].astype(F32).reshape(256, 128)
     gwc[...] = got[:, 32:64, :].astype(F32).reshape(256, 128)
     rows = jnp.transpose(got[:, 64:96, :].astype(F32).reshape(256, 128))
     gswt[...] = rows[0:64]
     sums = rows[64:80]
-    crossed = jnp.sum(rows[88:104], axis=1, keepdims=True)
+    here = cross[0]
+    for k in range(1, GROUPS):
+        here = here + cross[k]
+    crossed = jnp.transpose(jnp.broadcast_to(here[:, 256:384], (128, 128)))[88:104, 0:1]
     unit = scale[:, 0:1]
     gt[...] = unit * gain[...] * sums - table[...] * (unit * unit * unit / D) * crossed
     gg[...] = jnp.sum(table[...] * unit * sums, axis=0, keepdims=True)
@@ -566,18 +606,32 @@
     edge = ((8, 256), F32)
     square = ((ROWS, 256), F32)
     half_square = ((ROWS, 256), BF16)
-    (squares,) = call(squares_kernel, (((GROUPS, 1, 128), F32),), table)
+    (squares,) = call(squares_kernel, (((GROUPS, 1, 128), F32),), table, near=False)
     squares = swap(squares, "fsdp")
-    marked = token_ids[None] + 1
-    ids_prev = shift(marked, up)
-    ids_next = shift(marked, down)
-    gain = norm_gain[None]
-    group = lax.axis_index("zh").reshape(1, 1)
-    swt = jnp.transpose(step_weight)
-    bias = jnp.tile(step_bias, 2)[:, None]
-    rate = jnp.tile(log_rate, 2)[:, None]
-    skip = jnp.repeat(skip_gain, 64)[None]
-
+    ids = token_ids[None]
+    ids_prev = shift(ids, up)
+    ids_next = shift(ids, down)
+    place = lax.axis_index(CTX).reshape(1, 1)
+    table, gain, cw, cb, wb, wc, swt, swx, bias, rate, skip, dy = call(
+        fetch_kernel,
+        (
+            ((16, 256), F32),
+            ((1, 256), F32),
+            ((4, 256), F32),
+            ((1, 256), F32),
+            ((256, 128), BF16),
+            ((256, 128), BF16),
+            ((64, 256), BF16),
+            ((128, 256), BF16),
+            ((8, 1), F32),
+            ((8, 1), F32),
+            ((1, 256), F32),
+            half_square,
+        ),
+        table, norm_gain[None], conv_weight, conv_bias[None], weight_b, weight_c,
+        jnp.transpose(step_weight), step_bias[None], log_rate[None], skip_gain[None], out_grad,
+        near=False,
+    )
     xf, xr, gf, gr, part, oht, scale = call(
         tokens_kernel,
         (
@@ -589,8 +643,7 @@
             ((128, 256), BF16),
             ((16, 128), F32),
         ),
-        marked, ids_prev, ids_next, squares, table, gain, conv_weight, conv_bias[None],
-        weight_b, weight_c, swt,
+        ids, ids_prev, ids_next, place, squares, table, gain, cw, cb, wb, wc, swx,
     )
     bc, raw = call(reduce_kernel, (((GROUPS, 16, 512), BF16), ((8, 256), F32)), swap(part, "fsdp"))
     bc = swap(bc, "fsdp").reshape(ROWS, 512)
@@ -598,7 +651,7 @@
     cols, rows, weighted, turned, packed = call(
         steps_kernel,
         (((ROWS, 128), F32), ((48, ROWS), F32), half_pair, half_pair, edge),
-        raw, bias, rate, xf, xr, out_grad,
+        raw, bias, rate, xf, xr, dy,
     )
     (states,) = call(
         states_kernel, (((NEAR, 72, 256), BF16),), bc, weighted, turned, packed
@@ -606,12 +659,12 @@
     arrived = swap(states, BESIDE)
     y0, dxf0, dxr0, dbc0, side, line = call(
         within_kernel,
-        (square, square, square, ((ROWS, 512), F32), ((8, ROWS), F32), ((8, ROWS), F32)),
-        bc, cols, rows, xf, xr, out_grad, skip,
+        (square, square, square, ((ROWS, 512), BF16), edge, edge),
+        bc, cols, rows, xf, xr, dy, skip,
     )
     (groups,) = call(group_kernel, (((FAR, 72, 256), BF16),), arrived)
     groups = swap(groups, "zh")
-    (entering,) = call(chain_kernel, (((NEAR, 64, 256), BF16),), arrived, groups, group)
+    (entering,) = call(chain_kernel, (((NEAR, 64, 256), BF16),), arrived, groups, place)
     entering = swap(entering, BESIDE)
     mixer_out, dxf, dxr, dpart, draw, small = call(
         carried_kernel,
@@ -623,30 +676,35 @@
             ((8, 256), BF16),
             edge,
         ),
-        entering, bc, cols, weighted, turned, rows, xf, xr, out_grad,
+        entering, bc, cols, weighted, turned, rows, xf, xr, dy,
         y0, dxf0, dxr0, dbc0, side, line, rate,
         final=(0,),
     )
     (totals,) = call(total_kernel, (((GROUPS, 24, 512), BF16),), swap(dpart, "fsdp"), draw)
-    dpf, dpr, to_prev, to_next, gsend, cpart = call(
+    dpf, dpr, to_prev, to_next, gsend = call(
         project_back_kernel,
-        (square, square, edge, edge, ((NEAR, 96, 128), BF16), ((1, 128), F32)),
-        swap(totals, "fsdp"), xf, xr, gf, gr, dxf, dxr, weight_b,
-        weight_c, swt, oht, table, scale, gain, conv_weight, small,
+        (square, square, edge, edge, ((NEAR, 96, 128), BF16)),
+        swap(totals, "fsdp"), xf, xr, gf, gr, dxf, dxr, wb,
+        wc, swt, oht, table, scale, gain, cw, small,
     )
     from_next = shift(to_prev, down)
     from_prev = shift(to_next, up)
     reduced = swap(gsend, BESIDE)
+    (ahead,) = call(
+        ahead_kernel, (square,), dpf, from_next, cw, scratch=[VMEM((ROWS + 8, 256), F32)]
+    )
     gn, cross = call(
         normed_kernel,
-        (half_square, ((GROUPS, 1, 384), F32)),
-        dpf, dpr, from_next, from_prev, conv_weight, gain, table, oht, cpart,
-        scratch=[VMEM((ROWS + 8, 256), F32), VMEM((ROWS + 8, 256), F32)],
-    )
-    crossed = swap(cross, "fsdp")
-    (summed,) = call(near_kernel, (((FAR, 96, 128), BF16),), reduced, crossed)
+        (half_square, ((1, 256), F32)),
+        ahead, dpr, from_prev, cw, gain, table, oht,
+        scratch=[VMEM((ROWS + 8, 256), F32)],
+    )
+    (summed,) = call(near_kernel, (((FAR, 96, 128), BF16),), reduced)
     summed = swap(summed, "zh")
-    (gathered,) = call(far_kernel, (((NEAR, 96, 128), BF16),), summed)
+    gathered, payload = call(
+        far_kernel, (((NEAR, 96, 128), BF16), ((GROUPS, 1, 384), F32)), summed, cross
+    )
+    crossed = swap(payload, "fsdp")
     (grad_embedded,) = call(
         embedded_kernel, (half_square,), crossed, gn, gain, table, scale, oht, final=(0,)
     )
@@ -664,7 +722,7 @@
             ((1, 4), F32),
             ((1, 4), F32),
         ),
-        swap(gathered, BESIDE), table, scale, gain,
+        swap(gathered, BESIDE), crossed, table, scale, gain,
         final=range(10),
     )
     gt, gg, gcw, gcb, gwb, gwc, gswt, gsb, glr, gsg = outs

time: 209 us -> 188 us (0.90)
  waiting for transfers between devices: 37.2 us -> 23.6 us
  starting transfers between devices: 52.5 us -> 42.8 us
  blocking collectives: 92.3 us -> 101 us
  local copies, waits for them, and re-layouts: 7.68 us -> 0.67 us
    all_to_all x5, waiting for transfers between devices: 27.9 us -> 16.8 us  [swap(): return lax.all_to_all(value, axis, 0, 0, tiled=True)]
    all_to_all x5, starting transfers between devices: 35.8 us -> 26.1 us  [swap(): return lax.all_to_all(value, axis, 0, 0, tiled=True)]
    all_to_all x7, blocking collectives: 92.3 us -> 101 us  [swap(): return lax.all_to_all(value, axis, 0, 0, tiled=True)]
    unnamed x34 -> x2, local copies, waits for them, and re-layouts: 7.37 us -> 0.67 us
    ppermute x4, waiting for transfers between devices: 9.26 us -> 6.82 us  [shift(): return lax.ppermute(value, CTX, pairs)]
    pallas_call x16 -> x18, Pallas kernels: 14.2 us -> 16.1 us  [call(): pl.pallas_call(kernel, out_shape=shapes, scratch_shapes=scratch, compiler...]
  transfers between devices with their start and end apart: 9 -> 9, of which waited for: 6 -> 6; matrix products, arithmetic and copies ran while one was open for 0% -> 0% of each run, Pallas kernels for 2% -> 4%
where the time goes in v4:
time: 188 us; the launch traced here: 185 us
  blocking collectives  101 us (54%)
  starting transfers between devices  42.8 us (23%)
  waiting for transfers between devices  23.6 us (13%)
  Pallas kernels  16.1 us (9%)
    all_to_all x7, blocking collectives, swap(): return lax.all_to_all(value, axis, 0, 0, tiled=True)  101 us
    all_to_all x5, starting transfers between devices, swap(): return lax.all_to_all(value, axis, 0, 0, tiled=True)  26.1 us
    all_to_all x5, waiting for transfers between devices, swap(): return lax.all_to_all(value, axis, 0, 0, tiled=True)  16.8 us
    ppermute x4, starting transfers between devices, shift(): return lax.ppermute(value, CTX, pairs)  16.7 us
    pallas_call x18, Pallas kernels, call(): pl.pallas_call(kernel, out_shape=shapes, scratch_shapes=scratch, compiler...  16.1 us
    ppermute x4, waiting for transfers between devices, shift(): return lax.ppermute(value, CTX, pairs)  6.82 us
  transfers between devices with their start and end apart: 9, of which 6 were waited for; matrix products, arithmetic and copies ran while one was open for 0% of the time, Pallas kernels for 4%

profile of v4, /device:TPU:6, one launch (start us, length us, event | category | flops | bytes accessed | tf_op | source)
XLA Modules:
  0.0 185.2 jit_solution(2685392042838128132)
XLA Ops:
  0.6 1.5 shard_map.211
  2.1 5.9 %all-to-all-start = ((f32[16,1,128]{2,1,0:T(1,128)}), f32[16,1,128]{2,1,0:T(1,128)S(1)}, u32[]{:S(2)}, u32[]{:S(2)}) async-start(f32[16,1,128]{2,1,0:T(1,128)} %shard_map.211), calls=%async_computation | async-start | bytes 16384 | tf_op jit(solution)/shard_map/all_to_all | solution.py:582
  8.1 0.0 copy-start
  8.1 0.7 copy-done
  8.7 6.5 %collective-permute-start.1 = (s32[1,256]{1,0:T(1,128)S(1)}, s32[1,256]{1,0:T(1,128)S(1)}, u32[]{:S(2)}, u32[]{:S(2)}) collective-permute-start(s32[1,256]{1,0:T(1,128)S(1)} %bitcast.18), channel_id=1, source_target_pairs={{1,0},{2,1},{3,2},{4,3},{5,4},{6,5},{7,6},{8,7},{9,8},{10,9},{11,1... | collective-permute-start | bytes 3080 | tf_op jit(solution)/shard_map/ppermute | solution.py:586
  15.3 1.9 %collective-permute-start = (s32[1,256]{1,0:T(1,128)S(1)}, s32[1,256]{1,0:T(1,128)S(1)}, u32[]{:S(2)}, u32[]{:S(2)}) collective-permute-start(s32[1,256]{1,0:T(1,128)S(1)} %bitcast.19), channel_id=1, source_target_pairs={{0,1},{1,2},{2,3},{3,4},{4,5},{5,6},{6,7},{7,8},{8,9},{9,10},{10,1... | collective-permute-start | bytes 3080 | tf_op jit(solution)/shard_map/ppermute | solution.py:586
  17.2 1.2 shard_map.212
  18.4 0.0 collective-permute-done.1.ids_next
  18.5 3.8 %collective-permute-done.ids_prev = s32[1,256]{1,0:T(1,128)S(1)} collective-permute-done((s32[1,256]{1,0:T(1,128)S(1)}, s32[1,256]{1,0:T(1,128)S(1)}, u32[]{:S(2)}, u32[]{:S(2)}) %collective-permute-start) | collective-permute-done | bytes 1056 | tf_op jit(solution)/shard_map/ppermute | solution.py:586
  22.2 0.0 all-to-all-done.got
  22.2 0.9 shard_map.213
  23.2 13.9 %all_to_all.60.got = bf16[16,24,512]{2,1,0:T(8,128)(2,1)S(1)} all-to-all(bf16[16,24,512]{2,1,0:T(8,128)(2,1)S(1)} %get-tuple-element.76), channel_id=1, replica_groups=mesh['fsdp'=16,'zh'=4,'zl'=4,'xh'=2] {'fsdp'}, dimensions={0} | all-to-all | bytes 786432 | tf_op jit(solution)/shard_map/all_to_all | solution.py:582
  37.0 0.8 shard_map.214
  37.8 4.6 %all-to-all-start.2 = ((bf16[16,16,512]{2,1,0:T(8,128)(2,1)}), bf16[16,16,512]{2,1,0:T(8,128)(2,1)S(1)}, u32[]{:S(2)}, u32[]{:S(2)}) async-start(bf16[16,16,512]{2,1,0:T(8,128)(2,1)} %get-tuple-element.77), calls=%async_computation.2 | async-start | bytes 524288 | tf_op jit(solution)/shard_map/all_to_all | solution.py:582
  42.4 1.2 shard_map.215
  43.5 5.6 %all-to-all-done.2 = bf16[16,16,512]{2,1,0:T(8,128)(2,1)S(1)} async-done(((bf16[16,16,512]{2,1,0:T(8,128)(2,1)}), bf16[16,16,512]{2,1,0:T(8,128)(2,1)S(1)}, u32[]{:S(2)}, u32[]{:S(2)}) %all-to-all-start.2) | async-done | bytes 262176 | tf_op jit(solution)/shard_map/all_to_all | solution.py:582
  49.1 0.3 shard_map.216
  49.4 15.2 %all_to_all.61.got = bf16[8,72,256]{2,1,0:T(8,128)(2,1)S(1)} all-to-all(bf16[8,72,256]{2,1,0:T(8,128)(2,1)S(1)} %shard_map.216), channel_id=1, replica_groups=mesh['fsdp'=16,'zh'=4,'zl'=4,'xh'=2] {'zl','xh'}, dimensions={0} | all-to-all | bytes 589824 | tf_op jit(solution)/shard_map/all_to_all | solution.py:582
  64.6 0.1 shard_map.217
  64.7 27.5 %all_to_all.62.far = bf16[4,72,256]{2,1,0:T(8,128)(2,1)S(1)} all-to-all(bf16[4,72,256]{2,1,0:T(8,128)(2,1)S(1)} %shard_map.217), channel_id=1, replica_groups=mesh['fsdp'=16,'zh'=4,'zl'=4,'xh'=2] {'zh'}, dimensions={0} | all-to-all | bytes 294912 | tf_op jit(solution)/shard_map/all_to_all | solution.py:582
  92.2 0.9 shard_map.218
  93.0 5.9 %all-to-all-start.5 = ((bf16[8,64,256]{2,1,0:T(8,128)(2,1)}), bf16[8,64,256]{2,1,0:T(8,128)(2,1)S(1)}, u32[]{:S(2)}, u32[]{:S(2)}) async-start(bf16[8,64,256]{2,1,0:T(8,128)(2,1)} %shard_map.218), calls=%async_computation.5 | async-start | bytes 524288 | tf_op jit(solution)/shard_map/all_to_all | solution.py:582
  98.9 2.3 %shard_map.219 = (f32[256,256]{1,0:T(8,128)S(1)}, f32[256,256]{1,0:T(8,128)S(1)}, f32[256,256]{1,0:T(8,128)S(1)}, bf16[256,512]{1,0:T(8,128)(2,1)S(1)}, f32[8,256]{1,0:T(8,128)S(1)}, /*index=5*/f32[8,256]{1,0:T(8,128)S(1)}) custom-call(bf16[256,512]{1,0:T(8,128)(2,1)S(1)} %bitcast.16, f32[256,128]{1,0:T(8,128)S(1)} %get-tuple-element.87.cols_ref, ...), custom_call_target="tpu_custom_call" | custom-call | tf_op jit(solution)/shard_map/pallas_call | solution.py:29
  101.2 3.9 %all-to-all-done.5.got = bf16[8,64,256]{2,1,0:T(8,128)(2,1)S(1)} async-done(((bf16[8,64,256]{2,1,0:T(8,128)(2,1)}), bf16[8,64,256]{2,1,0:T(8,128)(2,1)S(1)}, u32[]{:S(2)}, u32[]{:S(2)}) %all-to-all-start.5) | async-done | bytes 262176 | tf_op jit(solution)/shard_map/all_to_all | solution.py:582
  105.1 1.6 shard_map.220
  106.8 10.8 %all_to_all.63.got = bf16[16,16,512]{2,1,0:T(8,128)(2,1)S(1)} all-to-all(bf16[16,16,512]{2,1,0:T(8,128)(2,1)S(1)} %get-tuple-element.97), channel_id=1, replica_groups=mesh['fsdp'=16,'zh'=4,'zl'=4,'xh'=2] {'fsdp'}, dimensions={0} | all-to-all | bytes 524288 | tf_op jit(solution)/shard_map/all_to_all | solution.py:582
  117.6 12.2 %all_to_all.64.got = bf16[16,24,512]{2,1,0:T(8,128)(2,1)S(1)} all-to-all(bf16[16,24,512]{2,1,0:T(8,128)(2,1)S(1)} %shard_map.221), channel_id=1, replica_groups=mesh['fsdp'=16,'zh'=4,'zl'=4,'xh'=2] {'fsdp'}, dimensions={0} | all-to-all | bytes 786432 | tf_op jit(solution)/shard_map/all_to_all | solution.py:582
  129.8 1.2 shard_map.222
  130.9 13.4 %all_to_all.65.got = bf16[8,96,128]{2,1,0:T(8,128)(2,1)S(1)} all-to-all(bf16[8,96,128]{2,1,0:T(8,128)(2,1)S(1)} %get-tuple-element.107), channel_id=1, replica_groups=mesh['fsdp'=16,'zh'=4,'zl'=4,'xh'=2] {'zl','xh'}, dimensions={0} | all-to-all | bytes 393216 | tf_op jit(solution)/shard_map/all_to_all | solution.py:582
  144.4 0.7 shard_map.223
  145.1 3.4 %all-to-all-start.9 = ((bf16[4,96,128]{2,1,0:T(8,128)(2,1)}), bf16[4,96,128]{2,1,0:T(8,128)(2,1)S(1)}, u32[]{:S(2)}, u32[]{:S(2)}) async-start(bf16[4,96,128]{2,1,0:T(8,128)(2,1)} %shard_map.223), calls=%async_computation.9 | async-start | bytes 196608 | tf_op jit(solution)/shard_map/all_to_all | solution.py:582
  148.4 4.5 %collective-permute-start.2 = (f32[8,256]{1,0:T(8,128)S(1)}, f32[8,256]{1,0:T(8,128)S(1)}, u32[]{:S(2)}, u32[]{:S(2)}) collective-permute-start(f32[8,256]{1,0:T(8,128)S(1)} %get-tuple-element.109), channel_id=1, source_target_pairs={{1,0},{2,1},{3,2},{4,3},{5,4},{6,5},{7,6},{8,7},{9,8},{10,9},{11,1... | collective-permute-start | bytes 24584 | tf_op jit(solution)/shard_map/ppermute | solution.py:586
  152.9 3.8 %collective-permute-start.3 = (f32[8,256]{1,0:T(8,128)S(1)}, f32[8,256]{1,0:T(8,128)S(1)}, u32[]{:S(2)}, u32[]{:S(2)}) collective-permute-start(f32[8,256]{1,0:T(8,128)S(1)} %get-tuple-element.111), channel_id=1, source_target_pairs={{0,1},{1,2},{2,3},{3,4},{4,5},{5,6},{6,7},{7,8},{8,9},{9,10},{10,1... | collective-permute-start | bytes 24584 | tf_op jit(solution)/shard_map/ppermute | solution.py:586
  156.7 0.0 collective-permute-done.2.from_next
  156.7 0.2 shard_map.224.part
  156.9 3.0 %collective-permute-done.3.from_prev = f32[8,256]{1,0:T(8,128)S(1)} collective-permute-done((f32[8,256]{1,0:T(8,128)S(1)}, f32[8,256]{1,0:T(8,128)S(1)}, u32[]{:S(2)}, u32[]{:S(2)}) %collective-permute-start.3) | collective-permute-done | bytes 8224 | tf_op jit(solution)/shard_map/ppermute | solution.py:586
  159.9 0.6 shard_map.225
  160.6 1.1 all-to-all-done.9.got
  161.7 0.7 shard_map.226
  162.4 8.3 %all_to_all.66.got.cross = f32[16,1,384]{2,1,0:T(1,128)S(1)} all-to-all(f32[16,1,384]{2,1,0:T(1,128)S(1)} %get-tuple-element.113), channel_id=1, replica_groups=mesh['fsdp'=16,'zh'=4,'zl'=4,'xh'=2] {'fsdp'}, dimensions={0} | all-to-all | bytes 49152 | tf_op jit(solution)/shard_map/all_to_all | solution.py:582
  170.7 6.4 %all-to-all-start.11 = ((bf16[8,96,128]{2,1,0:T(8,128)(2,1)}), bf16[8,96,128]{2,1,0:T(8,128)(2,1)S(1)}, u32[]{:S(2)}, u32[]{:S(2)}) async-start(bf16[8,96,128]{2,1,0:T(8,128)(2,1)} %get-tuple-element.115), calls=%async_computation.11 | async-start | bytes 393216 | tf_op jit(solution)/shard_map/all_to_all | solution.py:582
  177.1 1.1 shard_map.227
  178.2 6.1 %all-to-all-done.11.got = bf16[8,96,128]{2,1,0:T(8,128)(2,1)S(1)} async-done(((bf16[8,96,128]{2,1,0:T(8,128)(2,1)}), bf16[8,96,128]{2,1,0:T(8,128)(2,1)S(1)}, u32[]{:S(2)}, u32[]{:S(2)}) %all-to-all-start.11) | async-done | bytes 196640 | tf_op jit(solution)/shard_map/all_to_all | solution.py:582
  184.3 0.9 shard_map.228
  (1 shorter events, 0.0 us)
Async XLA Ops:
  2.1 20.1 %all-to-all-start = ((f32[16,1,128]{2,1,0:T(1,128)}), f32[16,1,128]{2,1,0:T(1,128)S(1)}, u32[]{:S(2)}, u32[]{:S(2)}) async-start(f32[16,1,128]{2,1,0:T(1,128)} %shard_map.211), calls=%async_computation | async-start | bytes 16384 | tf_op jit(solution)/shard_map/all_to_all | solution.py:582
  8.1 0.7 copy-start
  8.7 9.7 %collective-permute-start.1 = (s32[1,256]{1,0:T(1,128)S(1)}, s32[1,256]{1,0:T(1,128)S(1)}, u32[]{:S(2)}, u32[]{:S(2)}) collective-permute-start(s32[1,256]{1,0:T(1,128)S(1)} %bitcast.18), channel_id=1, source_target_pairs={{1,0},{2,1},{3,2},{4,3},{5,4},{6,5},{7,6},{8,7},{9,8},{10,9},{11,1... | collective-permute-start | bytes 3080 | tf_op jit(solution)/shard_map/ppermute | solution.py:586
  15.3 7.0 %collective-permute-start = (s32[1,256]{1,0:T(1,128)S(1)}, s32[1,256]{1,0:T(1,128)S(1)}, u32[]{:S(2)}, u32[]{:S(2)}) collective-permute-start(s32[1,256]{1,0:T(1,128)S(1)} %bitcast.19), channel_id=1, source_target_pairs={{0,1},{1,2},{2,3},{3,4},{4,5},{5,6},{6,7},{7,8},{8,9},{9,10},{10,1... | collective-permute-start | bytes 3080 | tf_op jit(solution)/shard_map/ppermute | solution.py:586
  37.8 11.3 %all-to-all-start.2 = ((bf16[16,16,512]{2,1,0:T(8,128)(2,1)}), bf16[16,16,512]{2,1,0:T(8,128)(2,1)S(1)}, u32[]{:S(2)}, u32[]{:S(2)}) async-start(bf16[16,16,512]{2,1,0:T(8,128)(2,1)} %get-tuple-element.77), calls=%async_computation.2 | async-start | bytes 524288 | tf_op jit(solution)/shard_map/all_to_all | solution.py:582
  93.0 12.1 %all-to-all-start.5 = ((bf16[8,64,256]{2,1,0:T(8,128)(2,1)}), bf16[8,64,256]{2,1,0:T(8,128)(2,1)S(1)}, u32[]{:S(2)}, u32[]{:S(2)}) async-start(bf16[8,64,256]{2,1,0:T(8,128)(2,1)} %shard_map.218), calls=%async_computation.5 | async-start | bytes 524288 | tf_op jit(solution)/shard_map/all_to_all | solution.py:582
  145.1 16.6 %all-to-all-start.9 = ((bf16[4,96,128]{2,1,0:T(8,128)(2,1)}), bf16[4,96,128]{2,1,0:T(8,128)(2,1)S(1)}, u32[]{:S(2)}, u32[]{:S(2)}) async-start(bf16[4,96,128]{2,1,0:T(8,128)(2,1)} %shard_map.223), calls=%async_computation.9 | async-start | bytes 196608 | tf_op jit(solution)/shard_map/all_to_all | solution.py:582
  148.4 8.3 %collective-permute-start.2 = (f32[8,256]{1,0:T(8,128)S(1)}, f32[8,256]{1,0:T(8,128)S(1)}, u32[]{:S(2)}, u32[]{:S(2)}) collective-permute-start(f32[8,256]{1,0:T(8,128)S(1)} %get-tuple-element.109), channel_id=1, source_target_pairs={{1,0},{2,1},{3,2},{4,3},{5,4},{6,5},{7,6},{8,7},{9,8},{10,9},{11,1... | collective-permute-start | bytes 24584 | tf_op jit(solution)/shard_map/ppermute | solution.py:586
  152.9 7.0 %collective-permute-start.3 = (f32[8,256]{1,0:T(8,128)S(1)}, f32[8,256]{1,0:T(8,128)S(1)}, u32[]{:S(2)}, u32[]{:S(2)}) collective-permute-start(f32[8,256]{1,0:T(8,128)S(1)} %get-tuple-element.111), channel_id=1, source_target_pairs={{0,1},{1,2},{2,3},{3,4},{4,5},{5,6},{6,7},{7,8},{8,9},{9,10},{10,1... | collective-permute-start | bytes 24584 | tf_op jit(solution)/shard_map/ppermute | solution.py:586
  170.7 13.6 %all-to-all-start.11 = ((bf16[8,96,128]{2,1,0:T(8,128)(2,1)}), bf16[8,96,128]{2,1,0:T(8,128)(2,1)S(1)}, u32[]{:S(2)}, u32[]{:S(2)}) async-start(bf16[8,96,128]{2,1,0:T(8,128)(2,1)} %get-tuple-element.115), calls=%async_computation.11 | async-start | bytes 393216 | tf_op jit(solution)/shard_map/all_to_all | solution.py:582

commit v5 on v4

--- a/solution.py
+++ b/solution.py
@@ -96,7 +96,8 @@
     return jnp.where(before, 1.0, 0.0).astype(BF16), jnp.where(after, 1.0, 0.0).astype(BF16)
 
 
-def squares_kernel(table, send):
+def squares_kernel(table, ids, send, ids_v):
+    ids_v[...] = ids[...]
     squares = jnp.concatenate([table[...] * table[...], jnp.zeros((112, 256), F32)], axis=0)
     sums = exact(mm_nt, jnp.ones((8, 256), BF16), squares, 3, False)
     send[...] = jnp.broadcast_to(sums[0:1][None], (GROUPS, 1, 128))
@@ -128,7 +129,7 @@
 
 
 def tokens_kernel(
-    ids, ids_prev, ids_next, place, got, table, gain, cw, cb, wb, wc, swx,
+    ids, ids_pair, ids_side, place, got, table, gain, cw, cb, wb, wc, swx,
     xf, xr, gf, gr, send, oht_ref, scale,
 ):
     total = got[0]
@@ -142,8 +143,11 @@
     vocab = iota((16, ROWS), 0)
     lane = iota((1, ROWS), 1)
     here = ids[...]
-    following = jnp.where(place[...] == FAR * NEAR - 1, -1, ids_next[...])
-    preceding = jnp.where(place[...] == 0, -1, ids_prev[...])
+    even = place[...] % 2 == 0
+    following = jnp.where(even, ids_pair[...], ids_side[...])
+    following = jnp.where(place[...] == FAR * NEAR - 1, -1, following)
+    preceding = jnp.where(even, ids_side[...], ids_pair[...])
+    preceding = jnp.where(place[...] == 0, -1, preceding)
     hits = []
     for o in range(7):
         d = o - 3
@@ -350,18 +354,27 @@
     line[...] = jnp.concatenate(lines, axis=0)
 
 
+def state(got, ch):
+    return got[:, ch * 16 : ch * 16 + 16, :].reshape(STATE, 256)
+
+
+def partials_kernel(got, weighted, turned, dbc0, send):
+    for br, at_state, at_grad in ((0, 0, 3), (1, 2, 1)):
+        dc = mm_nt(turned[br], state(got, at_state))
+        db = mm_nt(weighted[br], state(got, at_grad))
+        at = br * 256
+        part = dbc0[:, at : at + 256].astype(F32) + jnp.concatenate([db, dc], axis=1)
+        send[:, :, at : at + 256] = part.astype(BF16).reshape(16, 16, 256)
+
+
 def carried_kernel(
-    got, bc, cols_ref, weighted, turned, rows_ref, xf, xr, dy,
-    y0, dxf0, dxr0, dbc0, side, line, rate,
-    out, dxf, dxr, send, draw_ref, small,
+    got, bc, cols_ref, rows_ref, xf, xr, dy, y0, dxf0, dxr0, side, line, rate,
+    out, dxf, dxr, draw_ref, small,
 ):
     dyf = dy[...].astype(F32)
 
     masks = head_masks(ROWS)
     cols = cols_ref[...]
-
-    def state(ch):
-        return got[:, ch * 16 : ch * 16 + 16, :].reshape(STATE, 256)
 
     row_at = iota((8, 256), 0)
     lane_head = iota((8, 256), 1) // 64
@@ -370,8 +383,8 @@
     dw = jnp.zeros((8, ROWS), F32)
     d_end = jnp.zeros((8, 1), F32)
     for br, x, dx0, dx_ref, at_state, at_grad in ((0, xf, dxf0, dxf, 0, 3), (1, xr, dxr0, dxr, 2, 1)):
-        start_half = state(at_state)
-        ahead_half = state(at_grad)
+        start_half = state(got, at_state)
+        ahead_half = state(got, at_grad)
         b = bc[:, br * 256 : br * 256 + 128]
         c = bc[:, br * 256 + 128 : br * 256 + 256]
         heads = jnp.where(lane_head + 4 * br == row_at, 1.0, 0.0).astype(BF16)
@@ -382,13 +395,6 @@
         toward = mm(b, ahead_half)
         dx_ref[...] = dx0[...] + expand(cols, 16 + 4 * br, masks) * toward
         dw = dw + exact(mm_nt, heads, xv * toward, 2, False)
-        dc = mm_nt(turned[br], start_half)
-        db = mm_nt(weighted[br], ahead_half)
-        at = br * 256
-        send[:, :, at : at + 128] = (dbc0[:, at : at + 128] + db).astype(BF16).reshape(16, 16, 128)
-        send[:, :, at + 128 : at + 256] = (
-            (dbc0[:, at + 128 : at + 256] + dc).astype(BF16).reshape(16, 16, 128)
-        )
         both = jnp.sum(start_half.astype(F32) * ahead_half.astype(F32), axis=0, keepdims=True)
         spread = jnp.where(lane_head + 4 * br == row_at, both, 0.0)
         d_end = d_end + jnp.sum(spread, axis=1, keepdims=True)
@@ -603,14 +609,20 @@
     size = lax.axis_size(CTX)
     up = [(i, i + 1) for i in range(size - 1)]
     down = [(i + 1, i) for i in range(size - 1)]
+    within = [(i, i ^ 1) for i in range(size)]
+    across = [pair for i in range(1, size - 1, 2) for pair in ((i, i + 1), (i + 1, i))]
     edge = ((8, 256), F32)
     square = ((ROWS, 256), F32)
     half_square = ((ROWS, 256), BF16)
-    (squares,) = call(squares_kernel, (((GROUPS, 1, 128), F32),), table, near=False)
+    squares, ids = call(
+        squares_kernel,
+        (((GROUPS, 1, 128), F32), ((1, ROWS), jnp.int32)),
+        table, token_ids[None],
+        near=False,
+    )
     squares = swap(squares, "fsdp")
-    ids = token_ids[None]
-    ids_prev = shift(ids, up)
-    ids_next = shift(ids, down)
+    ids_pair = shift(ids, within)
+    ids_side = shift(ids, across)
     place = lax.axis_index(CTX).reshape(1, 1)
     table, gain, cw, cb, wb, wc, swt, swx, bias, rate, skip, dy = call(
         fetch_kernel,
@@ -643,7 +655,7 @@
             ((128, 256), BF16),
             ((16, 128), F32),
         ),
-        ids, ids_prev, ids_next, place, squares, table, gain, cw, cb, wb, wc, swx,
+        ids, ids_pair, ids_side, place, squares, table, gain, cw, cb, wb, wc, swx,
     )
     bc, raw = call(reduce_kernel, (((GROUPS, 16, 512), BF16), ((8, 256), F32)), swap(part, "fsdp"))
     bc = swap(bc, "fsdp").reshape(ROWS, 512)
@@ -666,18 +678,13 @@
     groups = swap(groups, "zh")
     (entering,) = call(chain_kernel, (((NEAR, 64, 256), BF16),), arrived, groups, place)
     entering = swap(entering, BESIDE)
-    mixer_out, dxf, dxr, dpart, draw, small = call(
+    (dpart,) = call(
+        partials_kernel, (((GROUPS, 16, 512), BF16),), entering, weighted, turned, dbc0
+    )
+    mixer_out, dxf, dxr, draw, small = call(
         carried_kernel,
-        (
-            half_square,
-            square,
-            square,
-            ((GROUPS, 16, 512), BF16),
-            ((8, 256), BF16),
-            edge,
-        ),
-        entering, bc, cols, weighted, turned, rows, xf, xr, dy,
-        y0, dxf0, dxr0, dbc0, side, line, rate,
+        (half_square, square, square, ((8, 256), BF16), edge),
+        entering, bc, cols, rows, xf, xr, dy, y0, dxf0, dxr0, side, line, rate,
         final=(0,),
     )
     (totals,) = call(total_kernel, (((GROUPS, 24, 512), BF16),), swap(dpart, "fsdp"), draw)

time: 188 us -> 188 us (level)
  blocking collectives: 101 us -> 92.9 us
  waiting for transfers between devices: 23.6 us -> 27.5 us
  starting transfers between devices: 42.8 us -> 46 us
    all_to_all x7 -> x6, blocking collectives: 101 us -> 92.9 us  [swap(): return lax.all_to_all(value, axis, 0, 0, tiled=True)]
    all_to_all x5 -> x6, starting transfers between devices: 26.1 us -> 30.7 us  [swap(): return lax.all_to_all(value, axis, 0, 0, tiled=True)]
    all_to_all x5 -> x6, waiting for transfers between devices: 16.8 us -> 21.3 us  [swap(): return lax.all_to_all(value, axis, 0, 0, tiled=True)]
    pallas_call x18 -> x19, Pallas kernels: 16.1 us -> 17.5 us  [call(): pl.pallas_call(kernel, out_shape=shapes, scratch_shapes=scratch, compiler...]
  transfers between devices with their start and end apart: 9 -> 10, of which waited for: 6 -> 7; matrix products, arithmetic and copies ran while one was open for 0% -> 0% of each run, Pallas kernels for 4% -> 5%
where the time goes in v5:
time: 188 us; the launch traced here: 185 us
  blocking collectives  92.9 us (49%)
  starting transfers between devices  46 us (24%)
  waiting for transfers between devices  27.5 us (15%)
  Pallas kernels  17.5 us (9%)
    all_to_all x6, blocking collectives, swap(): return lax.all_to_all(value, axis, 0, 0, tiled=True)  92.9 us
    all_to_all x6, starting transfers between devices, swap(): return lax.all_to_all(value, axis, 0, 0, tiled=True)  30.7 us
    all_to_all x6, waiting for transfers between devices, swap(): return lax.all_to_all(value, axis, 0, 0, tiled=True)  21.3 us
    pallas_call x19, Pallas kernels, call(): pl.pallas_call(kernel, out_shape=shapes, scratch_shapes=scratch, compiler...  17.5 us
    ppermute x4, starting transfers between devices, shift(): return lax.ppermute(value, CTX, pairs)  15.4 us
    ppermute x4, waiting for transfers between devices, shift(): return lax.ppermute(value, CTX, pairs)  6.24 us
  transfers between devices with their start and end apart: 10, of which 7 were waited for; matrix products, arithmetic and copies ran while one was open for 0% of the time, Pallas kernels for 5%

profile of v5, /device:TPU:6, one launch (start us, length us, event | category | flops | bytes accessed | tf_op | source)
XLA Modules:
  0.0 184.7 jit_solution(8577083285824427029)
XLA Ops:
  0.6 1.5 shard_map.211
  2.1 5.9 %all-to-all-start = ((f32[16,1,128]{2,1,0:T(1,128)}), f32[16,1,128]{2,1,0:T(1,128)S(1)}, u32[]{:S(2)}, u32[]{:S(2)}) async-start(f32[16,1,128]{2,1,0:T(1,128)} %get-tuple-element.71), calls=%async_computation | async-start | bytes 16384 | tf_op jit(solution)/shard_map/all_to_all | solution.py:588
  8.1 4.7 %collective-permute-start.1 = (s32[1,256]{1,0:T(1,128)S(1)}, s32[1,256]{1,0:T(1,128)S(1)}, u32[]{:S(2)}, u32[]{:S(2)}) collective-permute-start(s32[1,256]{1,0:T(1,128)S(1)} %get-tuple-element.70.ids), channel_id=1, source_target_pairs={{1,2},{2,1},{3,4},{4,3},{5,6},{6,5},{7,8},{8,7},{9,10},{10,9},{11,... | collective-permute-start | bytes 3080 | tf_op jit(solution)/shard_map/ppermute | solution.py:592
  12.7 2.5 %collective-permute-start = (s32[1,256]{1,0:T(1,128)S(1)}, s32[1,256]{1,0:T(1,128)S(1)}, u32[]{:S(2)}, u32[]{:S(2)}) collective-permute-start(s32[1,256]{1,0:T(1,128)S(1)} %get-tuple-element.70.ids), channel_id=1, source_target_pairs={{0,1},{1,0},{2,3},{3,2},{4,5},{5,4},{6,7},{7,6},{8,9},{9,8},{10,11... | collective-permute-start | bytes 3080 | tf_op jit(solution)/shard_map/ppermute | solution.py:592
  15.3 1.2 shard_map.212
  16.5 0.0 collective-permute-done.1.ids_side
  16.5 3.2 %collective-permute-done.ids_pair = s32[1,256]{1,0:T(1,128)S(1)} collective-permute-done((s32[1,256]{1,0:T(1,128)S(1)}, s32[1,256]{1,0:T(1,128)S(1)}, u32[]{:S(2)}, u32[]{:S(2)}) %collective-permute-start) | collective-permute-done | bytes 1056 | tf_op jit(solution)/shard_map/ppermute | solution.py:592
  19.7 0.0 all-to-all-done.got
  19.7 1.0 shard_map.213
  20.7 13.8 %all_to_all.60.got = bf16[16,24,512]{2,1,0:T(8,128)(2,1)S(1)} all-to-all(bf16[16,24,512]{2,1,0:T(8,128)(2,1)S(1)} %get-tuple-element.79), channel_id=1, replica_groups=mesh['fsdp'=16,'zh'=4,'zl'=4,'xh'=2] {'fsdp'}, dimensions={0} | all-to-all | bytes 786432 | tf_op jit(solution)/shard_map/all_to_all | solution.py:588
  34.5 0.8 shard_map.214
  35.2 4.6 %all-to-all-start.2 = ((bf16[16,16,512]{2,1,0:T(8,128)(2,1)}), bf16[16,16,512]{2,1,0:T(8,128)(2,1)S(1)}, u32[]{:S(2)}, u32[]{:S(2)}) async-start(bf16[16,16,512]{2,1,0:T(8,128)(2,1)} %get-tuple-element.80), calls=%async_computation.2 | async-start | bytes 524288 | tf_op jit(solution)/shard_map/all_to_all | solution.py:588
  39.8 1.2 shard_map.215
  41.0 5.6 %all-to-all-done.2 = bf16[16,16,512]{2,1,0:T(8,128)(2,1)S(1)} async-done(((bf16[16,16,512]{2,1,0:T(8,128)(2,1)}), bf16[16,16,512]{2,1,0:T(8,128)(2,1)S(1)}, u32[]{:S(2)}, u32[]{:S(2)}) %all-to-all-start.2) | async-done | bytes 262176 | tf_op jit(solution)/shard_map/all_to_all | solution.py:588
  46.6 0.3 shard_map.216
  46.8 19.2 %all_to_all.61.got = bf16[8,72,256]{2,1,0:T(8,128)(2,1)S(1)} all-to-all(bf16[8,72,256]{2,1,0:T(8,128)(2,1)S(1)} %shard_map.216), channel_id=1, replica_groups=mesh['fsdp'=16,'zh'=4,'zl'=4,'xh'=2] {'zl','xh'}, dimensions={0} | all-to-all | bytes 589824 | tf_op jit(solution)/shard_map/all_to_all | solution.py:588
  66.0 0.1 shard_map.217
  66.1 25.4 %all_to_all.62.far = bf16[4,72,256]{2,1,0:T(8,128)(2,1)S(1)} all-to-all(bf16[4,72,256]{2,1,0:T(8,128)(2,1)S(1)} %shard_map.217), channel_id=1, replica_groups=mesh['fsdp'=16,'zh'=4,'zl'=4,'xh'=2] {'zh'}, dimensions={0} | all-to-all | bytes 294912 | tf_op jit(solution)/shard_map/all_to_all | solution.py:588
  91.5 0.9 shard_map.218
  92.3 5.9 %all-to-all-start.5 = ((bf16[8,64,256]{2,1,0:T(8,128)(2,1)}), bf16[8,64,256]{2,1,0:T(8,128)(2,1)S(1)}, u32[]{:S(2)}, u32[]{:S(2)}) async-start(bf16[8,64,256]{2,1,0:T(8,128)(2,1)} %shard_map.218), calls=%async_computation.5 | async-start | bytes 524288 | tf_op jit(solution)/shard_map/all_to_all | solution.py:588
  98.2 2.3 %shard_map.219 = (f32[256,256]{1,0:T(8,128)S(1)}, f32[256,256]{1,0:T(8,128)S(1)}, f32[256,256]{1,0:T(8,128)S(1)}, bf16[256,512]{1,0:T(8,128)(2,1)S(1)}, f32[8,256]{1,0:T(8,128)S(1)}, /*index=5*/f32[8,256]{1,0:T(8,128)S(1)}) custom-call(bf16[256,512]{1,0:T(8,128)(2,1)S(1)} %bitcast.16, f32[256,128]{1,0:T(8,128)S(1)} %get-tuple-element.90.cols_ref, ...), custom_call_target="tpu_custom_call" | custom-call | tf_op jit(solution)/shard_map/pallas_call | solution.py:29
  100.5 3.9 %all-to-all-done.5.got = bf16[8,64,256]{2,1,0:T(8,128)(2,1)S(1)} async-done(((bf16[8,64,256]{2,1,0:T(8,128)(2,1)}), bf16[8,64,256]{2,1,0:T(8,128)(2,1)S(1)}, u32[]{:S(2)}, u32[]{:S(2)}) %all-to-all-start.5) | async-done | bytes 262176 | tf_op jit(solution)/shard_map/all_to_all | solution.py:588
  104.4 1.0 shard_map.221
  105.4 4.2 %all-to-all-start.6 = ((bf16[16,16,512]{2,1,0:T(8,128)(2,1)}), bf16[16,16,512]{2,1,0:T(8,128)(2,1)S(1)}, u32[]{:S(2)}, u32[]{:S(2)}) async-start(bf16[16,16,512]{2,1,0:T(8,128)(2,1)} %shard_map.221), calls=%async_computation.6 | async-start | bytes 524288 | tf_op jit(solution)/shard_map/all_to_all | solution.py:588
  109.6 2.1 %shard_map.220 = (bf16[256,256]{1,0:T(8,128)(2,1)}, f32[256,256]{1,0:T(8,128)S(1)}, f32[256,256]{1,0:T(8,128)S(1)}, bf16[8,256]{1,0:T(8,128)(2,1)S(1)}, f32[8,256]{1,0:T(8,128)S(1)}) custom-call(bf16[8,64,256]{2,1,0:T(8,128)(2,1)S(1)} %all-to-all-done.5.got, bf16[256,512]{1,0:T(8,128)(2,1)S(1)} %bitcast.17, f32[256,128]{1,0:T(8,128)S(1)} %get-tuple-element.90.cols_ref, ...), custom_call_target="tpu_custom_call" | custom-call | tf_op jit(solution)/shard_map/pallas_call | solution.py:29
  111.7 4.6 %all-to-all-done.6.got = bf16[16,16,512]{2,1,0:T(8,128)(2,1)S(1)} async-done(((bf16[16,16,512]{2,1,0:T(8,128)(2,1)}), bf16[16,16,512]{2,1,0:T(8,128)(2,1)S(1)}, u32[]{:S(2)}, u32[]{:S(2)}) %all-to-all-start.6) | async-done | bytes 262176 | tf_op jit(solution)/shard_map/all_to_all | solution.py:588
  116.4 12.2 %all_to_all.63.got = bf16[16,24,512]{2,1,0:T(8,128)(2,1)S(1)} all-to-all(bf16[16,24,512]{2,1,0:T(8,128)(2,1)S(1)} %shard_map.222), channel_id=1, replica_groups=mesh['fsdp'=16,'zh'=4,'zl'=4,'xh'=2] {'fsdp'}, dimensions={0} | all-to-all | bytes 786432 | tf_op jit(solution)/shard_map/all_to_all | solution.py:588
  128.6 1.2 shard_map.223
  129.7 13.9 %all_to_all.64.got = bf16[8,96,128]{2,1,0:T(8,128)(2,1)S(1)} all-to-all(bf16[8,96,128]{2,1,0:T(8,128)(2,1)S(1)} %get-tuple-element.109), channel_id=1, replica_groups=mesh['fsdp'=16,'zh'=4,'zl'=4,'xh'=2] {'zl','xh'}, dimensions={0} | all-to-all | bytes 393216 | tf_op jit(solution)/shard_map/all_to_all | solution.py:588
  143.7 0.7 shard_map.224
  144.3 3.6 %all-to-all-start.9 = ((bf16[4,96,128]{2,1,0:T(8,128)(2,1)}), bf16[4,96,128]{2,1,0:T(8,128)(2,1)S(1)}, u32[]{:S(2)}, u32[]{:S(2)}) async-start(bf16[4,96,128]{2,1,0:T(8,128)(2,1)} %shard_map.224), calls=%async_computation.9 | async-start | bytes 196608 | tf_op jit(solution)/shard_map/all_to_all | solution.py:588
  147.9 4.5 %collective-permute-start.2 = (f32[8,256]{1,0:T(8,128)S(1)}, f32[8,256]{1,0:T(8,128)S(1)}, u32[]{:S(2)}, u32[]{:S(2)}) collective-permute-start(f32[8,256]{1,0:T(8,128)S(1)} %get-tuple-element.111), channel_id=1, source_target_pairs={{1,0},{2,1},{3,2},{4,3},{5,4},{6,5},{7,6},{8,7},{9,8},{10,9},{11,1... | collective-permute-start | bytes 24584 | tf_op jit(solution)/shard_map/ppermute | solution.py:592
  152.4 3.8 %collective-permute-start.3 = (f32[8,256]{1,0:T(8,128)S(1)}, f32[8,256]{1,0:T(8,128)S(1)}, u32[]{:S(2)}, u32[]{:S(2)}) collective-permute-start(f32[8,256]{1,0:T(8,128)S(1)} %get-tuple-element.113), channel_id=1, source_target_pairs={{0,1},{1,2},{2,3},{3,4},{4,5},{5,6},{6,7},{7,8},{8,9},{9,10},{10,1... | collective-permute-start | bytes 24584 | tf_op jit(solution)/shard_map/ppermute | solution.py:592
  156.2 0.0 collective-permute-done.2.from_next
  156.2 0.2 shard_map.225.part
  156.4 3.1 %collective-permute-done.3.from_prev = f32[8,256]{1,0:T(8,128)S(1)} collective-permute-done((f32[8,256]{1,0:T(8,128)S(1)}, f32[8,256]{1,0:T(8,128)S(1)}, u32[]{:S(2)}, u32[]{:S(2)}) %collective-permute-start.3) | collective-permute-done | bytes 8224 | tf_op jit(solution)/shard_map/ppermute | solution.py:592
  159.4 0.6 shard_map.226
  160.1 1.0 all-to-all-done.9.got
  161.1 0.7 shard_map.227
  161.8 8.4 %all_to_all.65.got.cross = f32[16,1,384]{2,1,0:T(1,128)S(1)} all-to-all(f32[16,1,384]{2,1,0:T(1,128)S(1)} %get-tuple-element.115), channel_id=1, replica_groups=mesh['fsdp'=16,'zh'=4,'zl'=4,'xh'=2] {'fsdp'}, dimensions={0} | all-to-all | bytes 49152 | tf_op jit(solution)/shard_map/all_to_all | solution.py:588
  170.2 6.5 %all-to-all-start.11 = ((bf16[8,96,128]{2,1,0:T(8,128)(2,1)}), bf16[8,96,128]{2,1,0:T(8,128)(2,1)S(1)}, u32[]{:S(2)}, u32[]{:S(2)}) async-start(bf16[8,96,128]{2,1,0:T(8,128)(2,1)} %get-tuple-element.117), calls=%async_computation.11 | async-start | bytes 393216 | tf_op jit(solution)/shard_map/all_to_all | solution.py:588
  176.7 1.1 shard_map.228
  177.7 6.1 %all-to-all-done.11.got = bf16[8,96,128]{2,1,0:T(8,128)(2,1)S(1)} async-done(((bf16[8,96,128]{2,1,0:T(8,128)(2,1)}), bf16[8,96,128]{2,1,0:T(8,128)(2,1)S(1)}, u32[]{:S(2)}, u32[]{:S(2)}) %all-to-all-start.11) | async-done | bytes 196640 | tf_op jit(solution)/shard_map/all_to_all | solution.py:588
  183.8 0.9 shard_map.229
  (1 shorter events, 0.0 us)
Async XLA Ops:
  2.1 17.6 %all-to-all-start = ((f32[16,1,128]{2,1,0:T(1,128)}), f32[16,1,128]{2,1,0:T(1,128)S(1)}, u32[]{:S(2)}, u32[]{:S(2)}) async-start(f32[16,1,128]{2,1,0:T(1,128)} %get-tuple-element.71), calls=%async_computation | async-start | bytes 16384 | tf_op jit(solution)/shard_map/all_to_all | solution.py:588
  8.1 8.4 %collective-permute-start.1 = (s32[1,256]{1,0:T(1,128)S(1)}, s32[1,256]{1,0:T(1,128)S(1)}, u32[]{:S(2)}, u32[]{:S(2)}) collective-permute-start(s32[1,256]{1,0:T(1,128)S(1)} %get-tuple-element.70.ids), channel_id=1, source_target_pairs={{1,2},{2,1},{3,4},{4,3},{5,6},{6,5},{7,8},{8,7},{9,10},{10,9},{11,... | collective-permute-start | bytes 3080 | tf_op jit(solution)/shard_map/ppermute | solution.py:592
  12.7 7.0 %collective-permute-start = (s32[1,256]{1,0:T(1,128)S(1)}, s32[1,256]{1,0:T(1,128)S(1)}, u32[]{:S(2)}, u32[]{:S(2)}) collective-permute-start(s32[1,256]{1,0:T(1,128)S(1)} %get-tuple-element.70.ids), channel_id=1, source_target_pairs={{0,1},{1,0},{2,3},{3,2},{4,5},{5,4},{6,7},{7,6},{8,9},{9,8},{10,11... | collective-permute-start | bytes 3080 | tf_op jit(solution)/shard_map/ppermute | solution.py:592
  35.2 11.3 %all-to-all-start.2 = ((bf16[16,16,512]{2,1,0:T(8,128)(2,1)}), bf16[16,16,512]{2,1,0:T(8,128)(2,1)S(1)}, u32[]{:S(2)}, u32[]{:S(2)}) async-start(bf16[16,16,512]{2,1,0:T(8,128)(2,1)} %get-tuple-element.80), calls=%async_computation.2 | async-start | bytes 524288 | tf_op jit(solution)/shard_map/all_to_all | solution.py:588
  92.3 12.1 %all-to-all-start.5 = ((bf16[8,64,256]{2,1,0:T(8,128)(2,1)}), bf16[8,64,256]{2,1,0:T(8,128)(2,1)S(1)}, u32[]{:S(2)}, u32[]{:S(2)}) async-start(bf16[8,64,256]{2,1,0:T(8,128)(2,1)} %shard_map.218), calls=%async_computation.5 | async-start | bytes 524288 | tf_op jit(solution)/shard_map/all_to_all | solution.py:588
  105.4 11.0 %all-to-all-start.6 = ((bf16[16,16,512]{2,1,0:T(8,128)(2,1)}), bf16[16,16,512]{2,1,0:T(8,128)(2,1)S(1)}, u32[]{:S(2)}, u32[]{:S(2)}) async-start(bf16[16,16,512]{2,1,0:T(8,128)(2,1)} %shard_map.221), calls=%async_computation.6 | async-start | bytes 524288 | tf_op jit(solution)/shard_map/all_to_all | solution.py:588
  144.3 16.7 %all-to-all-start.9 = ((bf16[4,96,128]{2,1,0:T(8,128)(2,1)}), bf16[4,96,128]{2,1,0:T(8,128)(2,1)S(1)}, u32[]{:S(2)}, u32[]{:S(2)}) async-start(bf16[4,96,128]{2,1,0:T(8,128)(2,1)} %shard_map.224), calls=%async_computation.9 | async-start | bytes 196608 | tf_op jit(solution)/shard_map/all_to_all | solution.py:588
  147.9 8.3 %collective-permute-start.2 = (f32[8,256]{1,0:T(8,128)S(1)}, f32[8,256]{1,0:T(8,128)S(1)}, u32[]{:S(2)}, u32[]{:S(2)}) collective-permute-start(f32[8,256]{1,0:T(8,128)S(1)} %get-tuple-element.111), channel_id=1, source_target_pairs={{1,0},{2,1},{3,2},{4,3},{5,4},{6,5},{7,6},{8,7},{9,8},{10,9},{11,1... | collective-permute-start | bytes 24584 | tf_op jit(solution)/shard_map/ppermute | solution.py:592
  152.4 7.0 %collective-permute-start.3 = (f32[8,256]{1,0:T(8,128)S(1)}, f32[8,256]{1,0:T(8,128)S(1)}, u32[]{:S(2)}, u32[]{:S(2)}) collective-permute-start(f32[8,256]{1,0:T(8,128)S(1)} %get-tuple-element.113), channel_id=1, source_target_pairs={{0,1},{1,2},{2,3},{3,4},{4,5},{5,6},{6,7},{7,8},{8,9},{9,10},{10,1... | collective-permute-start | bytes 24584 | tf_op jit(solution)/shard_map/ppermute | solution.py:592
  170.2 13.7 %all-to-all-start.11 = ((bf16[8,96,128]{2,1,0:T(8,128)(2,1)}), bf16[8,96,128]{2,1,0:T(8,128)(2,1)S(1)}, u32[]{:S(2)}, u32[]{:S(2)}) async-start(bf16[8,96,128]{2,1,0:T(8,128)(2,1)} %get-tuple-element.117), calls=%async_computation.11 | async-start | bytes 393216 | tf_op jit(solution)/shard_map/all_to_all | solution.py:588

commit v6 on v5

--- a/solution.py
+++ b/solution.py
@@ -170,7 +170,7 @@
     for rows, x_ref, slope_ref in ((fwd_rows, xf, gf), (rev_rows, xr, gr)):
         pre = exact(mm_tn, oht, rows, 3, False) + cb[...]
         gate = 1.0 / (1.0 + jnp.exp(-pre))
-        slope_ref[...] = gate * (1.0 + pre * (1.0 - gate))
+        slope_ref[...] = (gate * (1.0 + pre * (1.0 - gate))).astype(BF16)
         half = (pre * gate).astype(BF16)
         x_ref[...] = half
         halves.append(half)
@@ -264,7 +264,8 @@
     return decay_first * state[0] + piece[0:16], decay_second * state[1] + piece[16:32]
 
 
-def group_kernel(got, send):
+def group_kernel(got, place, send):
+    here = place[...] // NEAR
     nothing = jnp.zeros((16, 256), F32)
     up = (nothing, nothing)
     down = (nothing, nothing)
@@ -278,8 +279,12 @@
         j = NEAR - 1 - i
         fwd_decay, rev_decay = join_decays(got[j, 64:72, :])
         down = advance(down, rev_decay, fwd_decay, got[j, 32:64, :].astype(F32))
-    totals = jnp.concatenate([up[0], up[1], down[0], down[1], split_decays(fwd_all, rev_all)], axis=0)
-    send[...] = jnp.broadcast_to(totals.astype(BF16)[None], (FAR, 72, 256))
+    upward = jnp.concatenate(up, axis=0)
+    downward = jnp.concatenate(down, axis=0)
+    decays = split_decays(fwd_all, rev_all).astype(BF16)
+    for g in range(FAR):
+        send[g, 0:32, :] = jnp.where(here < g, upward, downward).astype(BF16)
+        send[g, 32:40, :] = decays
 
 
 def chain_kernel(got, far, place, out):
@@ -288,12 +293,12 @@
     up = (nothing, nothing)
     down = (nothing, nothing)
     for g in range(FAR):
-        fwd_decay, rev_decay = join_decays(far[g, 64:72, :])
+        fwd_decay, rev_decay = join_decays(far[g, 32:40, :])
         moved = advance(up, fwd_decay, rev_decay, far[g, 0:32, :].astype(F32))
         up = tuple(jnp.where(here > g, new, old) for new, old in zip(moved, up))
         k = FAR - 1 - g
-        fwd_decay, rev_decay = join_decays(far[k, 64:72, :])
-        moved = advance(down, rev_decay, fwd_decay, far[k, 32:64, :].astype(F32))
+        fwd_decay, rev_decay = join_decays(far[k, 32:40, :])
+        moved = advance(down, rev_decay, fwd_decay, far[k, 0:32, :].astype(F32))
         down = tuple(jnp.where(here < k, new, old) for new, old in zip(moved, down))
     for i in range(NEAR):
         out[i, 0:16, :] = up[0].astype(BF16)
@@ -436,9 +441,10 @@
     total = got[0].astype(F32)
     for k in range(1, GROUPS):
         total = total + got[k].astype(F32)
-    send[:, 0:16, :] = jnp.broadcast_to(total.astype(BF16)[None], (GROUPS, 16, 512))
-    padded = jnp.concatenate([draw[...].astype(F32), jnp.zeros((8, 256), F32)], axis=1)
-    send[:, 16:24, :] = jnp.broadcast_to(padded.astype(BF16)[None], (GROUPS, 8, 512))
+    half = total.astype(BF16)
+    send[:, 0:16, :] = jnp.broadcast_to(half[None, :, 0:256], (GROUPS, 16, 256))
+    send[:, 16:32, :] = jnp.broadcast_to(half[None, :, 256:512], (GROUPS, 16, 256))
+    send[:, 32:40, :] = jnp.broadcast_to(draw[...][None], (GROUPS, 8, 256))
 
 
 def split_row(value, rows):
@@ -449,10 +455,9 @@
 
 def project_back_kernel(
     got, xf, xr, gf, gr, dxf, dxr, wb, wc, swt, oht, table, scale, gain, cw, small,
-    dpf, dpr, to_prev, to_next, send,
+    place, dpf, dpr, to_pair, to_side, send,
 ):
-    dbc = got[:, 0:16, :].reshape(ROWS, 512)
-    draw = got[:, 16:24, 0:256].astype(F32).reshape(128, 256).astype(BF16)
+    draw = got[:, 32:40, :].astype(F32).reshape(128, 256).astype(BF16)
     pick_row = iota((128, 64), 0)
     pick_col = iota((128, 64), 1)
     wanted = pick_row // 8 * 4 + pick_row % 4
@@ -465,11 +470,11 @@
     for br, x, slope, dx, out in ((0, xf, gf, dxf, dpf), (1, xr, gr, dxr, dpr)):
         mine = (wanted == pick_col) & ((pick_row % 8 < 4) == (br == 0))
         dstep = mm_tn(draw, jnp.where(mine, 1.0, 0.0).astype(BF16)).astype(BF16)
-        half = dbc[:, br * 256 : br * 256 + 256]
+        half = got[:, br * 16 : br * 16 + 16, :].reshape(ROWS, 256)
         into = mm_nt(half[:, 0:128], wb[...]) + mm_nt(half[:, 128:256], wc[...])
         into = into + mm(dstep, swt[...])
         whole = (dx[...] + into).astype(BF16).astype(F32)
-        dpre = whole * slope[...]
+        dpre = whole * slope[...].astype(F32)
         out[...] = dpre
         wide = wide + mm_tn(x[...], half)
         thin = thin + mm_tn(x[...], dstep)
@@ -481,8 +486,9 @@
             part = jnp.sum(normed * block, axis=0, keepdims=True)
             taps[k] = taps[k] + part
         bias_row = bias_row + jnp.sum(dpre, axis=0, keepdims=True)
-    to_prev[...] = dpf[0:8]
-    to_next[...] = dpr[ROWS - 8 : ROWS]
+    even = place[...] % 2 == 0
+    to_pair[...] = jnp.where(even, dpr[ROWS - 8 : ROWS], dpf[0:8])
+    to_side[...] = jnp.where(even, dpf[0:8], dpr[ROWS - 8 : ROWS])
     shared = table[...] * gain[...] * ids_sum
     placed = jnp.concatenate(
         [jnp.zeros((88, 256), F32), shared, jnp.zeros((24, 256), F32)], axis=0
@@ -499,21 +505,22 @@
     send[:, 64:96, :] = last.astype(BF16).reshape(NEAR, 32, 128)
 
 
-def ahead_kernel(dpf, from_next, cw, part, ahead):
+def catch_kernel(edge, caught):
+    caught[...] = edge[...]
+
+
+def normed_kernel(
+    dpf, dpr, from_pair, from_side, place, cw, gain, table, oht,
+    gn_ref, cross, ahead, behind,
+):
+    even = place[...] % 2 == 0
     ahead[0:ROWS] = dpf[...]
-    ahead[ROWS : ROWS + 8] = from_next[...]
-    total = cw[0:1] * ahead[0:ROWS]
-    for k in range(1, 4):
-        total = total + cw[k : k + 1] * ahead[k : k + ROWS]
-    part[...] = total
-
-
-def normed_kernel(part, dpr, from_prev, cw, gain, table, oht, gn_ref, cross, behind):
-    behind[0:8] = from_prev[...]
+    ahead[ROWS : ROWS + 8] = jnp.where(even, from_pair[...], from_side[...])
+    behind[0:8] = jnp.where(even, from_side[...], from_pair[...])
     behind[8 : ROWS + 8] = dpr[...]
-    dn = part[...]
+    dn = jnp.zeros((ROWS, 256), F32)
     for k in range(4):
-        dn = dn + cw[k : k + 1] * behind[8 - k : 8 - k + ROWS]
+        dn = dn + cw[k : k + 1] * (ahead[k : k + ROWS] + behind[8 - k : 8 - k + ROWS])
     gn = dn.astype(BF16)
     gn_ref[...] = gn
     rated = exact(mm_tn, oht[48:64], table[...] * gain[...], 3, False)
@@ -607,8 +614,6 @@
     out_grad,
 ):
     size = lax.axis_size(CTX)
-    up = [(i, i + 1) for i in range(size - 1)]
-    down = [(i + 1, i) for i in range(size - 1)]
     within = [(i, i ^ 1) for i in range(size)]
     across = [pair for i in range(1, size - 1, 2) for pair in ((i, i + 1), (i + 1, i))]
     edge = ((8, 256), F32)
@@ -649,8 +654,8 @@
         (
             half_square,
             half_square,
-            square,
-            square,
+            half_square,
+            half_square,
             ((GROUPS, 24, 512), BF16),
             ((128, 256), BF16),
             ((16, 128), F32),
@@ -674,7 +679,7 @@
         (square, square, square, ((ROWS, 512), BF16), edge, edge),
         bc, cols, rows, xf, xr, dy, skip,
     )
-    (groups,) = call(group_kernel, (((FAR, 72, 256), BF16),), arrived)
+    (groups,) = call(group_kernel, (((FAR, 40, 256), BF16),), arrived, place)
     groups = swap(groups, "zh")
     (entering,) = call(chain_kernel, (((NEAR, 64, 256), BF16),), arrived, groups, place)
     entering = swap(entering, BESIDE)
@@ -687,24 +692,22 @@
         entering, bc, cols, rows, xf, xr, dy, y0, dxf0, dxr0, side, line, rate,
         final=(0,),
     )
-    (totals,) = call(total_kernel, (((GROUPS, 24, 512), BF16),), swap(dpart, "fsdp"), draw)
-    dpf, dpr, to_prev, to_next, gsend = call(
+    (totals,) = call(total_kernel, (((GROUPS, 40, 256), BF16),), swap(dpart, "fsdp"), draw)
+    dpf, dpr, to_pair, to_side, gsend = call(
         project_back_kernel,
         (square, square, edge, edge, ((NEAR, 96, 128), BF16)),
         swap(totals, "fsdp"), xf, xr, gf, gr, dxf, dxr, wb,
-        wc, swt, oht, table, scale, gain, cw, small,
-    )
-    from_next = shift(to_prev, down)
-    from_prev = shift(to_next, up)
+        wc, swt, oht, table, scale, gain, cw, small, place,
+    )
+    from_pair = shift(to_pair, within)
+    from_side = shift(to_side, across)
     reduced = swap(gsend, BESIDE)
-    (ahead,) = call(
-        ahead_kernel, (square,), dpf, from_next, cw, scratch=[VMEM((ROWS + 8, 256), F32)]
-    )
+    (from_pair,) = call(catch_kernel, (edge,), from_pair)
     gn, cross = call(
         normed_kernel,
         (half_square, ((1, 256), F32)),
-        ahead, dpr, from_prev, cw, gain, table, oht,
-        scratch=[VMEM((ROWS + 8, 256), F32)],
+        dpf, dpr, from_pair, from_side, place, cw, gain, table, oht,
+        scratch=[VMEM((ROWS + 8, 256), F32), VMEM((ROWS + 8, 256), F32)],
     )
     (summed,) = call(near_kernel, (((FAR, 96, 128), BF16),), reduced)
     summed = swap(summed, "zh")

time: 188 us -> 185 us (0.984)
  blocking collectives: 92.9 us -> 89.9 us
    all_to_all x6, blocking collectives: 92.9 us -> 89.9 us  [swap(): return lax.all_to_all(value, axis, 0, 0, tiled=True)]
    ppermute x4, waiting for transfers between devices: 6.24 us -> 8.37 us  [shift(): return lax.ppermute(value, CTX, pairs)]
where the time goes in v6:
time: 185 us; the launch traced here: 182 us
  blocking collectives  89.9 us (49%)
  starting transfers between devices  45.3 us (24%)
  waiting for transfers between devices  28.9 us (16%)
  Pallas kernels  17.5 us (9%)
    all_to_all x6, blocking collectives, swap(): return lax.all_to_all(value, axis, 0, 0, tiled=True)  89.9 us
    all_to_all x6, starting transfers between devices, swap(): return lax.all_to_all(value, axis, 0, 0, tiled=True)  30.9 us
    all_to_all x6, waiting for transfers between devices, swap(): return lax.all_to_all(value, axis, 0, 0, tiled=True)  20.5 us
    pallas_call x19, Pallas kernels, call(): pl.pallas_call(kernel, out_shape=shapes, scratch_shapes=scratch, compiler...  17.5 us
    ppermute x4, starting transfers between devices, shift(): return lax.ppermute(value, CTX, pairs)  14.4 us
    ppermute x4, waiting for transfers between devices, shift(): return lax.ppermute(value, CTX, pairs)  8.37 us
  transfers between devices with their start and end apart: 10, of which 7 were waited for; matrix products, arithmetic and copies ran while one was open for 0% of the time, Pallas kernels for 5%

profile of v6, /device:TPU:6, one launch (start us, length us, event | category | flops | bytes accessed | tf_op | source)
XLA Modules:
  0.0 182.3 jit_solution(15086692544217364879)
XLA Ops:
  0.6 1.5 shard_map.211
  2.1 5.9 %all-to-all-start = ((f32[16,1,128]{2,1,0:T(1,128)}), f32[16,1,128]{2,1,0:T(1,128)S(1)}, u32[]{:S(2)}, u32[]{:S(2)}) async-start(f32[16,1,128]{2,1,0:T(1,128)} %get-tuple-element.71), calls=%async_computation | async-start | bytes 16384 | tf_op jit(solution)/shard_map/all_to_all | solution.py:595
  8.1 4.7 %collective-permute-start.1 = (s32[1,256]{1,0:T(1,128)S(1)}, s32[1,256]{1,0:T(1,128)S(1)}, u32[]{:S(2)}, u32[]{:S(2)}) collective-permute-start(s32[1,256]{1,0:T(1,128)S(1)} %get-tuple-element.70.ids), channel_id=1, source_target_pairs={{1,2},{2,1},{3,4},{4,3},{5,6},{6,5},{7,8},{8,7},{9,10},{10,9},{11,... | collective-permute-start | bytes 3080 | tf_op jit(solution)/shard_map/ppermute | solution.py:599
  12.7 2.5 %collective-permute-start = (s32[1,256]{1,0:T(1,128)S(1)}, s32[1,256]{1,0:T(1,128)S(1)}, u32[]{:S(2)}, u32[]{:S(2)}) collective-permute-start(s32[1,256]{1,0:T(1,128)S(1)} %get-tuple-element.70.ids), channel_id=1, source_target_pairs={{0,1},{1,0},{2,3},{3,2},{4,5},{5,4},{6,7},{7,6},{8,9},{9,8},{10,11... | collective-permute-start | bytes 3080 | tf_op jit(solution)/shard_map/ppermute | solution.py:599
  15.3 1.2 shard_map.212
  16.5 0.0 collective-permute-done.1.ids_side
  16.5 3.2 %collective-permute-done.ids_pair = s32[1,256]{1,0:T(1,128)S(1)} collective-permute-done((s32[1,256]{1,0:T(1,128)S(1)}, s32[1,256]{1,0:T(1,128)S(1)}, u32[]{:S(2)}, u32[]{:S(2)}) %collective-permute-start) | collective-permute-done | bytes 1056 | tf_op jit(solution)/shard_map/ppermute | solution.py:599
  19.7 0.0 all-to-all-done.got
  19.7 1.0 shard_map.213
  20.7 13.8 %all_to_all.60.got = bf16[16,24,512]{2,1,0:T(8,128)(2,1)S(1)} all-to-all(bf16[16,24,512]{2,1,0:T(8,128)(2,1)S(1)} %get-tuple-element.79), channel_id=1, replica_groups=mesh['fsdp'=16,'zh'=4,'zl'=4,'xh'=2] {'fsdp'}, dimensions={0} | all-to-all | bytes 786432 | tf_op jit(solution)/shard_map/all_to_all | solution.py:595
  34.5 0.8 shard_map.214
  35.3 4.6 %all-to-all-start.2 = ((bf16[16,16,512]{2,1,0:T(8,128)(2,1)}), bf16[16,16,512]{2,1,0:T(8,128)(2,1)S(1)}, u32[]{:S(2)}, u32[]{:S(2)}) async-start(bf16[16,16,512]{2,1,0:T(8,128)(2,1)} %get-tuple-element.80), calls=%async_computation.2 | async-start | bytes 524288 | tf_op jit(solution)/shard_map/all_to_all | solution.py:595
  39.8 1.2 shard_map.215
  41.0 5.6 %all-to-all-done.2 = bf16[16,16,512]{2,1,0:T(8,128)(2,1)S(1)} async-done(((bf16[16,16,512]{2,1,0:T(8,128)(2,1)}), bf16[16,16,512]{2,1,0:T(8,128)(2,1)S(1)}, u32[]{:S(2)}, u32[]{:S(2)}) %all-to-all-start.2) | async-done | bytes 262176 | tf_op jit(solution)/shard_map/all_to_all | solution.py:595
  46.6 0.3 shard_map.216
  46.9 19.2 %all_to_all.61.got = bf16[8,72,256]{2,1,0:T(8,128)(2,1)S(1)} all-to-all(bf16[8,72,256]{2,1,0:T(8,128)(2,1)S(1)} %shard_map.216), channel_id=1, replica_groups=mesh['fsdp'=16,'zh'=4,'zl'=4,'xh'=2] {'zl','xh'}, dimensions={0} | all-to-all | bytes 589824 | tf_op jit(solution)/shard_map/all_to_all | solution.py:595
  66.0 0.1 shard_map.217
  66.1 23.2 %all_to_all.62.far = bf16[4,40,256]{2,1,0:T(8,128)(2,1)S(1)} all-to-all(bf16[4,40,256]{2,1,0:T(8,128)(2,1)S(1)} %shard_map.217), channel_id=1, replica_groups=mesh['fsdp'=16,'zh'=4,'zl'=4,'xh'=2] {'zh'}, dimensions={0} | all-to-all | bytes 163840 | tf_op jit(solution)/shard_map/all_to_all | solution.py:595
  89.3 0.9 shard_map.218
  90.2 6.4 %all-to-all-start.5 = ((bf16[8,64,256]{2,1,0:T(8,128)(2,1)}), bf16[8,64,256]{2,1,0:T(8,128)(2,1)S(1)}, u32[]{:S(2)}, u32[]{:S(2)}) async-start(bf16[8,64,256]{2,1,0:T(8,128)(2,1)} %shard_map.218), calls=%async_computation.5 | async-start | bytes 524288 | tf_op jit(solution)/shard_map/all_to_all | solution.py:595
  96.6 2.3 %shard_map.219 = (f32[256,256]{1,0:T(8,128)S(1)}, f32[256,256]{1,0:T(8,128)S(1)}, f32[256,256]{1,0:T(8,128)S(1)}, bf16[256,512]{1,0:T(8,128)(2,1)S(1)}, f32[8,256]{1,0:T(8,128)S(1)}, /*index=5*/f32[8,256]{1,0:T(8,128)S(1)}) custom-call(bf16[256,512]{1,0:T(8,128)(2,1)S(1)} %bitcast.16, f32[256,128]{1,0:T(8,128)S(1)} %get-tuple-element.90.cols_ref, ...), custom_call_target="tpu_custom_call" | custom-call | tf_op jit(solution)/shard_map/pallas_call | solution.py:29
  98.9 3.9 %all-to-all-done.5.got = bf16[8,64,256]{2,1,0:T(8,128)(2,1)S(1)} async-done(((bf16[8,64,256]{2,1,0:T(8,128)(2,1)}), bf16[8,64,256]{2,1,0:T(8,128)(2,1)S(1)}, u32[]{:S(2)}, u32[]{:S(2)}) %all-to-all-start.5) | async-done | bytes 262176 | tf_op jit(solution)/shard_map/all_to_all | solution.py:595
  102.9 1.0 shard_map.221
  103.9 4.0 %all-to-all-start.6 = ((bf16[16,16,512]{2,1,0:T(8,128)(2,1)}), bf16[16,16,512]{2,1,0:T(8,128)(2,1)S(1)}, u32[]{:S(2)}, u32[]{:S(2)}) async-start(bf16[16,16,512]{2,1,0:T(8,128)(2,1)} %shard_map.221), calls=%async_computation.6 | async-start | bytes 524288 | tf_op jit(solution)/shard_map/all_to_all | solution.py:595
  107.9 2.1 %shard_map.220 = (bf16[256,256]{1,0:T(8,128)(2,1)}, f32[256,256]{1,0:T(8,128)S(1)}, f32[256,256]{1,0:T(8,128)S(1)}, bf16[8,256]{1,0:T(8,128)(2,1)S(1)}, f32[8,256]{1,0:T(8,128)S(1)}) custom-call(bf16[8,64,256]{2,1,0:T(8,128)(2,1)S(1)} %all-to-all-done.5.got, bf16[256,512]{1,0:T(8,128)(2,1)S(1)} %bitcast.17, f32[256,128]{1,0:T(8,128)S(1)} %get-tuple-element.90.cols_ref, ...), custom_call_target="tpu_custom_call" | custom-call | tf_op jit(solution)/shard_map/pallas_call | solution.py:29
  110.0 4.7 %all-to-all-done.6.got = bf16[16,16,512]{2,1,0:T(8,128)(2,1)S(1)} async-done(((bf16[16,16,512]{2,1,0:T(8,128)(2,1)}), bf16[16,16,512]{2,1,0:T(8,128)(2,1)S(1)}, u32[]{:S(2)}, u32[]{:S(2)}) %all-to-all-start.6) | async-done | bytes 262176 | tf_op jit(solution)/shard_map/all_to_all | solution.py:595
  114.7 11.4 %all_to_all.63.got = bf16[16,40,256]{2,1,0:T(8,128)(2,1)S(1)} all-to-all(bf16[16,40,256]{2,1,0:T(8,128)(2,1)S(1)} %shard_map.222), channel_id=1, replica_groups=mesh['fsdp'=16,'zh'=4,'zl'=4,'xh'=2] {'fsdp'}, dimensions={0} | all-to-all | bytes 655360 | tf_op jit(solution)/shard_map/all_to_all | solution.py:595
  126.1 1.2 shard_map.223
  127.3 14.0 %all_to_all.64.got = bf16[8,96,128]{2,1,0:T(8,128)(2,1)S(1)} all-to-all(bf16[8,96,128]{2,1,0:T(8,128)(2,1)S(1)} %get-tuple-element.109), channel_id=1, replica_groups=mesh['fsdp'=16,'zh'=4,'zl'=4,'xh'=2] {'zl','xh'}, dimensions={0} | all-to-all | bytes 393216 | tf_op jit(solution)/shard_map/all_to_all | solution.py:595
  141.3 0.7 shard_map.224
  142.0 3.3 %all-to-all-start.9 = ((bf16[4,96,128]{2,1,0:T(8,128)(2,1)}), bf16[4,96,128]{2,1,0:T(8,128)(2,1)S(1)}, u32[]{:S(2)}, u32[]{:S(2)}) async-start(bf16[4,96,128]{2,1,0:T(8,128)(2,1)} %shard_map.224), calls=%async_computation.9 | async-start | bytes 196608 | tf_op jit(solution)/shard_map/all_to_all | solution.py:595
  145.3 4.5 %collective-permute-start.2 = (f32[8,256]{1,0:T(8,128)S(1)}, f32[8,256]{1,0:T(8,128)S(1)}, u32[]{:S(2)}, u32[]{:S(2)}) collective-permute-start(f32[8,256]{1,0:T(8,128)S(1)} %get-tuple-element.112), channel_id=1, source_target_pairs={{0,1},{1,0},{2,3},{3,2},{4,5},{5,4},{6,7},{7,6},{8,9},{9,8},{10,11... | collective-permute-start | bytes 24584 | tf_op jit(solution)/shard_map/ppermute | solution.py:599
  149.8 2.7 %collective-permute-start.3 = (f32[8,256]{1,0:T(8,128)S(1)}, f32[8,256]{1,0:T(8,128)S(1)}, u32[]{:S(2)}, u32[]{:S(2)}) collective-permute-start(f32[8,256]{1,0:T(8,128)S(1)} %get-tuple-element.113), channel_id=1, source_target_pairs={{1,2},{2,1},{3,4},{4,3},{5,6},{6,5},{7,8},{8,7},{9,10},{10,9},{11,... | collective-permute-start | bytes 24584 | tf_op jit(solution)/shard_map/ppermute | solution.py:599
  152.5 0.0 collective-permute-done.2.edge
  152.5 5.2 %collective-permute-done.3.from_side = f32[8,256]{1,0:T(8,128)S(1)} collective-permute-done((f32[8,256]{1,0:T(8,128)S(1)}, f32[8,256]{1,0:T(8,128)S(1)}, u32[]{:S(2)}, u32[]{:S(2)}) %collective-permute-start.3) | collective-permute-done | bytes 8224 | tf_op jit(solution)/shard_map/ppermute | solution.py:599
  157.7 0.7 shard_map.226
  158.5 0.2 all-to-all-done.9.got
  158.6 0.7 shard_map.227
  159.3 8.3 %all_to_all.65.got.cross = f32[16,1,384]{2,1,0:T(1,128)S(1)} all-to-all(f32[16,1,384]{2,1,0:T(1,128)S(1)} %get-tuple-element.115), channel_id=1, replica_groups=mesh['fsdp'=16,'zh'=4,'zl'=4,'xh'=2] {'fsdp'}, dimensions={0} | all-to-all | bytes 49152 | tf_op jit(solution)/shard_map/all_to_all | solution.py:595
  167.6 6.6 %all-to-all-start.11 = ((bf16[8,96,128]{2,1,0:T(8,128)(2,1)}), bf16[8,96,128]{2,1,0:T(8,128)(2,1)S(1)}, u32[]{:S(2)}, u32[]{:S(2)}) async-start(bf16[8,96,128]{2,1,0:T(8,128)(2,1)} %get-tuple-element.117), calls=%async_computation.11 | async-start | bytes 393216 | tf_op jit(solution)/shard_map/all_to_all | solution.py:595
  174.2 1.1 shard_map.228
  175.3 6.1 %all-to-all-done.11.got = bf16[8,96,128]{2,1,0:T(8,128)(2,1)S(1)} async-done(((bf16[8,96,128]{2,1,0:T(8,128)(2,1)}), bf16[8,96,128]{2,1,0:T(8,128)(2,1)S(1)}, u32[]{:S(2)}, u32[]{:S(2)}) %all-to-all-start.11) | async-done | bytes 196640 | tf_op jit(solution)/shard_map/all_to_all | solution.py:595
  181.4 0.9 shard_map.229
  (2 shorter events, 0.0 us)
Async XLA Ops:
  2.1 17.6 %all-to-all-start = ((f32[16,1,128]{2,1,0:T(1,128)}), f32[16,1,128]{2,1,0:T(1,128)S(1)}, u32[]{:S(2)}, u32[]{:S(2)}) async-start(f32[16,1,128]{2,1,0:T(1,128)} %get-tuple-element.71), calls=%async_computation | async-start | bytes 16384 | tf_op jit(solution)/shard_map/all_to_all | solution.py:595
  8.1 8.4 %collective-permute-start.1 = (s32[1,256]{1,0:T(1,128)S(1)}, s32[1,256]{1,0:T(1,128)S(1)}, u32[]{:S(2)}, u32[]{:S(2)}) collective-permute-start(s32[1,256]{1,0:T(1,128)S(1)} %get-tuple-element.70.ids), channel_id=1, source_target_pairs={{1,2},{2,1},{3,4},{4,3},{5,6},{6,5},{7,8},{8,7},{9,10},{10,9},{11,... | collective-permute-start | bytes 3080 | tf_op jit(solution)/shard_map/ppermute | solution.py:599
  12.7 7.0 %collective-permute-start = (s32[1,256]{1,0:T(1,128)S(1)}, s32[1,256]{1,0:T(1,128)S(1)}, u32[]{:S(2)}, u32[]{:S(2)}) collective-permute-start(s32[1,256]{1,0:T(1,128)S(1)} %get-tuple-element.70.ids), channel_id=1, source_target_pairs={{0,1},{1,0},{2,3},{3,2},{4,5},{5,4},{6,7},{7,6},{8,9},{9,8},{10,11... | collective-permute-start | bytes 3080 | tf_op jit(solution)/shard_map/ppermute | solution.py:599
  35.3 11.3 %all-to-all-start.2 = ((bf16[16,16,512]{2,1,0:T(8,128)(2,1)}), bf16[16,16,512]{2,1,0:T(8,128)(2,1)S(1)}, u32[]{:S(2)}, u32[]{:S(2)}) async-start(bf16[16,16,512]{2,1,0:T(8,128)(2,1)} %get-tuple-element.80), calls=%async_computation.2 | async-start | bytes 524288 | tf_op jit(solution)/shard_map/all_to_all | solution.py:595
  90.2 12.6 %all-to-all-start.5 = ((bf16[8,64,256]{2,1,0:T(8,128)(2,1)}), bf16[8,64,256]{2,1,0:T(8,128)(2,1)S(1)}, u32[]{:S(2)}, u32[]{:S(2)}) async-start(bf16[8,64,256]{2,1,0:T(8,128)(2,1)} %shard_map.218), calls=%async_computation.5 | async-start | bytes 524288 | tf_op jit(solution)/shard_map/all_to_all | solution.py:595
  103.9 10.8 %all-to-all-start.6 = ((bf16[16,16,512]{2,1,0:T(8,128)(2,1)}), bf16[16,16,512]{2,1,0:T(8,128)(2,1)S(1)}, u32[]{:S(2)}, u32[]{:S(2)}) async-start(bf16[16,16,512]{2,1,0:T(8,128)(2,1)} %shard_map.221), calls=%async_computation.6 | async-start | bytes 524288 | tf_op jit(solution)/shard_map/all_to_all | solution.py:595
  142.0 16.6 %all-to-all-start.9 = ((bf16[4,96,128]{2,1,0:T(8,128)(2,1)}), bf16[4,96,128]{2,1,0:T(8,128)(2,1)S(1)}, u32[]{:S(2)}, u32[]{:S(2)}) async-start(bf16[4,96,128]{2,1,0:T(8,128)(2,1)} %shard_map.224), calls=%async_computation.9 | async-start | bytes 196608 | tf_op jit(solution)/shard_map/all_to_all | solution.py:595
  145.3 7.2 %collective-permute-start.2 = (f32[8,256]{1,0:T(8,128)S(1)}, f32[8,256]{1,0:T(8,128)S(1)}, u32[]{:S(2)}, u32[]{:S(2)}) collective-permute-start(f32[8,256]{1,0:T(8,128)S(1)} %get-tuple-element.112), channel_id=1, source_target_pairs={{0,1},{1,0},{2,3},{3,2},{4,5},{5,4},{6,7},{7,6},{8,9},{9,8},{10,11... | collective-permute-start | bytes 24584 | tf_op jit(solution)/shard_map/ppermute | solution.py:599
  149.8 7.9 %collective-permute-start.3 = (f32[8,256]{1,0:T(8,128)S(1)}, f32[8,256]{1,0:T(8,128)S(1)}, u32[]{:S(2)}, u32[]{:S(2)}) collective-permute-start(f32[8,256]{1,0:T(8,128)S(1)} %get-tuple-element.113), channel_id=1, source_target_pairs={{1,2},{2,1},{3,4},{4,3},{5,6},{6,5},{7,8},{8,7},{9,10},{10,9},{11,... | collective-permute-start | bytes 24584 | tf_op jit(solution)/shard_map/ppermute | solution.py:599
  167.6 13.8 %all-to-all-start.11 = ((bf16[8,96,128]{2,1,0:T(8,128)(2,1)}), bf16[8,96,128]{2,1,0:T(8,128)(2,1)S(1)}, u32[]{:S(2)}, u32[]{:S(2)}) async-start(bf16[8,96,128]{2,1,0:T(8,128)(2,1)} %get-tuple-element.117), calls=%async_computation.11 | async-start | bytes 393216 | tf_op jit(solution)/shard_map/all_to_all | solution.py:595

commit v7 on v6

--- a/solution.py
+++ b/solution.py
@@ -453,9 +453,24 @@
     return jnp.where(row == 0, high, 0.0) + jnp.where(row == 1, value - high, 0.0)
 
 
+def pack_edge(rows):
+    return jnp.concatenate([rows[:, 0:128], rows[:, 128:256], jnp.zeros((2, 128), F32)], axis=0)
+
+
+def open_edge(packed):
+    return jnp.concatenate([packed[0:3], packed[3:6]], axis=1)
+
+
+def picked(edges, at, count):
+    total = jnp.zeros((8, 128), F32)
+    for k in range(count):
+        total = jnp.where(at == k, edges[k, 96:104, :].astype(F32), total)
+    return total
+
+
 def project_back_kernel(
     got, xf, xr, gf, gr, dxf, dxr, wb, wc, swt, oht, table, scale, gain, cw, small,
-    place, dpf, dpr, to_pair, to_side, send,
+    place, dpf, dpr, send,
 ):
     draw = got[:, 32:40, :].astype(F32).reshape(128, 256).astype(BF16)
     pick_row = iota((128, 64), 0)
@@ -486,9 +501,11 @@
             part = jnp.sum(normed * block, axis=0, keepdims=True)
             taps[k] = taps[k] + part
         bias_row = bias_row + jnp.sum(dpre, axis=0, keepdims=True)
-    even = place[...] % 2 == 0
-    to_pair[...] = jnp.where(even, dpr[ROWS - 8 : ROWS], dpf[0:8])
-    to_side[...] = jnp.where(even, dpf[0:8], dpr[ROWS - 8 : ROWS])
+    ahead_edge = pack_edge(dpr[ROWS - 3 : ROWS]).astype(BF16)
+    behind_edge = pack_edge(dpf[0:3]).astype(BF16)
+    onward = (place[...] + 1) % NEAR
+    for k in range(NEAR):
+        send[k, 96:104, :] = jnp.where(onward == k, ahead_edge, behind_edge)
     shared = table[...] * gain[...] * ids_sum
     placed = jnp.concatenate(
         [jnp.zeros((88, 256), F32), shared, jnp.zeros((24, 256), F32)], axis=0
@@ -505,18 +522,17 @@
     send[:, 64:96, :] = last.astype(BF16).reshape(NEAR, 32, 128)
 
 
-def catch_kernel(edge, caught):
-    caught[...] = edge[...]
-
-
 def normed_kernel(
-    dpf, dpr, from_pair, from_side, place, cw, gain, table, oht,
-    gn_ref, cross, ahead, behind,
+    dpf, dpr, far, near_prev, near_next, place, cw, gain, table, oht,
+    gn_ref, payload, ahead, behind,
 ):
-    even = place[...] % 2 == 0
+    here = place[...] % NEAR
+    group = place[...] // NEAR
+    prev = jnp.where(here == 0, picked(far, group - 1, FAR), near_prev[...])
+    following = jnp.where(here == NEAR - 1, picked(far, group + 1, FAR), near_next[...])
     ahead[0:ROWS] = dpf[...]
-    ahead[ROWS : ROWS + 8] = jnp.where(even, from_pair[...], from_side[...])
-    behind[0:8] = jnp.where(even, from_side[...], from_pair[...])
+    ahead[ROWS : ROWS + 8] = jnp.concatenate([open_edge(following), jnp.zeros((5, 256), F32)], axis=0)
+    behind[0:8] = jnp.concatenate([jnp.zeros((5, 256), F32), open_edge(prev)], axis=0)
     behind[8 : ROWS + 8] = dpr[...]
     dn = jnp.zeros((ROWS, 256), F32)
     for k in range(4):
@@ -525,7 +541,14 @@
     gn_ref[...] = gn
     rated = exact(mm_tn, oht[48:64], table[...] * gain[...], 3, False)
     ones = jnp.ones((8, 256), BF16)
-    cross[...] = exact(mm_nt, ones, gn.astype(F32) * rated, 3, False)[0:1]
+    row = exact(mm_nt, ones, gn.astype(F32) * rated, 3, False)[0:1]
+    both = jnp.zeros((1, 128), F32)
+    for k in range(FAR):
+        both = both + far[k, 64:65, :].astype(F32) + far[k, 65:66, :].astype(F32)
+    lane = iota((1, 128), 1)
+    crossed = jnp.where((lane >= 88) & (lane < 104), both, 0.0)
+    row = jnp.concatenate([row, crossed], axis=1)
+    payload[...] = jnp.broadcast_to(row[None], (GROUPS, 1, 384))
 
 
 def embedded_kernel(got, gn, gain, table, scale, oht, out):
@@ -540,28 +563,29 @@
     out[...] = (turned * gn[...].astype(F32) - shrunk * cross).astype(BF16)
 
 
-def near_kernel(got, send):
-    total = got[0].astype(F32)
+def near_kernel(got, place, send, near_prev, near_next):
+    total = got[0, 0:96, :].astype(F32)
     for k in range(1, NEAR):
-        total = total + got[k].astype(F32)
+        total = total + got[k, 0:96, :].astype(F32)
     last = total[64:96]
     lane = iota((32, 128), 1)
     crossed = jnp.where((lane >= 88) & (lane < 104), last, 0.0)
     last = last - crossed + split_row(jnp.sum(crossed, axis=0, keepdims=True), 32)
-    total = jnp.concatenate([total[0:64], last], axis=0)
-    send[...] = jnp.broadcast_to(total.astype(BF16)[None], (FAR, 96, 128))
-
-
-def far_kernel(got, cross, send, payload):
-    total = got[0].astype(F32)
+    here = place[...] % NEAR
+    prev = picked(got, (here + NEAR - 1) % NEAR, NEAR)
+    following = picked(got, (here + 1) % NEAR, NEAR)
+    near_prev[...] = prev
+    near_next[...] = following
+    forward = jnp.where(here == 0, prev, following)
+    total = jnp.concatenate([total[0:64], last, forward], axis=0)
+    send[...] = jnp.broadcast_to(total.astype(BF16)[None], (FAR, 104, 128))
+
+
+def far_kernel(got, send):
+    total = got[0, 0:96, :].astype(F32)
     for k in range(1, FAR):
-        total = total + got[k].astype(F32)
+        total = total + got[k, 0:96, :].astype(F32)
     send[...] = jnp.broadcast_to(total.astype(BF16)[None], (NEAR, 96, 128))
-    lane = iota((1, 128), 1)
-    both = total[64:65] + total[65:66]
-    crossed = jnp.where((lane >= 88) & (lane < 104), both, 0.0)
-    row = jnp.concatenate([cross[...], crossed], axis=1)
-    payload[...] = jnp.broadcast_to(row[None], (GROUPS, 1, 384))
 
 
 def finish_kernel(got, cross, table, scale, gain, gt, gg, gcw, gcb, gwb, gwc, gswt, gsb, glr, gsg):
@@ -693,27 +717,26 @@
         final=(0,),
     )
     (totals,) = call(total_kernel, (((GROUPS, 40, 256), BF16),), swap(dpart, "fsdp"), draw)
-    dpf, dpr, to_pair, to_side, gsend = call(
+    dpf, dpr, gsend = call(
         project_back_kernel,
-        (square, square, edge, edge, ((NEAR, 96, 128), BF16)),
+        (square, square, ((NEAR, 104, 128), BF16)),
         swap(totals, "fsdp"), xf, xr, gf, gr, dxf, dxr, wb,
         wc, swt, oht, table, scale, gain, cw, small, place,
     )
-    from_pair = shift(to_pair, within)
-    from_side = shift(to_side, across)
-    reduced = swap(gsend, BESIDE)
-    (from_pair,) = call(catch_kernel, (edge,), from_pair)
-    gn, cross = call(
+    small_edge = ((8, 128), F32)
+    summed, near_prev, near_next = call(
+        near_kernel,
+        (((FAR, 104, 128), BF16), small_edge, small_edge),
+        swap(gsend, BESIDE), place,
+    )
+    summed = swap(summed, "zh")
+    gn, payload = call(
         normed_kernel,
-        (half_square, ((1, 256), F32)),
-        dpf, dpr, from_pair, from_side, place, cw, gain, table, oht,
+        (half_square, ((GROUPS, 1, 384), F32)),
+        dpf, dpr, summed, near_prev, near_next, place, cw, gain, table, oht,
         scratch=[VMEM((ROWS + 8, 256), F32), VMEM((ROWS + 8, 256), F32)],
     )
-    (summed,) = call(near_kernel, (((FAR, 96, 128), BF16),), reduced)
-    summed = swap(summed, "zh")
-    gathered, payload = call(
-        far_kernel, (((NEAR, 96, 128), BF16), ((GROUPS, 1, 384), F32)), summed, cross
-    )
+    (gathered,) = call(far_kernel, (((NEAR, 96, 128), BF16),), summed)
     crossed = swap(payload, "fsdp")
     (grad_embedded,) = call(
         embedded_kernel, (half_square,), crossed, gn, gain, table, scale, oht, final=(0,)

time: 185 us -> 186 us (level)
  blocking collectives: 89.9 us -> 97.8 us
  starting transfers between devices: 45.3 us -> 38.9 us
    all_to_all x6, blocking collectives: 89.9 us -> 97.8 us  [swap(): return lax.all_to_all(value, axis, 0, 0, tiled=True)]
    ppermute x4 -> x2, starting transfers between devices: 14.4 us -> 7.16 us  [shift(): return lax.ppermute(value, CTX, pairs)]
    ppermute x4 -> x2, waiting for transfers between devices: 8.37 us -> 3.18 us  [shift(): return lax.ppermute(value, CTX, pairs)]
    all_to_all x6, waiting for transfers between devices: 20.5 us -> 24.4 us  [swap(): return lax.all_to_all(value, axis, 0, 0, tiled=True)]
    pallas_call x19 -> x18, Pallas kernels: 17.5 us -> 17.6 us  [call(): pl.pallas_call(kernel, out_shape=shapes, scratch_shapes=scratch, compiler...]
  transfers between devices with their start and end apart: 10 -> 8, of which waited for: 7 -> 6; matrix products, arithmetic and copies ran while one was open for 0% -> 0% of each run, Pallas kernels for 5% -> 5%
where the time goes in v7:
time: 186 us; the launch traced here: 183 us
  blocking collectives  97.8 us (53%)
  starting transfers between devices  38.9 us (21%)
  waiting for transfers between devices  27.6 us (15%)
  Pallas kernels  17.6 us (9%)
    all_to_all x6, blocking collectives, swap(): return lax.all_to_all(value, axis, 0, 0, tiled=True)  97.8 us
    all_to_all x6, starting transfers between devices, swap(): return lax.all_to_all(value, axis, 0, 0, tiled=True)  31.7 us
    all_to_all x6, waiting for transfers between devices, swap(): return lax.all_to_all(value, axis, 0, 0, tiled=True)  24.4 us
    pallas_call x18, Pallas kernels, call(): pl.pallas_call(kernel, out_shape=shapes, scratch_shapes=scratch, compiler...  17.6 us
    ppermute x2, starting transfers between devices, shift(): return lax.ppermute(value, CTX, pairs)  7.16 us
  transfers between devices with their start and end apart: 8, of which 6 were waited for; matrix products, arithmetic and copies ran while one was open for 0% of the time, Pallas kernels for 5%

profile of v7, /device:TPU:6, one launch (start us, length us, event | category | flops | bytes accessed | tf_op | source)
XLA Modules:
  0.0 182.6 jit_solution(13002250371839630197)
XLA Ops:
  0.6 1.5 shard_map.211
  2.1 5.9 %all-to-all-start = ((f32[16,1,128]{2,1,0:T(1,128)}), f32[16,1,128]{2,1,0:T(1,128)S(1)}, u32[]{:S(2)}, u32[]{:S(2)}) async-start(f32[16,1,128]{2,1,0:T(1,128)} %get-tuple-element.70), calls=%async_computation | async-start | bytes 16384 | tf_op jit(solution)/shard_map/all_to_all | solution.py:619
  8.1 4.7 %collective-permute-start.1 = (s32[1,256]{1,0:T(1,128)S(1)}, s32[1,256]{1,0:T(1,128)S(1)}, u32[]{:S(2)}, u32[]{:S(2)}) collective-permute-start(s32[1,256]{1,0:T(1,128)S(1)} %get-tuple-element.69.ids), channel_id=1, source_target_pairs={{1,2},{2,1},{3,4},{4,3},{5,6},{6,5},{7,8},{8,7},{9,10},{10,9},{11,... | collective-permute-start | bytes 3080 | tf_op jit(solution)/shard_map/ppermute | solution.py:623
  12.7 2.5 %collective-permute-start = (s32[1,256]{1,0:T(1,128)S(1)}, s32[1,256]{1,0:T(1,128)S(1)}, u32[]{:S(2)}, u32[]{:S(2)}) collective-permute-start(s32[1,256]{1,0:T(1,128)S(1)} %get-tuple-element.69.ids), channel_id=1, source_target_pairs={{0,1},{1,0},{2,3},{3,2},{4,5},{5,4},{6,7},{7,6},{8,9},{9,8},{10,11... | collective-permute-start | bytes 3080 | tf_op jit(solution)/shard_map/ppermute | solution.py:623
  15.3 1.2 shard_map.212
  16.5 0.0 collective-permute-done.1.ids_side
  16.5 3.2 %collective-permute-done.ids_pair = s32[1,256]{1,0:T(1,128)S(1)} collective-permute-done((s32[1,256]{1,0:T(1,128)S(1)}, s32[1,256]{1,0:T(1,128)S(1)}, u32[]{:S(2)}, u32[]{:S(2)}) %collective-permute-start) | collective-permute-done | bytes 1056 | tf_op jit(solution)/shard_map/ppermute | solution.py:623
  19.7 0.0 all-to-all-done.got
  19.7 1.0 shard_map.213
  20.7 13.8 %all_to_all.60.got = bf16[16,24,512]{2,1,0:T(8,128)(2,1)S(1)} all-to-all(bf16[16,24,512]{2,1,0:T(8,128)(2,1)S(1)} %get-tuple-element.78), channel_id=1, replica_groups=mesh['fsdp'=16,'zh'=4,'zl'=4,'xh'=2] {'fsdp'}, dimensions={0} | all-to-all | bytes 786432 | tf_op jit(solution)/shard_map/all_to_all | solution.py:619
  34.5 0.8 shard_map.214
  35.3 4.6 %all-to-all-start.2 = ((bf16[16,16,512]{2,1,0:T(8,128)(2,1)}), bf16[16,16,512]{2,1,0:T(8,128)(2,1)S(1)}, u32[]{:S(2)}, u32[]{:S(2)}) async-start(bf16[16,16,512]{2,1,0:T(8,128)(2,1)} %get-tuple-element.79), calls=%async_computation.2 | async-start | bytes 524288 | tf_op jit(solution)/shard_map/all_to_all | solution.py:619
  39.8 1.2 shard_map.215
  41.0 5.6 %all-to-all-done.2 = bf16[16,16,512]{2,1,0:T(8,128)(2,1)S(1)} async-done(((bf16[16,16,512]{2,1,0:T(8,128)(2,1)}), bf16[16,16,512]{2,1,0:T(8,128)(2,1)S(1)}, u32[]{:S(2)}, u32[]{:S(2)}) %all-to-all-start.2) | async-done | bytes 262176 | tf_op jit(solution)/shard_map/all_to_all | solution.py:619
  46.6 0.3 shard_map.216
  46.9 19.2 %all_to_all.61.got = bf16[8,72,256]{2,1,0:T(8,128)(2,1)S(1)} all-to-all(bf16[8,72,256]{2,1,0:T(8,128)(2,1)S(1)} %shard_map.216), channel_id=1, replica_groups=mesh['fsdp'=16,'zh'=4,'zl'=4,'xh'=2] {'zl','xh'}, dimensions={0} | all-to-all | bytes 589824 | tf_op jit(solution)/shard_map/all_to_all | solution.py:619
  66.0 0.1 shard_map.217
  66.1 23.2 %all_to_all.62.far = bf16[4,40,256]{2,1,0:T(8,128)(2,1)S(1)} all-to-all(bf16[4,40,256]{2,1,0:T(8,128)(2,1)S(1)} %shard_map.217), channel_id=1, replica_groups=mesh['fsdp'=16,'zh'=4,'zl'=4,'xh'=2] {'zh'}, dimensions={0} | all-to-all | bytes 163840 | tf_op jit(solution)/shard_map/all_to_all | solution.py:619
  89.4 0.9 shard_map.218
  90.2 6.4 %all-to-all-start.5 = ((bf16[8,64,256]{2,1,0:T(8,128)(2,1)}), bf16[8,64,256]{2,1,0:T(8,128)(2,1)S(1)}, u32[]{:S(2)}, u32[]{:S(2)}) async-start(bf16[8,64,256]{2,1,0:T(8,128)(2,1)} %shard_map.218), calls=%async_computation.5 | async-start | bytes 524288 | tf_op jit(solution)/shard_map/all_to_all | solution.py:619
  96.7 2.3 %shard_map.219 = (f32[256,256]{1,0:T(8,128)S(1)}, f32[256,256]{1,0:T(8,128)S(1)}, f32[256,256]{1,0:T(8,128)S(1)}, bf16[256,512]{1,0:T(8,128)(2,1)S(1)}, f32[8,256]{1,0:T(8,128)S(1)}, /*index=5*/f32[8,256]{1,0:T(8,128)S(1)}) custom-call(bf16[256,512]{1,0:T(8,128)(2,1)S(1)} %bitcast.16, f32[256,128]{1,0:T(8,128)S(1)} %get-tuple-element.89.cols_ref, ...), custom_call_target="tpu_custom_call" | custom-call | tf_op jit(solution)/shard_map/pallas_call | solution.py:29
  98.9 3.9 %all-to-all-done.5.got = bf16[8,64,256]{2,1,0:T(8,128)(2,1)S(1)} async-done(((bf16[8,64,256]{2,1,0:T(8,128)(2,1)}), bf16[8,64,256]{2,1,0:T(8,128)(2,1)S(1)}, u32[]{:S(2)}, u32[]{:S(2)}) %all-to-all-start.5) | async-done | bytes 262176 | tf_op jit(solution)/shard_map/all_to_all | solution.py:619
  102.9 1.0 shard_map.221
  103.9 4.1 %all-to-all-start.6 = ((bf16[16,16,512]{2,1,0:T(8,128)(2,1)}), bf16[16,16,512]{2,1,0:T(8,128)(2,1)S(1)}, u32[]{:S(2)}, u32[]{:S(2)}) async-start(bf16[16,16,512]{2,1,0:T(8,128)(2,1)} %shard_map.221), calls=%async_computation.6 | async-start | bytes 524288 | tf_op jit(solution)/shard_map/all_to_all | solution.py:619
  107.9 2.1 %shard_map.220 = (bf16[256,256]{1,0:T(8,128)(2,1)}, f32[256,256]{1,0:T(8,128)S(1)}, f32[256,256]{1,0:T(8,128)S(1)}, bf16[8,256]{1,0:T(8,128)(2,1)S(1)}, f32[8,256]{1,0:T(8,128)S(1)}) custom-call(bf16[8,64,256]{2,1,0:T(8,128)(2,1)S(1)} %all-to-all-done.5.got, bf16[256,512]{1,0:T(8,128)(2,1)S(1)} %bitcast.17, f32[256,128]{1,0:T(8,128)S(1)} %get-tuple-element.89.cols_ref, ...), custom_call_target="tpu_custom_call" | custom-call | tf_op jit(solution)/shard_map/pallas_call | solution.py:29
  110.0 4.7 %all-to-all-done.6.got = bf16[16,16,512]{2,1,0:T(8,128)(2,1)S(1)} async-done(((bf16[16,16,512]{2,1,0:T(8,128)(2,1)}), bf16[16,16,512]{2,1,0:T(8,128)(2,1)S(1)}, u32[]{:S(2)}, u32[]{:S(2)}) %all-to-all-start.6) | async-done | bytes 262176 | tf_op jit(solution)/shard_map/all_to_all | solution.py:619
  114.8 11.4 %all_to_all.63.got = bf16[16,40,256]{2,1,0:T(8,128)(2,1)S(1)} all-to-all(bf16[16,40,256]{2,1,0:T(8,128)(2,1)S(1)} %shard_map.222), channel_id=1, replica_groups=mesh['fsdp'=16,'zh'=4,'zl'=4,'xh'=2] {'fsdp'}, dimensions={0} | all-to-all | bytes 655360 | tf_op jit(solution)/shard_map/all_to_all | solution.py:619
  126.2 1.2 shard_map.223
  127.4 14.3 %all_to_all.64.got = bf16[8,104,128]{2,1,0:T(8,128)(2,1)S(1)} all-to-all(bf16[8,104,128]{2,1,0:T(8,128)(2,1)S(1)} %get-tuple-element.110), channel_id=1, replica_groups=mesh['fsdp'=16,'zh'=4,'zl'=4,'xh'=2] {'zl','xh'}, dimensions={0} | all-to-all | bytes 425984 | tf_op jit(solution)/shard_map/all_to_all | solution.py:619
  141.7 0.1 shard_map.224
  141.8 15.8 %all_to_all.65.far.got = bf16[4,104,128]{2,1,0:T(8,128)(2,1)S(1)} all-to-all(bf16[4,104,128]{2,1,0:T(8,128)(2,1)S(1)} %get-tuple-element.111), channel_id=1, replica_groups=mesh['fsdp'=16,'zh'=4,'zl'=4,'xh'=2] {'zh'}, dimensions={0} | all-to-all | bytes 212992 | tf_op jit(solution)/shard_map/all_to_all | solution.py:619
  157.6 1.4 shard_map.225
  159.0 4.2 %all-to-all-start.10 = ((f32[16,1,384]{2,1,0:T(1,128)}), f32[16,1,384]{2,1,0:T(1,128)S(1)}, u32[]{:S(2)}, u32[]{:S(2)}) async-start(f32[16,1,384]{2,1,0:T(1,128)} %get-tuple-element.114), calls=%async_computation.10 | async-start | bytes 49152 | tf_op jit(solution)/shard_map/all_to_all | solution.py:619
  163.2 0.7 shard_map.227
  163.9 4.1 %all-to-all-done.10.got.cross = f32[16,1,384]{2,1,0:T(1,128)S(1)} async-done(((f32[16,1,384]{2,1,0:T(1,128)}), f32[16,1,384]{2,1,0:T(1,128)S(1)}, u32[]{:S(2)}, u32[]{:S(2)}) %all-to-all-start.10) | async-done | bytes 24608 | tf_op jit(solution)/shard_map/all_to_all | solution.py:619
  168.0 6.6 %all-to-all-start.11 = ((bf16[8,96,128]{2,1,0:T(8,128)(2,1)}), bf16[8,96,128]{2,1,0:T(8,128)(2,1)S(1)}, u32[]{:S(2)}, u32[]{:S(2)}) async-start(bf16[8,96,128]{2,1,0:T(8,128)(2,1)} %shard_map.227), calls=%async_computation.11 | async-start | bytes 393216 | tf_op jit(solution)/shard_map/all_to_all | solution.py:619
  174.5 1.1 shard_map.226
  175.6 6.1 %all-to-all-done.11.got = bf16[8,96,128]{2,1,0:T(8,128)(2,1)S(1)} async-done(((bf16[8,96,128]{2,1,0:T(8,128)(2,1)}), bf16[8,96,128]{2,1,0:T(8,128)(2,1)S(1)}, u32[]{:S(2)}, u32[]{:S(2)}) %all-to-all-start.11) | async-done | bytes 196640 | tf_op jit(solution)/shard_map/all_to_all | solution.py:619
  181.7 0.9 shard_map.228
  (1 shorter events, 0.0 us)
Async XLA Ops:
  2.1 17.6 %all-to-all-start = ((f32[16,1,128]{2,1,0:T(1,128)}), f32[16,1,128]{2,1,0:T(1,128)S(1)}, u32[]{:S(2)}, u32[]{:S(2)}) async-start(f32[16,1,128]{2,1,0:T(1,128)} %get-tuple-element.70), calls=%async_computation | async-start | bytes 16384 | tf_op jit(solution)/shard_map/all_to_all | solution.py:619
  8.1 8.4 %collective-permute-start.1 = (s32[1,256]{1,0:T(1,128)S(1)}, s32[1,256]{1,0:T(1,128)S(1)}, u32[]{:S(2)}, u32[]{:S(2)}) collective-permute-start(s32[1,256]{1,0:T(1,128)S(1)} %get-tuple-element.69.ids), channel_id=1, source_target_pairs={{1,2},{2,1},{3,4},{4,3},{5,6},{6,5},{7,8},{8,7},{9,10},{10,9},{11,... | collective-permute-start | bytes 3080 | tf_op jit(solution)/shard_map/ppermute | solution.py:623
  12.7 7.0 %collective-permute-start = (s32[1,256]{1,0:T(1,128)S(1)}, s32[1,256]{1,0:T(1,128)S(1)}, u32[]{:S(2)}, u32[]{:S(2)}) collective-permute-start(s32[1,256]{1,0:T(1,128)S(1)} %get-tuple-element.69.ids), channel_id=1, source_target_pairs={{0,1},{1,0},{2,3},{3,2},{4,5},{5,4},{6,7},{7,6},{8,9},{9,8},{10,11... | collective-permute-start | bytes 3080 | tf_op jit(solution)/shard_map/ppermute | solution.py:623
  35.3 11.3 %all-to-all-start.2 = ((bf16[16,16,512]{2,1,0:T(8,128)(2,1)}), bf16[16,16,512]{2,1,0:T(8,128)(2,1)S(1)}, u32[]{:S(2)}, u32[]{:S(2)}) async-start(bf16[16,16,512]{2,1,0:T(8,128)(2,1)} %get-tuple-element.79), calls=%async_computation.2 | async-start | bytes 524288 | tf_op jit(solution)/shard_map/all_to_all | solution.py:619
  90.2 12.6 %all-to-all-start.5 = ((bf16[8,64,256]{2,1,0:T(8,128)(2,1)}), bf16[8,64,256]{2,1,0:T(8,128)(2,1)S(1)}, u32[]{:S(2)}, u32[]{:S(2)}) async-start(bf16[8,64,256]{2,1,0:T(8,128)(2,1)} %shard_map.218), calls=%async_computation.5 | async-start | bytes 524288 | tf_op jit(solution)/shard_map/all_to_all | solution.py:619
  103.9 10.8 %all-to-all-start.6 = ((bf16[16,16,512]{2,1,0:T(8,128)(2,1)}), bf16[16,16,512]{2,1,0:T(8,128)(2,1)S(1)}, u32[]{:S(2)}, u32[]{:S(2)}) async-start(bf16[16,16,512]{2,1,0:T(8,128)(2,1)} %shard_map.221), calls=%async_computation.6 | async-start | bytes 524288 | tf_op jit(solution)/shard_map/all_to_all | solution.py:619
  159.0 9.0 %all-to-all-start.10 = ((f32[16,1,384]{2,1,0:T(1,128)}), f32[16,1,384]{2,1,0:T(1,128)S(1)}, u32[]{:S(2)}, u32[]{:S(2)}) async-start(f32[16,1,384]{2,1,0:T(1,128)} %get-tuple-element.114), calls=%async_computation.10 | async-start | bytes 49152 | tf_op jit(solution)/shard_map/all_to_all | solution.py:619
  168.0 13.7 %all-to-all-start.11 = ((bf16[8,96,128]{2,1,0:T(8,128)(2,1)}), bf16[8,96,128]{2,1,0:T(8,128)(2,1)S(1)}, u32[]{:S(2)}, u32[]{:S(2)}) async-start(bf16[8,96,128]{2,1,0:T(8,128)(2,1)} %shard_map.227), calls=%async_computation.11 | async-start | bytes 393216 | tf_op jit(solution)/shard_map/all_to_all | solution.py:619

commit v8 on v7

--- a/solution.py
+++ b/solution.py
@@ -176,23 +176,20 @@
         halves.append(half)
     for member, half in enumerate(halves):
         for side, weight in ((0, wb), (128, wc)):
-            at = member * 256 + side
             part = mm(half, weight[...]).astype(BF16).reshape(GROUPS, 16, 128)
-            send[:, 0:16, at : at + 128] = part
+            send[:, member * 16 : member * 16 + 16, side : side + 128] = part
     own = iota((128, 256), 0) % 8 < 4
     steps = jnp.where(own, mm_nt(swx[...], halves[0]), mm_nt(swx[...], halves[1]))
-    high, low = pieces(steps, 2)
-    send[:, 16:24, 0:256] = high.reshape(GROUPS, 8, 256)
-    send[:, 16:24, 256:512] = low.reshape(GROUPS, 8, 256)
+    send[:, 32:40, :] = steps.astype(BF16).reshape(GROUPS, 8, 256)
 
 
 def reduce_kernel(got, bc, raw):
     total = got[0].astype(F32)
     for k in range(1, GROUPS):
         total = total + got[k].astype(F32)
-    half = total[0:16].astype(BF16)
+    half = jnp.concatenate([total[0:16], total[16:32]], axis=1).astype(BF16)
     bc[...] = jnp.broadcast_to(half[None], (GROUPS, 16, 512))
-    raw[...] = total[16:24, 0:256] + total[16:24, 256:512]
+    raw[...] = total[32:40]
 
 
 def steps_kernel(
@@ -680,7 +677,7 @@
             half_square,
             half_square,
             half_square,
-            ((GROUPS, 24, 512), BF16),
+            ((GROUPS, 40, 256), BF16),
             ((128, 256), BF16),
             ((16, 128), F32),
         ),

time: 186 us -> 185 us (level)
  no operation moved by 1% of the time
where the time goes in v8:
time: 185 us; the launch traced here: 182 us
  blocking collectives  97.1 us (52%)
  starting transfers between devices  38.8 us (21%)
  waiting for transfers between devices  27.6 us (15%)
  Pallas kernels  17.6 us (10%)
    all_to_all x6, blocking collectives, swap(): return lax.all_to_all(value, axis, 0, 0, tiled=True)  97.1 us
    all_to_all x6, starting transfers between devices, swap(): return lax.all_to_all(value, axis, 0, 0, tiled=True)  31.7 us
    all_to_all x6, waiting for transfers between devices, swap(): return lax.all_to_all(value, axis, 0, 0, tiled=True)  24.4 us
    pallas_call x18, Pallas kernels, call(): pl.pallas_call(kernel, out_shape=shapes, scratch_shapes=scratch, compiler...  17.6 us
    ppermute x2, starting transfers between devices, shift(): return lax.ppermute(value, CTX, pairs)  7.16 us
  transfers between devices with their start and end apart: 8, of which 6 were waited for; matrix products, arithmetic and copies ran while one was open for 0% of the time, Pallas kernels for 5%

profile of v8, /device:TPU:6, one launch (start us, length us, event | category | flops | bytes accessed | tf_op | source)
XLA Modules:
  0.0 181.9 jit_solution(14262294075465537472)
XLA Ops:
  0.6 1.5 shard_map.211
  2.1 5.9 %all-to-all-start = ((f32[16,1,128]{2,1,0:T(1,128)}), f32[16,1,128]{2,1,0:T(1,128)S(1)}, u32[]{:S(2)}, u32[]{:S(2)}) async-start(f32[16,1,128]{2,1,0:T(1,128)} %get-tuple-element.70), calls=%async_computation | async-start | bytes 16384 | tf_op jit(solution)/shard_map/all_to_all | solution.py:616
  8.1 4.7 %collective-permute-start.1 = (s32[1,256]{1,0:T(1,128)S(1)}, s32[1,256]{1,0:T(1,128)S(1)}, u32[]{:S(2)}, u32[]{:S(2)}) collective-permute-start(s32[1,256]{1,0:T(1,128)S(1)} %get-tuple-element.69.ids), channel_id=1, source_target_pairs={{1,2},{2,1},{3,4},{4,3},{5,6},{6,5},{7,8},{8,7},{9,10},{10,9},{11,... | collective-permute-start | bytes 3080 | tf_op jit(solution)/shard_map/ppermute | solution.py:620
  12.7 2.5 %collective-permute-start = (s32[1,256]{1,0:T(1,128)S(1)}, s32[1,256]{1,0:T(1,128)S(1)}, u32[]{:S(2)}, u32[]{:S(2)}) collective-permute-start(s32[1,256]{1,0:T(1,128)S(1)} %get-tuple-element.69.ids), channel_id=1, source_target_pairs={{0,1},{1,0},{2,3},{3,2},{4,5},{5,4},{6,7},{7,6},{8,9},{9,8},{10,11... | collective-permute-start | bytes 3080 | tf_op jit(solution)/shard_map/ppermute | solution.py:620
  15.3 1.2 shard_map.212
  16.5 0.0 collective-permute-done.1.ids_side
  16.5 3.2 %collective-permute-done.ids_pair = s32[1,256]{1,0:T(1,128)S(1)} collective-permute-done((s32[1,256]{1,0:T(1,128)S(1)}, s32[1,256]{1,0:T(1,128)S(1)}, u32[]{:S(2)}, u32[]{:S(2)}) %collective-permute-start) | collective-permute-done | bytes 1056 | tf_op jit(solution)/shard_map/ppermute | solution.py:620
  19.7 0.0 all-to-all-done.got
  19.7 1.0 shard_map.213
  20.7 13.0 %all_to_all.60.got = bf16[16,40,256]{2,1,0:T(8,128)(2,1)S(1)} all-to-all(bf16[16,40,256]{2,1,0:T(8,128)(2,1)S(1)} %get-tuple-element.78), channel_id=1, replica_groups=mesh['fsdp'=16,'zh'=4,'zl'=4,'xh'=2] {'fsdp'}, dimensions={0} | all-to-all | bytes 655360 | tf_op jit(solution)/shard_map/all_to_all | solution.py:616
  33.7 0.8 shard_map.214
  34.5 4.6 %all-to-all-start.2 = ((bf16[16,16,512]{2,1,0:T(8,128)(2,1)}), bf16[16,16,512]{2,1,0:T(8,128)(2,1)S(1)}, u32[]{:S(2)}, u32[]{:S(2)}) async-start(bf16[16,16,512]{2,1,0:T(8,128)(2,1)} %get-tuple-element.79), calls=%async_computation.2 | async-start | bytes 524288 | tf_op jit(solution)/shard_map/all_to_all | solution.py:616
  39.1 1.2 shard_map.215
  40.3 5.6 %all-to-all-done.2 = bf16[16,16,512]{2,1,0:T(8,128)(2,1)S(1)} async-done(((bf16[16,16,512]{2,1,0:T(8,128)(2,1)}), bf16[16,16,512]{2,1,0:T(8,128)(2,1)S(1)}, u32[]{:S(2)}, u32[]{:S(2)}) %all-to-all-start.2) | async-done | bytes 262176 | tf_op jit(solution)/shard_map/all_to_all | solution.py:616
  45.9 0.3 shard_map.216
  46.2 19.2 %all_to_all.61.got = bf16[8,72,256]{2,1,0:T(8,128)(2,1)S(1)} all-to-all(bf16[8,72,256]{2,1,0:T(8,128)(2,1)S(1)} %shard_map.216), channel_id=1, replica_groups=mesh['fsdp'=16,'zh'=4,'zl'=4,'xh'=2] {'zl','xh'}, dimensions={0} | all-to-all | bytes 589824 | tf_op jit(solution)/shard_map/all_to_all | solution.py:616
  65.3 0.1 shard_map.217
  65.4 23.2 %all_to_all.62.far = bf16[4,40,256]{2,1,0:T(8,128)(2,1)S(1)} all-to-all(bf16[4,40,256]{2,1,0:T(8,128)(2,1)S(1)} %shard_map.217), channel_id=1, replica_groups=mesh['fsdp'=16,'zh'=4,'zl'=4,'xh'=2] {'zh'}, dimensions={0} | all-to-all | bytes 163840 | tf_op jit(solution)/shard_map/all_to_all | solution.py:616
  88.6 0.9 shard_map.218
  89.5 6.4 %all-to-all-start.5 = ((bf16[8,64,256]{2,1,0:T(8,128)(2,1)}), bf16[8,64,256]{2,1,0:T(8,128)(2,1)S(1)}, u32[]{:S(2)}, u32[]{:S(2)}) async-start(bf16[8,64,256]{2,1,0:T(8,128)(2,1)} %shard_map.218), calls=%async_computation.5 | async-start | bytes 524288 | tf_op jit(solution)/shard_map/all_to_all | solution.py:616
  96.0 2.3 %shard_map.219 = (f32[256,256]{1,0:T(8,128)S(1)}, f32[256,256]{1,0:T(8,128)S(1)}, f32[256,256]{1,0:T(8,128)S(1)}, bf16[256,512]{1,0:T(8,128)(2,1)S(1)}, f32[8,256]{1,0:T(8,128)S(1)}, /*index=5*/f32[8,256]{1,0:T(8,128)S(1)}) custom-call(bf16[256,512]{1,0:T(8,128)(2,1)S(1)} %bitcast.16, f32[256,128]{1,0:T(8,128)S(1)} %get-tuple-element.89.cols_ref, ...), custom_call_target="tpu_custom_call" | custom-call | tf_op jit(solution)/shard_map/pallas_call | solution.py:29
  98.2 3.9 %all-to-all-done.5.got = bf16[8,64,256]{2,1,0:T(8,128)(2,1)S(1)} async-done(((bf16[8,64,256]{2,1,0:T(8,128)(2,1)}), bf16[8,64,256]{2,1,0:T(8,128)(2,1)S(1)}, u32[]{:S(2)}, u32[]{:S(2)}) %all-to-all-start.5) | async-done | bytes 262176 | tf_op jit(solution)/shard_map/all_to_all | solution.py:616
  102.2 1.0 shard_map.221
  103.2 4.1 %all-to-all-start.6 = ((bf16[16,16,512]{2,1,0:T(8,128)(2,1)}), bf16[16,16,512]{2,1,0:T(8,128)(2,1)S(1)}, u32[]{:S(2)}, u32[]{:S(2)}) async-start(bf16[16,16,512]{2,1,0:T(8,128)(2,1)} %shard_map.221), calls=%async_computation.6 | async-start | bytes 524288 | tf_op jit(solution)/shard_map/all_to_all | solution.py:616
  107.2 2.1 %shard_map.220 = (bf16[256,256]{1,0:T(8,128)(2,1)}, f32[256,256]{1,0:T(8,128)S(1)}, f32[256,256]{1,0:T(8,128)S(1)}, bf16[8,256]{1,0:T(8,128)(2,1)S(1)}, f32[8,256]{1,0:T(8,128)S(1)}) custom-call(bf16[8,64,256]{2,1,0:T(8,128)(2,1)S(1)} %all-to-all-done.5.got, bf16[256,512]{1,0:T(8,128)(2,1)S(1)} %bitcast.17, f32[256,128]{1,0:T(8,128)S(1)} %get-tuple-element.89.cols_ref, ...), custom_call_target="tpu_custom_call" | custom-call | tf_op jit(solution)/shard_map/pallas_call | solution.py:29
  109.3 4.7 %all-to-all-done.6.got = bf16[16,16,512]{2,1,0:T(8,128)(2,1)S(1)} async-done(((bf16[16,16,512]{2,1,0:T(8,128)(2,1)}), bf16[16,16,512]{2,1,0:T(8,128)(2,1)S(1)}, u32[]{:S(2)}, u32[]{:S(2)}) %all-to-all-start.6) | async-done | bytes 262176 | tf_op jit(solution)/shard_map/all_to_all | solution.py:616
  114.1 11.4 %all_to_all.63.got = bf16[16,40,256]{2,1,0:T(8,128)(2,1)S(1)} all-to-all(bf16[16,40,256]{2,1,0:T(8,128)(2,1)S(1)} %shard_map.222), channel_id=1, replica_groups=mesh['fsdp'=16,'zh'=4,'zl'=4,'xh'=2] {'fsdp'}, dimensions={0} | all-to-all | bytes 655360 | tf_op jit(solution)/shard_map/all_to_all | solution.py:616
  125.5 1.2 shard_map.223
  126.7 14.3 %all_to_all.64.got = bf16[8,104,128]{2,1,0:T(8,128)(2,1)S(1)} all-to-all(bf16[8,104,128]{2,1,0:T(8,128)(2,1)S(1)} %get-tuple-element.110), channel_id=1, replica_groups=mesh['fsdp'=16,'zh'=4,'zl'=4,'xh'=2] {'zl','xh'}, dimensions={0} | all-to-all | bytes 425984 | tf_op jit(solution)/shard_map/all_to_all | solution.py:616
  141.0 0.1 shard_map.224
  141.1 16.0 %all_to_all.65.far.got = bf16[4,104,128]{2,1,0:T(8,128)(2,1)S(1)} all-to-all(bf16[4,104,128]{2,1,0:T(8,128)(2,1)S(1)} %get-tuple-element.111), channel_id=1, replica_groups=mesh['fsdp'=16,'zh'=4,'zl'=4,'xh'=2] {'zh'}, dimensions={0} | all-to-all | bytes 212992 | tf_op jit(solution)/shard_map/all_to_all | solution.py:616
  157.1 1.4 shard_map.225
  158.4 4.1 %all-to-all-start.10 = ((f32[16,1,384]{2,1,0:T(1,128)}), f32[16,1,384]{2,1,0:T(1,128)S(1)}, u32[]{:S(2)}, u32[]{:S(2)}) async-start(f32[16,1,384]{2,1,0:T(1,128)} %get-tuple-element.114), calls=%async_computation.10 | async-start | bytes 49152 | tf_op jit(solution)/shard_map/all_to_all | solution.py:616
  162.5 0.7 shard_map.227
  163.2 4.1 %all-to-all-done.10.got.cross = f32[16,1,384]{2,1,0:T(1,128)S(1)} async-done(((f32[16,1,384]{2,1,0:T(1,128)}), f32[16,1,384]{2,1,0:T(1,128)S(1)}, u32[]{:S(2)}, u32[]{:S(2)}) %all-to-all-start.10) | async-done | bytes 24608 | tf_op jit(solution)/shard_map/all_to_all | solution.py:616
  167.3 6.6 %all-to-all-start.11 = ((bf16[8,96,128]{2,1,0:T(8,128)(2,1)}), bf16[8,96,128]{2,1,0:T(8,128)(2,1)S(1)}, u32[]{:S(2)}, u32[]{:S(2)}) async-start(bf16[8,96,128]{2,1,0:T(8,128)(2,1)} %shard_map.227), calls=%async_computation.11 | async-start | bytes 393216 | tf_op jit(solution)/shard_map/all_to_all | solution.py:616
  173.8 1.1 shard_map.226
  174.9 6.1 %all-to-all-done.11.got = bf16[8,96,128]{2,1,0:T(8,128)(2,1)S(1)} async-done(((bf16[8,96,128]{2,1,0:T(8,128)(2,1)}), bf16[8,96,128]{2,1,0:T(8,128)(2,1)S(1)}, u32[]{:S(2)}, u32[]{:S(2)}) %all-to-all-start.11) | async-done | bytes 196640 | tf_op jit(solution)/shard_map/all_to_all | solution.py:616
  181.0 0.9 shard_map.228
  (1 shorter events, 0.0 us)
Async XLA Ops:
  2.1 17.6 %all-to-all-start = ((f32[16,1,128]{2,1,0:T(1,128)}), f32[16,1,128]{2,1,0:T(1,128)S(1)}, u32[]{:S(2)}, u32[]{:S(2)}) async-start(f32[16,1,128]{2,1,0:T(1,128)} %get-tuple-element.70), calls=%async_computation | async-start | bytes 16384 | tf_op jit(solution)/shard_map/all_to_all | solution.py:616
  8.1 8.4 %collective-permute-start.1 = (s32[1,256]{1,0:T(1,128)S(1)}, s32[1,256]{1,0:T(1,128)S(1)}, u32[]{:S(2)}, u32[]{:S(2)}) collective-permute-start(s32[1,256]{1,0:T(1,128)S(1)} %get-tuple-element.69.ids), channel_id=1, source_target_pairs={{1,2},{2,1},{3,4},{4,3},{5,6},{6,5},{7,8},{8,7},{9,10},{10,9},{11,... | collective-permute-start | bytes 3080 | tf_op jit(solution)/shard_map/ppermute | solution.py:620
  12.7 7.0 %collective-permute-start = (s32[1,256]{1,0:T(1,128)S(1)}, s32[1,256]{1,0:T(1,128)S(1)}, u32[]{:S(2)}, u32[]{:S(2)}) collective-permute-start(s32[1,256]{1,0:T(1,128)S(1)} %get-tuple-element.69.ids), channel_id=1, source_target_pairs={{0,1},{1,0},{2,3},{3,2},{4,5},{5,4},{6,7},{7,6},{8,9},{9,8},{10,11... | collective-permute-start | bytes 3080 | tf_op jit(solution)/shard_map/ppermute | solution.py:620
  34.5 11.4 %all-to-all-start.2 = ((bf16[16,16,512]{2,1,0:T(8,128)(2,1)}), bf16[16,16,512]{2,1,0:T(8,128)(2,1)S(1)}, u32[]{:S(2)}, u32[]{:S(2)}) async-start(bf16[16,16,512]{2,1,0:T(8,128)(2,1)} %get-tuple-element.79), calls=%async_computation.2 | async-start | bytes 524288 | tf_op jit(solution)/shard_map/all_to_all | solution.py:616
  89.5 12.6 %all-to-all-start.5 = ((bf16[8,64,256]{2,1,0:T(8,128)(2,1)}), bf16[8,64,256]{2,1,0:T(8,128)(2,1)S(1)}, u32[]{:S(2)}, u32[]{:S(2)}) async-start(bf16[8,64,256]{2,1,0:T(8,128)(2,1)} %shard_map.218), calls=%async_computation.5 | async-start | bytes 524288 | tf_op jit(solution)/shard_map/all_to_all | solution.py:616
  103.2 10.8 %all-to-all-start.6 = ((bf16[16,16,512]{2,1,0:T(8,128)(2,1)}), bf16[16,16,512]{2,1,0:T(8,128)(2,1)S(1)}, u32[]{:S(2)}, u32[]{:S(2)}) async-start(bf16[16,16,512]{2,1,0:T(8,128)(2,1)} %shard_map.221), calls=%async_computation.6 | async-start | bytes 524288 | tf_op jit(solution)/shard_map/all_to_all | solution.py:616
  158.4 8.8 %all-to-all-start.10 = ((f32[16,1,384]{2,1,0:T(1,128)}), f32[16,1,384]{2,1,0:T(1,128)S(1)}, u32[]{:S(2)}, u32[]{:S(2)}) async-start(f32[16,1,384]{2,1,0:T(1,128)} %get-tuple-element.114), calls=%async_computation.10 | async-start | bytes 49152 | tf_op jit(solution)/shard_map/all_to_all | solution.py:616
  167.3 13.7 %all-to-all-start.11 = ((bf16[8,96,128]{2,1,0:T(8,128)(2,1)}), bf16[8,96,128]{2,1,0:T(8,128)(2,1)S(1)}, u32[]{:S(2)}, u32[]{:S(2)}) async-start(bf16[8,96,128]{2,1,0:T(8,128)(2,1)} %shard_map.227), calls=%async_computation.11 | async-start | bytes 393216 | tf_op jit(solution)/shard_map/all_to_all | solution.py:616
